TPU v7x, 32 devices: a whole 2x2x4 slice. The times are simulated.
32 devices in a mesh: dp: 8 (over y, x, core), tensor: 4 (over z).
Axes of the slice: x: 2, y: 2, z: 4, core: 2. Of those that a mesh axis runs over, the one named last changes fastest.
Arguments:
- hidden: bfloat16 [4096, 8192], P('dp'), may hold values from -24 to 24
- weight: bfloat16 [1024, 8192], P('tensor', 'dp'), may hold values from -2 to 2, as said below
- qk_scale: float32 [4, 128], P('tensor'), may hold values from 0.5 to 2
- cotangent: bfloat16 [4096, 1024], P('dp', 'tensor'), may hold values from -12 to 12
Outputs:
- keys_values: bfloat16 [4096, 1024], P('dp', 'tensor')
- input_grad: bfloat16 [4096, 8192], P(('dp', 'tensor'))
- new_weight: bfloat16 [1024, 8192], P('tensor', 'dp')
Inputs may be any that keep to these rules, and one draw needn't show every extreme that they name: Entries of weight are of order 8192 ** -0.5 times a row scale.
All inputs are finite; a program needn't handle non-finite values.
Results may differ from a plain program's by a relative error of at most 0.009.
Values may be sent and summed in bfloat16 or wider, within the bound.
No kernel may reach another device: no remote copies, remote signals or barrier semaphores. Data moves between devices by JAX's collectives and lax.ppermute only.
A program may use at most 128 MiB of HBM per device.

v0:
```python
import math

import jax
import jax.numpy as jnp
from jax import lax
from jax.sharding import PartitionSpec as P

step_rate = 0.5
epsilon = 1e-06


def keys_and_grads(raw, qk_scale, cotangent):
    tok = raw.shape[0]
    heads = qk_scale.shape[0]
    size = qk_scale.shape[1]
    parts = raw.reshape(tok, heads, 2, size)
    key_raw = parts[:, :, 0]
    values = parts[:, :, 1]
    length = jnp.sqrt(jnp.sum(key_raw * key_raw, -1, keepdims=True) + epsilon)
    unit = key_raw / length
    factor = qk_scale * math.sqrt(size)
    keys = factor * unit
    outputs = jnp.stack([keys, values], 2).reshape(tok, -1).astype(jnp.bfloat16)
    cot = cotangent.astype(jnp.float32).reshape(tok, heads, 2, size)
    along = factor * cot[:, :, 0]
    key_grad = (along - unit * jnp.sum(unit * along, -1, keepdims=True)) / length
    d_raw = jnp.stack([key_grad, cot[:, :, 1]], 2).reshape(tok, -1).astype(jnp.bfloat16)
    return (outputs, d_raw)


def move_rows(w_rows, grad, grad_dot, w_square, g_square):
    tangent = grad - (grad_dot / w_square)[:, None] * w_rows
    scale_rows = step_rate * jnp.sqrt(w_square / (g_square + epsilon))
    return w_rows - scale_rows[:, None] * tangent


def local(hidden, weight, qk_scale, cotangent):
    full_w = lax.all_gather(weight, "dp", axis=1, tiled=True)
    width = full_w.shape[1]
    raw = jnp.einsum("td,rd->tr", hidden, full_w, preferred_element_type=jnp.float32)
    keys_values, d_raw = keys_and_grads(raw, qk_scale, cotangent)
    grad_block = lax.psum_scatter(
        jnp.einsum("tc,tr->cr", hidden, d_raw, preferred_element_type=jnp.float32),
        "dp",
        scatter_dimension=0,
        tiled=True,
    ).T
    input_grad = lax.psum_scatter(
        jnp.dot(d_raw, full_w, preferred_element_type=jnp.float32).astype(jnp.bfloat16),
        "tensor",
        scatter_dimension=0,
        tiled=True,
    )
    grad_full = lax.all_gather(grad_block.astype(jnp.bfloat16), "dp", axis=1, tiled=True).astype(
        grad_block.dtype
    )
    w_full = full_w.astype(jnp.float32)
    grad_dot = jnp.sum(grad_full * w_full, 1)
    w_square = jnp.sum(w_full * w_full, 1)
    g_square = jnp.sum(grad_full * grad_full, 1)
    moved_full = move_rows(w_full, grad_full, grad_dot, w_square, g_square)
    norm_sq = jnp.sum(moved_full * moved_full, 1)
    start = lax.axis_index("dp") * weight.shape[1]
    moved = lax.dynamic_slice_in_dim(moved_full, start, weight.shape[1], 1)
    new_weight = (math.sqrt(width) * moved / jnp.sqrt(norm_sq)[:, None]).astype(jnp.bfloat16)
    return (keys_values, input_grad, new_weight)


def solution(mesh):
    in_specs = (P("dp", None), P("tensor", "dp"), P("tensor", None), P("dp", "tensor"))
    out_specs = (P("dp", "tensor"), P(("dp", "tensor"), None), P("tensor", "dp"))
    return jax.shard_map(local, mesh=mesh, in_specs=in_specs, out_specs=out_specs, check_vma=False)
```

profile of v0, /device:TPU:0, one launch (start us, length us, event | category | flops | bytes accessed | tf_op | source)
XLA Modules:
  0.0 330.1 jit_solution(9406732910461633999)
XLA Ops:
  7.2 0.0 all-gather.3.cloned.1.call-start
  7.2 0.7 all-gather.3.cloned.1.call-update
  7.9 0.0 reduce-scatter.5.cloned.1.call-start
  7.9 1.1 copy.11
  9.1 0.7 multiply_bitcast_fusion
  9.7 39.5 %all-gather.3.cloned.1.call-done = bf16[256,8192]{1,0:T(8,128)(2,1)} async-done(((bf16[256,1024]{1,0:T(8,128)(2,1)}), bf16[256,8192]{1,0:T(8,128)(2,1)}) %all-gather.3.cloned.1.call-update) | async-done | bytes 4194320 | tf_op jit(solution)/shard_map/all_gather | solution.py:38
  49.2 6.9 %fusion.11 = f32[512,256]{0,1:T(8,128)S(1)} fusion(bf16[512,8192]{1,0:T(8,128)(2,1)} %param.4, bf16[256,8192]{1,0:T(8,128)(2,1)} %all-gather.3.cloned.1.call-done), kind=kOutput, calls=%fused_computation.35 | convolution fusion | flops 2147483648 | bytes 13107200 | tf_op jit(solution)/shard_map/td,rd->tr/dot_general | solution.py:40
  56.2 0.1 fusion.9
  56.4 0.1 fusion.6
  56.5 9.0 %convolution_bitcast_fusion = f32[8192,256]{0,1:T(8,128)} fusion(bf16[512,256]{0,1:T(8,128)(2,1)S(1)} %bitcast.31, bf16[512,8192]{1,0:T(8,128)(2,1)} %param.4), kind=kOutput, calls=%fused_computation.7 | convolution fusion | flops 2147483648 | bytes 17039360 | tf_op jit(solution)/shard_map/tc,tr->cr/dot_general | solution.py:43
  65.5 0.0 reduce-scatter.5.cloned.1.call-update
  65.5 0.0 all-gather.5.cloned.1.call-start
  65.6 71.5 %reduce-scatter.5.cloned.1.call-done = f32[1024,256]{0,1:T(8,128)} async-done(((f32[8192,256]{0,1:T(8,128)}), f32[1024,256]{0,1:T(8,128)}) %reduce-scatter.5.cloned.1.call-update) | async-done | bytes 1048592 | tf_op jit(solution)/shard_map/reduce_scatter | solution.py:42
  137.1 2.1 convert_bitcast_fusion
  139.2 0.0 all-gather.5.cloned.1.call-update
  139.2 0.0 reduce-scatter.3.cloned.1.call-start
  139.2 7.8 %convolution_convert_fusion = bf16[512,8192]{1,0:T(8,128)(2,1)} fusion(bf16[512,256]{0,1:T(8,128)(2,1)S(1)} %bitcast.32, bf16[256,8192]{1,0:T(8,128)(2,1)} %all-gather.3.cloned.1.call-done), kind=kOutput, calls=%fused_computation.6 | convolution fusion | flops 2151677952 | bytes 12845056 | tf_op jit(solution)/shard_map/dot_general | solution.py:49
  147.0 0.0 reduce-scatter.3.cloned.1.call-update
  147.0 0.8 copy.10
  147.9 28.3 %all-gather.5.cloned.1.call-done = bf16[256,8192]{1,0:T(8,128)(2,1)} async-done(((bf16[256,1024]{1,0:T(8,128)(2,1)}), bf16[256,8192]{1,0:T(8,128)(2,1)}) %all-gather.5.cloned.1.call-update) | async-done | bytes 4194320 | tf_op jit(solution)/shard_map/all_gather | solution.py:54
  176.2 0.0 copy-start
  176.2 0.0 copy-start.1
  176.2 5.2 %fusion = (f32[256]{0:T(256)S(1)}, f32[256]{0:T(256)S(1)}, f32[256]{0:T(256)S(1)}) fusion(bf16[256,8192]{1,0:T(8,128)(2,1)} %all-gather.5.cloned.1.call-done, bf16[256,8192]{1,0:T(8,128)(2,1)} %all-gather.3.cloned.1.call-done), kind=kLoop, calls=%fused_computation.8 | loop fusion | flops 16776448 | bytes 8391680 | tf_op jit(solution)/shard_map/reduce_sum | solution.py:60
  181.4 0.0 copy-done
  181.4 0.7 copy-done.1
  182.1 2.9 multiply_reduce_fusion
  185.0 1.0 divide_convert_fusion
  186.0 137.6 %reduce-scatter.3.cloned.1.call-done = bf16[128,8192]{1,0:T(8,128)(2,1)} async-done(((bf16[512,8192]{1,0:T(8,128)(2,1)}), bf16[128,8192]{1,0:T(8,128)(2,1)}) %reduce-scatter.3.cloned.1.call-update) | async-done | bytes 2097168 | tf_op jit(solution)/shard_map/reduce_scatter | solution.py:48
  (7 shorter events, 0.1 us)
Async XLA Ops:
  7.2 42.1 %all-gather.3.cloned.1.call-start = ((), (), s32[]{:S(2)}) async-start(), calls=%async_computation.2 | async-start | bytes 4718592 | tf_op jit(solution)/shard_map/all_gather | solution.py:38
  7.9 129.2 %reduce-scatter.5.cloned.1.call-start = ((), (), s32[]{:S(2)}) async-start(), calls=%async_computation.4 | async-start | bytes 9437184 | tf_op jit(solution)/shard_map/reduce_scatter | solution.py:42
  65.5 110.6 %all-gather.5.cloned.1.call-start = ((), (), s32[]{:S(2)}) async-start(), calls=%async_computation.5 | async-start | bytes 4718592 | tf_op jit(solution)/shard_map/all_gather | solution.py:54
  139.2 184.4 %reduce-scatter.3.cloned.1.call-start = ((), (), s32[]{:S(2)}) async-start(), calls=%async_computation.3 | async-start | bytes 10485760 | tf_op jit(solution)/shard_map/reduce_scatter | solution.py:48
  176.2 5.2 %copy-start = (bf16[256,8192]{1,0:T(8,128)(2,1)S(1)}, bf16[256,8192]{1,0:T(8,128)(2,1)}, u32[]{:S(2)}) copy-start(bf16[256,8192]{1,0:T(8,128)(2,1)} %all-gather.3.cloned.1.call-done) | copy-start | bytes 12582916
  176.2 5.9 %copy-start.1 = (bf16[256,8192]{1,0:T(8,128)(2,1)S(1)}, bf16[256,8192]{1,0:T(8,128)(2,1)}, u32[]{:S(2)}) copy-start(bf16[256,8192]{1,0:T(8,128)(2,1)} %all-gather.5.cloned.1.call-done) | copy-start | bytes 12582916
Sparse Core Ops, SparseCore 0:
  9.9 39.2 all-gather.2
  65.6 71.3 reduce-scatter.4
  139.5 36.5 all-gather.4
  178.9 144.6 reduce-scatter.2
where the time goes:
time: 330 us
  waiting for transfers between devices  278 us (84%)
  matrix products  23.7 us (7%)
  between operations  13.8 us (4%)
  other arithmetic  12.2 us (4%)
    reduce_scatter x1, waiting for transfers between devices, local(): lax.psum_scatter(jnp.dot(d_raw, full_w, preferred_element_type=jnp.float3...  138 us
    reduce_scatter x1, waiting for transfers between devices, local(): lax.psum_scatter(jnp.einsum('tc,tr->cr', hidden, d_raw, preferred_element...  71.5 us
    all_gather x1, waiting for transfers between devices, local(): full_w = lax.all_gather(weight, 'dp', axis=1, tiled=True)  39.5 us
    all_gather x1, waiting for transfers between devices, local(): lax.all_gather(grad_block.astype(jnp.bfloat16), 'dp', axis=1, tiled=True)  28.3 us
    dot_general x1, matrix products, local(): jnp.einsum('tc,tr->cr', hidden, d_raw, preferred_element_type=jnp.float32)  8.95 us
    dot_general x1, matrix products, local(): jnp.dot(d_raw, full_w, preferred_element_type=jnp.float32)  7.78 us
    dot_general x1, matrix products, local(): jnp.einsum('td,rd->tr', hidden, full_w, preferred_element_type=jnp.float32)  6.94 us
  transfers between devices with their start and end apart: 4, of which 4 were waited for; matrix products, arithmetic and copies ran while one was open for 6% of the time, Pallas kernels for 0%

commit v1 on v0

v1 whole, which is shorter than its diff:
```python
import math

import jax
import jax.numpy as jnp
from jax import lax
from jax.experimental import pallas as pl
from jax.experimental.pallas import tpu as pltpu
from jax.sharding import PartitionSpec as P

step_rate = 0.5
epsilon = 1e-06
F32 = jnp.float32
BF16 = jnp.bfloat16


def swap(x, bit, n_dp):
    return lax.ppermute(x, "dp", [(i, i ^ bit) for i in range(n_dp)])


def gather_blocks(w, n_dp):
    bits = [1 << i for i in range(1, n_dp.bit_length() - 1)]
    half = w.shape[0] // 2
    parts = []
    for rows, order in ((w[:half], bits), (w[half:], bits[::-1])):
        have = {0: rows}
        for bit in order:
            have.update({r ^ bit: swap(x, bit, n_dp) for r, x in list(have.items())})
        have.update({r ^ 1: swap(x, 1, n_dp) for r, x in list(have.items())})
        parts.append(have)
    return parts


def project(hidden, parts, qk_scale, cotangent, where):
    tok = hidden.shape[0]
    n_blocks = len(parts[0])
    half, width = parts[0][0].shape
    rows = 2 * half
    heads, size = qk_scale.shape

    def body(where_ref, h_ref, s_ref, c_ref, *rest):
        w_refs = rest[: 2 * n_blocks]
        out_ref, d_ref, dt_ref, acc = rest[2 * n_blocks :]
        step = pl.program_id(0)
        for r in range(n_blocks):

            @pl.when(step == r)
            def _():
                for side in range(2):
                    part = lax.dot_general(
                        h_ref[...], w_refs[2 * r + side][...], (((1,), (1,)), ((), ())), preferred_element_type=F32
                    )
                    at = slice(side * half, (side + 1) * half)
                    if r == 0:
                        acc[:, at] = part
                    else:
                        acc[:, at] += part

        @pl.when(step == n_blocks - 1)
        def _():
            for h in range(heads):
                k_at = slice(2 * h * size, (2 * h + 1) * size)
                v_at = slice((2 * h + 1) * size, (2 * h + 2) * size)
                key_raw = acc[:, k_at]
                length = jnp.sqrt(jnp.sum(key_raw * key_raw, -1, keepdims=True) + epsilon)
                unit = key_raw / length
                factor = s_ref[h : h + 1, :] * math.sqrt(size)
                out_ref[:, k_at] = (factor * unit).astype(BF16)
                out_ref[:, v_at] = acc[:, v_at].astype(BF16)
                along = factor * c_ref[:, k_at].astype(F32)
                grad = (along - unit * jnp.sum(unit * along, -1, keepdims=True)) / length
                d_ref[:, k_at] = grad.astype(BF16)
                d_ref[:, v_at] = c_ref[:, v_at]
                dt_ref[k_at, :] = grad.T.astype(BF16)
                dt_ref[v_at, :] = c_ref[:, v_at].astype(F32).T.astype(BF16)

    fixed = lambda i, where_ref: (0, 0)
    return pl.pallas_call(
        body,
        grid_spec=pltpu.PrefetchScalarGridSpec(
            num_scalar_prefetch=1,
            grid=(n_blocks,),
            in_specs=[
                pl.BlockSpec((tok, width), lambda i, where_ref: (0, where_ref[0] ^ i)),
                pl.BlockSpec((heads, size), fixed),
                pl.BlockSpec((tok, rows), fixed),
            ]
            + [pl.BlockSpec((half, width), fixed)] * (2 * n_blocks),
            out_specs=[
                pl.BlockSpec((tok, rows), fixed),
                pl.BlockSpec((tok, rows), fixed),
                pl.BlockSpec((rows, tok), fixed),
            ],
            scratch_shapes=[pltpu.VMEM((tok, rows), F32)],
        ),
        out_shape=[
            jax.ShapeDtypeStruct((tok, rows), BF16),
            jax.ShapeDtypeStruct((tok, rows), BF16),
            jax.ShapeDtypeStruct((rows, tok), BF16),
        ],
        name="project",
    )(where, hidden, qk_scale, cotangent, *[parts[s][r] for r in range(n_blocks) for s in range(2)])


def weight_grad(d_t, hidden, where, n_blocks, odd, dtype):
    rows, tok = d_t.shape
    width = hidden.shape[1] // n_blocks

    def body(where_ref, d_ref, h_ref, out_ref):
        out_ref[0] = jnp.dot(d_ref[...], h_ref[...], preferred_element_type=F32).astype(dtype)

    return pl.pallas_call(
        body,
        grid_spec=pltpu.PrefetchScalarGridSpec(
            num_scalar_prefetch=1,
            grid=(n_blocks // 2,),
            in_specs=[
                pl.BlockSpec((rows, tok), lambda i, where_ref: (0, 0)),
                pl.BlockSpec((tok, width), lambda i, where_ref: (0, where_ref[0] ^ (2 * i + odd))),
            ],
            out_specs=pl.BlockSpec((1, rows, width), lambda i, where_ref: (i, 0, 0)),
        ),
        out_shape=jax.ShapeDtypeStruct((n_blocks // 2, rows, width), dtype),
        name="weight_grad_odd" if odd else "weight_grad_even",
    )(where, d_t, hidden)


def hidden_grad(d_raw, parts, where):
    tok = d_raw.shape[0]
    n_blocks = len(parts[0])
    half, width = parts[0][0].shape

    def body(where_ref, d_ref, *rest):
        w_refs, out_ref = rest[:-1], rest[-1]
        step = pl.program_id(0)
        for r in range(n_blocks):

            @pl.when(step == r)
            def _():
                w = jnp.concatenate([w_refs[2 * r][...], w_refs[2 * r + 1][...]], 0)
                out_ref[...] = jnp.dot(d_ref[...], w, preferred_element_type=F32).astype(BF16)

    fixed = lambda i, where_ref: (0, 0)
    return pl.pallas_call(
        body,
        grid_spec=pltpu.PrefetchScalarGridSpec(
            num_scalar_prefetch=1,
            grid=(n_blocks,),
            in_specs=[pl.BlockSpec(d_raw.shape, fixed)] + [pl.BlockSpec((half, width), fixed)] * (2 * n_blocks),
            out_specs=pl.BlockSpec((tok, width), lambda i, where_ref: (0, where_ref[0] ^ i)),
        ),
        out_shape=jax.ShapeDtypeStruct((tok, n_blocks * width), BF16),
        name="hidden_grad",
    )(where, d_raw, *[parts[s][r] for r in range(n_blocks) for s in range(2)])


def scatter_sum(keep, sent, n_dp):
    total = keep + swap(sent, 1, n_dp).astype(F32)
    count = n_dp.bit_length() - 2
    rows, width = keep.shape[1:]
    total = total.reshape((2,) * count + (rows, width))
    half = rows // 2
    sides = []
    for at, order in ((0, list(range(count))), (half, list(range(count))[::-1])):
        part = lax.slice_in_dim(total, at, at + half, axis=count)
        left = list(range(count))[::-1]
        for b in order:
            axis = left.index(b)
            left.remove(b)
            go = lax.index_in_dim(part, 1, axis, keepdims=False).astype(BF16)
            stay = lax.index_in_dim(part, 0, axis, keepdims=False)
            part = stay + swap(go, 2 << b, n_dp).astype(F32)
        sides.append(part)
    return jnp.concatenate(sides, 0)


def local(hidden, weight, qk_scale, cotangent, n_dp):
    where = lax.axis_index("dp").astype(jnp.int32).reshape(1)
    parts = gather_blocks(weight, n_dp)
    keys_values, d_raw, d_t = project(hidden, parts, qk_scale, cotangent, where)
    sent = weight_grad(d_t, hidden, where, n_dp, 1, BF16)
    input_share = hidden_grad(d_raw, parts, where)
    keep = weight_grad(d_t, hidden, where, n_dp, 0, F32)
    input_grad = lax.psum_scatter(input_share, "tensor", scatter_dimension=0, tiled=True)
    grad = scatter_sum(keep, sent, n_dp)
    w = weight.astype(F32)
    sums = jnp.stack([jnp.sum(grad * w, 1), jnp.sum(w * w, 1), jnp.sum(grad * grad, 1)])
    bit = 1
    while bit < n_dp:
        sums = sums + swap(sums, bit, n_dp)
        bit *= 2
    gw, ww, gg = sums[0], sums[1], sums[2]
    ratio = gw / ww
    rate = step_rate * jnp.sqrt(ww / (gg + epsilon))
    norm_sq = ww + rate * rate * (gg - ratio * gw)
    scale = math.sqrt(n_dp * weight.shape[1]) / jnp.sqrt(norm_sq)
    moved = w - rate[:, None] * (grad - ratio[:, None] * w)
    new_weight = (scale[:, None] * moved).astype(BF16)
    return (keys_values, input_grad, new_weight)


def solution(mesh):
    in_specs = (P("dp", None), P("tensor", "dp"), P("tensor", None), P("dp", "tensor"))
    out_specs = (P("dp", "tensor"), P(("dp", "tensor"), None), P("tensor", "dp"))
    n_dp = mesh.shape["dp"]

    def body(hidden, weight, qk_scale, cotangent):
        return local(hidden, weight, qk_scale, cotangent, n_dp)

    return jax.shard_map(body, mesh=mesh, in_specs=in_specs, out_specs=out_specs, check_vma=False)
```

time: 330 us -> 206 us (0.62)
  waiting for transfers between devices: 278 us -> 136 us
  Pallas kernels: 0 us -> 30.9 us
  matrix products: 23.7 us -> 0 us
  starting transfers between devices: 0.16 us -> 17.6 us
  other arithmetic: 12.2 us -> 5.33 us
    reduce_scatter x2 -> x1, waiting for transfers between devices: 209 us -> 96.5 us  [local(): lax.psum_scatter(input_share, 'tensor', scatter_dimension=0, tiled=True)]
    all_gather x2 -> x0, waiting for transfers between devices: 67.8 us -> none  [the longest x1 39.5 us: local(): full_w = lax.all_gather(weight, 'dp', axis=1, tiled=True)]
    ppermute x0 -> x22, waiting for transfers between devices: none -> 39.6 us  [swap(): return lax.ppermute(x, 'dp', [(i, i ^ bit) for i in range(n_dp)])]
    pallas_call x0 -> x4, Pallas kernels: none -> 30.9 us  [the longest x1 11.4 us: project(): pl.pallas_call(body, grid_spec=pltpu.PrefetchScalarGridSpec(num_scalar_pr...]
    dot_general x3 -> x0, matrix products: 23.7 us -> none  [the longest x1 8.95 us: local(): jnp.einsum('tc,tr->cr', hidden, d_raw, preferred_element_type=jnp.float32)]
    ppermute x0 -> x22, starting transfers between devices: none -> 17.5 us  [swap(): return lax.ppermute(x, 'dp', [(i, i ^ bit) for i in range(n_dp)])]
    reduce_sum x4 -> x1, other arithmetic: 8.27 us -> 0.41 us  [local(): jnp.sum(grad * w, 1)]
    add x0 -> x7, other arithmetic: none -> 3.37 us  [the longest x1 2.87 us: scatter_sum(): total = keep + swap(sent, 1, n_dp).astype(F32)]
  transfers between devices with their start and end apart: 4 -> 23, of which waited for: 4 -> 14; matrix products, arithmetic and copies ran while one was open for 6% -> 3% of each run, Pallas kernels for 0% -> 5%
where the time goes in v1:
time: 206 us
  waiting for transfers between devices  136 us (66%)
  Pallas kernels  30.9 us (15%)
  starting transfers between devices  17.6 us (9%)
  between operations  14.3 us (7%)
  other arithmetic  5.33 us (3%)
    reduce_scatter x1, waiting for transfers between devices, local(): lax.psum_scatter(input_share, 'tensor', scatter_dimension=0, tiled=True)  96.5 us
    ppermute x22, waiting for transfers between devices, swap(): return lax.ppermute(x, 'dp', [(i, i ^ bit) for i in range(n_dp)])  39.6 us
    ppermute x22, starting transfers between devices, swap(): return lax.ppermute(x, 'dp', [(i, i ^ bit) for i in range(n_dp)])  17.5 us
    pallas_call x1, Pallas kernels, project(): pl.pallas_call(body, grid_spec=pltpu.PrefetchScalarGridSpec(num_scalar_pr...  11.4 us
    pallas_call x2, Pallas kernels, weight_grad(): pl.pallas_call(body, grid_spec=pltpu.PrefetchScalarGridSpec(num_scalar_pr...  10.9 us
    pallas_call x1, Pallas kernels, hidden_grad(): pl.pallas_call(body, grid_spec=pltpu.PrefetchScalarGridSpec(num_scalar_pr...  8.67 us
  transfers between devices with their start and end apart: 23, of which 14 were waited for; matrix products, arithmetic and copies ran while one was open for 3% of the time, Pallas kernels for 5%

profile of v1, /device:TPU:0, one launch (start us, length us, event | category | flops | bytes accessed | tf_op | source)
XLA Modules:
  0.0 205.5 jit_solution(12706903300744806391)
XLA Ops:
  7.2 1.1 fusion.13
  8.3 0.6 collective-permute-start
  8.9 2.6 %collective-permute-start.2 = (bf16[128,1024]{1,0:T(8,128)(2,1)S(1)}, bf16[128,1024]{1,0:T(8,128)(2,1)S(1)}, u32[]{:S(2)}, u32[]{:S(2)}) collective-permute-start(bf16[128,1024]{1,0:T(8,128)(2,1)S(1)} %get-tuple-element.17.rest_0_), channel_id=1, source_target_pairs={{0,8},{4,12},{8,0},{12,4},{16,24},{20,28},{24,16},{28,20},{1,9},{5... | collective-permute-start | bytes 786440 | tf_op jit(solution)/shard_map/ppermute | solution.py:17
  11.6 1.5 collective-permute-start.7
  13.1 0.5 collective-permute-start.3
  13.9 4.7 %collective-permute-done.2.rest_4_ = bf16[128,1024]{1,0:T(8,128)(2,1)S(1)} collective-permute-done((bf16[128,1024]{1,0:T(8,128)(2,1)S(1)}, bf16[128,1024]{1,0:T(8,128)(2,1)S(1)}, u32[]{:S(2)}, u32[]{:S(2)}) %collective-permute-start.2) | collective-permute-done | bytes 262176 | tf_op jit(solution)/shard_map/ppermute | solution.py:17
  18.6 2.1 %collective-permute-start.10 = (bf16[128,1024]{1,0:T(8,128)(2,1)S(1)}, bf16[128,1024]{1,0:T(8,128)(2,1)S(1)}, u32[]{:S(2)}, u32[]{:S(2)}) collective-permute-start(bf16[128,1024]{1,0:T(8,128)(2,1)S(1)} %collective-permute-done.2.rest_4_), channel_id=1, source_target_pairs={{0,16},{4,20},{8,24},{12,28},{16,0},{20,4},{24,8},{28,12},{1,17},{... | collective-permute-start | bytes 786440 | tf_op jit(solution)/shard_map/ppermute | solution.py:17
  20.7 1.5 collective-permute-start.11
  22.2 2.0 collective-permute-done.3.rest_5_
  24.2 2.2 %collective-permute-done.6.rest_8_ = bf16[128,1024]{1,0:T(8,128)(2,1)S(1)} collective-permute-done((bf16[128,1024]{1,0:T(8,128)(2,1)S(1)}, bf16[128,1024]{1,0:T(8,128)(2,1)S(1)}, u32[]{:S(2)}, u32[]{:S(2)}) %collective-permute-start.6) | collective-permute-done | bytes 262176 | tf_op jit(solution)/shard_map/ppermute | solution.py:17
  26.4 0.5 collective-permute-start.8
  26.9 4.5 %collective-permute-done.10.rest_12_ = bf16[128,1024]{1,0:T(8,128)(2,1)S(1)} collective-permute-done((bf16[128,1024]{1,0:T(8,128)(2,1)S(1)}, bf16[128,1024]{1,0:T(8,128)(2,1)S(1)}, u32[]{:S(2)}, u32[]{:S(2)}) %collective-permute-start.10) | collective-permute-done | bytes 262176 | tf_op jit(solution)/shard_map/ppermute | solution.py:17
  31.4 0.5 collective-permute-start.13
  31.9 1.1 collective-permute-done.12.rest_14_
  33.5 11.4 %project.1 = (bf16[512,256]{1,0:T(8,128)(2,1)}, bf16[512,256]{1,0:T(8,128)(2,1)}, bf16[256,512]{1,0:T(8,128)(2,1)}) custom-call(s32[1]{0:T(128)} %bitcast.where_ref, bf16[512,8192]{1,0:T(8,128)(2,1)} %h_ref.5, f32[1,128]{1,0:T(1,128)} %s_ref.1, bf16[512,256]{1,0:T(8,128)(2,1)} %c_ref.1, bf16[128,1024]{1,0:T(8,128)(2,1)} %copy-done.2, ...), custom_call_target="tpu_custom_call" | custom-call | tf_op jit(solution)/shard_map/project/pallas_call | solution.py:77
  44.9 8.7 %hidden_grad.1 = bf16[512,8192]{1,0:T(8,128)(2,1)} custom-call(s32[1]{0:T(128)} %bitcast.where_ref, bf16[512,256]{1,0:T(8,128)(2,1)} %get-tuple-element.7.d_ref, bf16[128,1024]{1,0:T(8,128)(2,1)} %copy-done.2, bf16[128,1024]{1,0:T(8,128)(2,1)} %copy-done.1, bf16[128,1024]{1,0:T(8,128)(2,1)} %copy-done.3, bf16[128,1024]{1,0:T(8,128)(2,1)} %copy-done.5, ...), custom_call_target="tpu_custom_call" | custom-call | tf_op jit(solution)/shard_map/hidden_grad/pallas_call | solution.py:143
  53.6 5.1 %weight_grad_odd.1 = bf16[4,256,1024]{2,1,0:T(8,128)(2,1)} custom-call(s32[1]{0:T(128)} %bitcast.where_ref, bf16[256,512]{1,0:T(8,128)(2,1)} %get-tuple-element.8.d_ref, bf16[512,8192]{1,0:T(8,128)(2,1)} %h_ref.5), custom_call_target="tpu_custom_call" | custom-call | tf_op jit(solution)/shard_map/weight_grad_odd/pallas_call | solution.py:111
  58.9 5.8 %weight_grad_even.1 = f32[4,256,1024]{2,1,0:T(8,128)} custom-call(s32[1]{0:T(128)} %bitcast.where_ref, bf16[256,512]{1,0:T(8,128)(2,1)} %get-tuple-element.8.d_ref, bf16[512,8192]{1,0:T(8,128)(2,1)} %h_ref.5), custom_call_target="tpu_custom_call" | custom-call | tf_op jit(solution)/shard_map/weight_grad_even/pallas_call | solution.py:111
  64.7 2.9 %convert_add_fusion = f32[4,256,1024]{2,1,0:T(8,128)S(1)} fusion(f32[4,256,1024]{2,1,0:T(8,128)} %weight_grad_even.1, bf16[4,256,1024]{2,1,0:T(8,128)(2,1)S(1)} %collective-permute-done.14), kind=kLoop, calls=%fused_computation | loop fusion | flops 2097152 | bytes 10485760 | tf_op jit(solution)/shard_map/add | solution.py:157
  68.3 1.7 collective-permute-start.17
  70.0 12.2 %collective-permute-done.15 = bf16[2,128,1024]{2,1,0:T(8,128)(2,1)S(1)} collective-permute-done((bf16[2,128,1024]{2,1,0:T(8,128)(2,1)S(1)}, bf16[2,128,1024]{2,1,0:T(8,128)(2,1)S(1)}, u32[]{:S(2)}, u32[]{:S(2)}) %collective-permute-start.15) | collective-permute-done | bytes 524320 | tf_op jit(solution)/shard_map/ppermute | solution.py:17
  82.7 1.7 collective-permute-start.18
  84.4 1.4 collective-permute-start.16
  85.9 4.6 %collective-permute-done.18 = bf16[128,1024]{1,0:T(8,128)(2,1)S(1)} collective-permute-done((bf16[128,1024]{1,0:T(8,128)(2,1)S(1)}, bf16[128,1024]{1,0:T(8,128)(2,1)S(1)}, u32[]{:S(2)}, u32[]{:S(2)}) %collective-permute-start.18) | collective-permute-done | bytes 262176 | tf_op jit(solution)/shard_map/ppermute | solution.py:17
  90.6 1.2 collective-permute-done.16
  92.4 1.2 collective-permute-done.19
  93.5 0.6 collective-permute-start.20
  94.2 3.0 %collective-permute-done.20 = f32[3,256]{1,0:T(4,128)S(1)} collective-permute-done((f32[3,256]{1,0:T(4,128)S(1)}, f32[3,256]{1,0:T(4,128)S(1)}, u32[]{:S(2)}, u32[]{:S(2)}) %collective-permute-start.20) | collective-permute-done | bytes 3104 | tf_op jit(solution)/shard_map/ppermute | solution.py:17
  97.2 1.4 collective-permute-start.21
  98.6 2.3 %collective-permute-done.21 = f32[3,256]{1,0:T(4,128)S(1)} collective-permute-done((f32[3,256]{1,0:T(4,128)S(1)}, f32[3,256]{1,0:T(4,128)S(1)}, u32[]{:S(2)}, u32[]{:S(2)}) %collective-permute-start.21) | collective-permute-done | bytes 3104 | tf_op jit(solution)/shard_map/ppermute | solution.py:17
  100.9 1.2 fusion.5
  102.1 96.5 %reduce-scatter.2.cloned.1.call-done = bf16[128,8192]{1,0:T(8,128)(2,1)} async-done(((bf16[512,8192]{1,0:T(8,128)(2,1)}), bf16[128,8192]{1,0:T(8,128)(2,1)}) %reduce-scatter.2.cloned.1.call-update) | async-done | bytes 2097168 | tf_op jit(solution)/shard_map/reduce_scatter | solution.py:183
  (65 shorter events, 3.0 us)
Async XLA Ops:
  7.2 191.5 %reduce-scatter.2.cloned.1.call-start = ((), (), s32[]{:S(2)}) async-start(), calls=%async_computation.1 | async-start | bytes 10485760 | tf_op jit(solution)/shard_map/reduce_scatter | solution.py:183
  8.3 25.1 %copy-start.1 = (bf16[128,1024]{1,0:T(8,128)(2,1)}, bf16[128,1024]{1,0:T(8,128)(2,1)S(1)}, u32[]{:S(2)}) copy-start(bf16[128,1024]{1,0:T(8,128)(2,1)S(1)} %get-tuple-element.16.rest_1_) | copy-start | bytes 786436
  8.3 25.1 %copy-start.2 = (bf16[128,1024]{1,0:T(8,128)(2,1)}, bf16[128,1024]{1,0:T(8,128)(2,1)S(1)}, u32[]{:S(2)}) copy-start(bf16[128,1024]{1,0:T(8,128)(2,1)S(1)} %get-tuple-element.17.rest_0_) | copy-start | bytes 786436
  8.3 5.3 %collective-permute-start = (bf16[128,1024]{1,0:T(8,128)(2,1)S(1)}, bf16[128,1024]{1,0:T(8,128)(2,1)S(1)}, u32[]{:S(2)}, u32[]{:S(2)}) collective-permute-start(bf16[128,1024]{1,0:T(8,128)(2,1)S(1)} %get-tuple-element.17.rest_0_), channel_id=1, source_target_pairs={{0,4},{4,0},{8,12},{12,8},{16,20},{20,16},{24,28},{28,24},{1,5},{5... | collective-permute-start | bytes 786440 | tf_op jit(solution)/shard_map/ppermute | solution.py:17
  8.9 9.7 %collective-permute-start.2 = (bf16[128,1024]{1,0:T(8,128)(2,1)S(1)}, bf16[128,1024]{1,0:T(8,128)(2,1)S(1)}, u32[]{:S(2)}, u32[]{:S(2)}) collective-permute-start(bf16[128,1024]{1,0:T(8,128)(2,1)S(1)} %get-tuple-element.17.rest_0_), channel_id=1, source_target_pairs={{0,8},{4,12},{8,0},{12,4},{16,24},{20,28},{24,16},{28,20},{1,9},{5... | collective-permute-start | bytes 786440 | tf_op jit(solution)/shard_map/ppermute | solution.py:17
  11.4 7.2 %collective-permute-start.1 = (bf16[128,1024]{1,0:T(8,128)(2,1)S(1)}, bf16[128,1024]{1,0:T(8,128)(2,1)S(1)}, u32[]{:S(2)}, u32[]{:S(2)}) collective-permute-start(bf16[128,1024]{1,0:T(8,128)(2,1)S(1)} %get-tuple-element.16.rest_1_), channel_id=1, source_target_pairs={{0,4},{4,0},{8,12},{12,8},{16,20},{20,16},{24,28},{28,24},{1,5},{5... | collective-permute-start | bytes 786440 | tf_op jit(solution)/shard_map/ppermute | solution.py:17
  11.6 9.2 %collective-permute-start.7 = (bf16[128,1024]{1,0:T(8,128)(2,1)S(1)}, bf16[128,1024]{1,0:T(8,128)(2,1)S(1)}, u32[]{:S(2)}, u32[]{:S(2)}) collective-permute-start(bf16[128,1024]{1,0:T(8,128)(2,1)S(1)} %get-tuple-element.16.rest_1_), channel_id=1, source_target_pairs={{0,16},{4,20},{8,24},{12,28},{16,0},{20,4},{24,8},{28,12},{1,17},{... | collective-permute-start | bytes 786440 | tf_op jit(solution)/shard_map/ppermute | solution.py:17
  13.1 11.1 %collective-permute-start.3 = (bf16[128,1024]{1,0:T(8,128)(2,1)S(1)}, bf16[128,1024]{1,0:T(8,128)(2,1)S(1)}, u32[]{:S(2)}, u32[]{:S(2)}) collective-permute-start(bf16[128,1024]{1,0:T(8,128)(2,1)S(1)} %get-tuple-element.16.rest_1_), channel_id=1, source_target_pairs={{0,8},{4,12},{8,0},{12,4},{16,24},{20,28},{24,16},{28,20},{1,9},{5... | collective-permute-start | bytes 786440 | tf_op jit(solution)/shard_map/ppermute | solution.py:17
  13.6 19.8 %copy-start.3 = (bf16[128,1024]{1,0:T(8,128)(2,1)}, bf16[128,1024]{1,0:T(8,128)(2,1)S(1)}, u32[]{:S(2)}) copy-start(bf16[128,1024]{1,0:T(8,128)(2,1)S(1)} %collective-permute-done.rest_2_) | copy-start | bytes 786436
  13.6 12.7 %collective-permute-start.6 = (bf16[128,1024]{1,0:T(8,128)(2,1)S(1)}, bf16[128,1024]{1,0:T(8,128)(2,1)S(1)}, u32[]{:S(2)}, u32[]{:S(2)}) collective-permute-start(bf16[128,1024]{1,0:T(8,128)(2,1)S(1)} %get-tuple-element.17.rest_0_), channel_id=1, source_target_pairs={{0,16},{4,20},{8,24},{12,28},{16,0},{20,4},{24,8},{28,12},{1,17},{... | collective-permute-start | bytes 786440 | tf_op jit(solution)/shard_map/ppermute | solution.py:17
  18.6 14.9 %copy-start.4 = (bf16[128,1024]{1,0:T(8,128)(2,1)}, bf16[128,1024]{1,0:T(8,128)(2,1)S(1)}, u32[]{:S(2)}) copy-start(bf16[128,1024]{1,0:T(8,128)(2,1)S(1)} %collective-permute-done.2.rest_4_) | copy-start | bytes 786436
  18.6 7.8 %collective-permute-start.4 = (bf16[128,1024]{1,0:T(8,128)(2,1)S(1)}, bf16[128,1024]{1,0:T(8,128)(2,1)S(1)}, u32[]{:S(2)}, u32[]{:S(2)}) collective-permute-start(bf16[128,1024]{1,0:T(8,128)(2,1)S(1)} %collective-permute-done.2.rest_4_), channel_id=1, source_target_pairs={{0,4},{4,0},{8,12},{12,8},{16,20},{20,16},{24,28},{28,24},{1,5},{5... | collective-permute-start | bytes 786440 | tf_op jit(solution)/shard_map/ppermute | solution.py:17
  18.6 14.9 %copy-start.5 = (bf16[128,1024]{1,0:T(8,128)(2,1)}, bf16[128,1024]{1,0:T(8,128)(2,1)S(1)}, u32[]{:S(2)}) copy-start(bf16[128,1024]{1,0:T(8,128)(2,1)S(1)} %collective-permute-done.1.rest_3_) | copy-start | bytes 786436
  18.6 12.8 %collective-permute-start.10 = (bf16[128,1024]{1,0:T(8,128)(2,1)S(1)}, bf16[128,1024]{1,0:T(8,128)(2,1)S(1)}, u32[]{:S(2)}, u32[]{:S(2)}) collective-permute-start(bf16[128,1024]{1,0:T(8,128)(2,1)S(1)} %collective-permute-done.2.rest_4_), channel_id=1, source_target_pairs={{0,16},{4,20},{8,24},{12,28},{16,0},{20,4},{24,8},{28,12},{1,17},{... | collective-permute-start | bytes 786440 | tf_op jit(solution)/shard_map/ppermute | solution.py:17
  20.7 12.7 %copy-start.6 = (bf16[128,1024]{1,0:T(8,128)(2,1)}, bf16[128,1024]{1,0:T(8,128)(2,1)S(1)}, u32[]{:S(2)}) copy-start(bf16[128,1024]{1,0:T(8,128)(2,1)S(1)} %collective-permute-done.7.rest_9_) | copy-start | bytes 786436
  20.7 10.6 %collective-permute-start.11 = (bf16[128,1024]{1,0:T(8,128)(2,1)S(1)}, bf16[128,1024]{1,0:T(8,128)(2,1)S(1)}, u32[]{:S(2)}, u32[]{:S(2)}) collective-permute-start(bf16[128,1024]{1,0:T(8,128)(2,1)S(1)} %collective-permute-done.7.rest_9_), channel_id=1, source_target_pairs={{0,8},{4,12},{8,0},{12,4},{16,24},{20,28},{24,16},{28,20},{1,9},{5... | collective-permute-start | bytes 786440 | tf_op jit(solution)/shard_map/ppermute | solution.py:17
  24.2 9.3 %copy-start.7 = (bf16[128,1024]{1,0:T(8,128)(2,1)}, bf16[128,1024]{1,0:T(8,128)(2,1)S(1)}, u32[]{:S(2)}) copy-start(bf16[128,1024]{1,0:T(8,128)(2,1)S(1)} %collective-permute-done.3.rest_5_) | copy-start | bytes 786436
  24.2 7.7 %collective-permute-start.9 = (bf16[128,1024]{1,0:T(8,128)(2,1)S(1)}, bf16[128,1024]{1,0:T(8,128)(2,1)S(1)}, u32[]{:S(2)}, u32[]{:S(2)}) collective-permute-start(bf16[128,1024]{1,0:T(8,128)(2,1)S(1)} %collective-permute-done.7.rest_9_), channel_id=1, source_target_pairs={{0,4},{4,0},{8,12},{12,8},{16,20},{20,16},{24,28},{28,24},{1,5},{5... | collective-permute-start | bytes 786440 | tf_op jit(solution)/shard_map/ppermute | solution.py:17
  26.4 7.1 %copy-start.8 = (bf16[128,1024]{1,0:T(8,128)(2,1)}, bf16[128,1024]{1,0:T(8,128)(2,1)S(1)}, u32[]{:S(2)}) copy-start(bf16[128,1024]{1,0:T(8,128)(2,1)S(1)} %collective-permute-done.6.rest_8_) | copy-start | bytes 786436
  26.4 5.5 %collective-permute-start.5 = (bf16[128,1024]{1,0:T(8,128)(2,1)S(1)}, bf16[128,1024]{1,0:T(8,128)(2,1)S(1)}, u32[]{:S(2)}, u32[]{:S(2)}) collective-permute-start(bf16[128,1024]{1,0:T(8,128)(2,1)S(1)} %collective-permute-done.3.rest_5_), channel_id=1, source_target_pairs={{0,4},{4,0},{8,12},{12,8},{16,20},{20,16},{24,28},{28,24},{1,5},{5... | collective-permute-start | bytes 786440 | tf_op jit(solution)/shard_map/ppermute | solution.py:17
  26.4 5.5 %collective-permute-start.8 = (bf16[128,1024]{1,0:T(8,128)(2,1)S(1)}, bf16[128,1024]{1,0:T(8,128)(2,1)}, u32[]{:S(2)}, u32[]{:S(2)}) collective-permute-start(bf16[128,1024]{1,0:T(8,128)(2,1)S(1)} %collective-permute-done.6.rest_8_), channel_id=1, source_target_pairs={{0,4},{4,0},{8,12},{12,8},{16,20},{20,16},{24,28},{28,24},{1,5},{5... | collective-permute-start | bytes 786440 | tf_op jit(solution)/shard_map/ppermute | solution.py:17
  31.4 1.7 collective-permute-start.12
  31.4 2.0 collective-permute-start.13
  58.7 5.9 %collective-permute-start.14 = (bf16[4,256,1024]{2,1,0:T(8,128)(2,1)}, bf16[4,256,1024]{2,1,0:T(8,128)(2,1)S(1)}, u32[]{:S(2)}, u32[]{:S(2)}) collective-permute-start(bf16[4,256,1024]{2,1,0:T(8,128)(2,1)} %weight_grad_odd.1), channel_id=1, source_target_pairs={{0,4},{4,0},{8,12},{12,8},{16,20},{20,16},{24,28},{28,24},{1,5},{5... | collective-permute-start | bytes 6291464 | tf_op jit(solution)/shard_map/ppermute | solution.py:17
  67.9 23.9 %copy-start = (bf16[256,1024]{1,0:T(8,128)(2,1)S(1)}, bf16[256,1024]{1,0:T(8,128)(2,1)}, u32[]{:S(2)}) copy-start(bf16[256,1024]{1,0:T(8,128)(2,1)} %param.5) | copy-start | bytes 1572868
  68.0 14.3 %collective-permute-start.15 = (bf16[2,128,1024]{2,1,0:T(8,128)(2,1)S(1)}, bf16[2,128,1024]{2,1,0:T(8,128)(2,1)S(1)}, u32[]{:S(2)}, u32[]{:S(2)}) collective-permute-start(bf16[2,128,1024]{2,1,0:T(8,128)(2,1)S(1)} %slice_bitcast_fusion.5), channel_id=1, source_target_pairs={{0,8},{4,12},{8,0},{12,4},{16,24},{20,28},{24,16},{28,20},{1,9},{5... | collective-permute-start | bytes 1572872 | tf_op jit(solution)/shard_map/ppermute | solution.py:17
  68.3 14.0 %collective-permute-start.17 = (bf16[2,128,1024]{2,1,0:T(8,128)(2,1)S(1)}, bf16[2,128,1024]{2,1,0:T(8,128)(2,1)S(1)}, u32[]{:S(2)}, u32[]{:S(2)}) collective-permute-start(bf16[2,128,1024]{2,1,0:T(8,128)(2,1)S(1)} %slice_bitcast_fusion.3), channel_id=1, source_target_pairs={{0,16},{4,20},{8,24},{12,28},{16,0},{20,4},{24,8},{28,12},{1,17},{... | collective-permute-start | bytes 1572872 | tf_op jit(solution)/shard_map/ppermute | solution.py:17
  82.7 7.8 %collective-permute-start.18 = (bf16[128,1024]{1,0:T(8,128)(2,1)S(1)}, bf16[128,1024]{1,0:T(8,128)(2,1)S(1)}, u32[]{:S(2)}, u32[]{:S(2)}) collective-permute-start(bf16[128,1024]{1,0:T(8,128)(2,1)S(1)} %fusion.11), channel_id=1, source_target_pairs={{0,8},{4,12},{8,0},{12,4},{16,24},{20,28},{24,16},{28,20},{1,9},{5... | collective-permute-start | bytes 786440 | tf_op jit(solution)/shard_map/ppermute | solution.py:17
  84.4 7.3 %collective-permute-start.16 = (bf16[128,1024]{1,0:T(8,128)(2,1)S(1)}, bf16[128,1024]{1,0:T(8,128)(2,1)S(1)}, u32[]{:S(2)}, u32[]{:S(2)}) collective-permute-start(bf16[128,1024]{1,0:T(8,128)(2,1)S(1)} %fusion.10), channel_id=1, source_target_pairs={{0,16},{4,20},{8,24},{12,28},{16,0},{20,4},{24,8},{28,12},{1,17},{... | collective-permute-start | bytes 786440 | tf_op jit(solution)/shard_map/ppermute | solution.py:17
  92.3 1.2 collective-permute-start.19
  93.5 3.7 %collective-permute-start.20 = (f32[3,256]{1,0:T(4,128)S(1)}, f32[3,256]{1,0:T(4,128)S(1)}, u32[]{:S(2)}, u32[]{:S(2)}) collective-permute-start(f32[3,256]{1,0:T(4,128)S(1)} %fusion.12), channel_id=1, source_target_pairs={{0,8},{4,12},{8,0},{12,4},{16,24},{20,28},{24,16},{28,20},{1,9},{5... | collective-permute-start | bytes 9224 | tf_op jit(solution)/shard_map/ppermute | solution.py:17
  97.2 3.7 %collective-permute-start.21 = (f32[3,256]{1,0:T(4,128)S(1)}, f32[3,256]{1,0:T(4,128)S(1)}, u32[]{:S(2)}, u32[]{:S(2)}) collective-permute-start(f32[3,256]{1,0:T(4,128)S(1)} %fusion.15), channel_id=1, source_target_pairs={{0,16},{4,20},{8,24},{12,28},{16,0},{20,4},{24,8},{28,12},{1,17},{... | collective-permute-start | bytes 9224 | tf_op jit(solution)/shard_map/ppermute | solution.py:17
  (5 other events, 14.6 us)
Sparse Core Ops, SparseCore 0:
  53.7 144.9 reduce-scatter.1

commit v2 on v1

--- a/solution.py
+++ b/solution.py
@@ -30,12 +30,13 @@
     return parts
 
 
-def project(hidden, parts, qk_scale, cotangent, where):
+def project(hidden, parts, qk_scale, cotangent, where, n_tensor):
     tok = hidden.shape[0]
     n_blocks = len(parts[0])
     half, width = parts[0][0].shape
     rows = 2 * half
     heads, size = qk_scale.shape
+    chunk = tok // n_tensor
 
     def body(where_ref, h_ref, s_ref, c_ref, *rest):
         w_refs = rest[: 2 * n_blocks]
@@ -45,15 +46,12 @@
 
             @pl.when(step == r)
             def _():
-                for side in range(2):
-                    part = lax.dot_general(
-                        h_ref[...], w_refs[2 * r + side][...], (((1,), (1,)), ((), ())), preferred_element_type=F32
-                    )
-                    at = slice(side * half, (side + 1) * half)
-                    if r == 0:
-                        acc[:, at] = part
-                    else:
-                        acc[:, at] += part
+                w = jnp.concatenate([w_refs[2 * r][...], w_refs[2 * r + 1][...]], 0)
+                part = lax.dot_general(h_ref[...], w, (((1,), (1,)), ((), ())), preferred_element_type=F32)
+                if r == 0:
+                    acc[...] = part
+                else:
+                    acc[...] += part
 
         @pl.when(step == n_blocks - 1)
         def _():
@@ -68,8 +66,11 @@
                 out_ref[:, v_at] = acc[:, v_at].astype(BF16)
                 along = factor * c_ref[:, k_at].astype(F32)
                 grad = (along - unit * jnp.sum(unit * along, -1, keepdims=True)) / length
-                d_ref[:, k_at] = grad.astype(BF16)
-                d_ref[:, v_at] = c_ref[:, v_at]
+                for j in range(n_tensor):
+                    slot = lax.rem(where_ref[1] + (n_tensor - j), n_tensor)
+                    at = slice(j * chunk, (j + 1) * chunk)
+                    d_ref[slot, :, k_at] = grad[at].astype(BF16)
+                    d_ref[slot, :, v_at] = c_ref[at, v_at]
                 dt_ref[k_at, :] = grad.T.astype(BF16)
                 dt_ref[v_at, :] = c_ref[:, v_at].astype(F32).T.astype(BF16)
 
@@ -87,14 +88,14 @@
             + [pl.BlockSpec((half, width), fixed)] * (2 * n_blocks),
             out_specs=[
                 pl.BlockSpec((tok, rows), fixed),
-                pl.BlockSpec((tok, rows), fixed),
+                pl.BlockSpec((n_tensor, chunk, rows), lambda i, where_ref: (0, 0, 0)),
                 pl.BlockSpec((rows, tok), fixed),
             ],
             scratch_shapes=[pltpu.VMEM((tok, rows), F32)],
         ),
         out_shape=[
             jax.ShapeDtypeStruct((tok, rows), BF16),
-            jax.ShapeDtypeStruct((tok, rows), BF16),
+            jax.ShapeDtypeStruct((n_tensor, chunk, rows), BF16),
             jax.ShapeDtypeStruct((rows, tok), BF16),
         ],
         name="project",
@@ -124,33 +125,138 @@
     )(where, d_t, hidden)
 
 
-def hidden_grad(d_raw, parts, where):
-    tok = d_raw.shape[0]
-    n_blocks = len(parts[0])
+def shift(x, by, n_tensor):
+    return lax.ppermute(x, "tensor", [(i, (i - by) % n_tensor) for i in range(n_tensor)])
+
+
+def gather_others(w, n_tensor, n_dp):
+    half = w.shape[0] // 2
+    slots = {1: shift(w, 1, n_tensor), n_tensor - 1: shift(w, -1, n_tensor)}
+    for k in range(2, n_tensor - 1):
+        low = shift(slots[1][:half], k - 1, n_tensor)
+        high = shift(slots[n_tensor - 1][half:], k + 1, n_tensor)
+        slots[k] = jnp.concatenate([low, high], 0)
+    rest = {}
+    bit = 2
+    while bit < n_dp:
+        for k, x in slots.items():
+            rest[bit, k] = swap(x, bit, n_dp)
+        bit *= 2
+    rest.update({(0, k): x for k, x in slots.items()})
+    rest.update({(r ^ 1, k): swap(x, 1, n_dp) for (r, k), x in list(rest.items())})
+    return rest
+
+
+def hidden_share(d_slots, parts, blocks):
+    n_tensor, chunk, rows = d_slots.shape
     half, width = parts[0][0].shape
 
-    def body(where_ref, d_ref, *rest):
+    def body(d_ref, *rest):
         w_refs, out_ref = rest[:-1], rest[-1]
         step = pl.program_id(0)
-        for r in range(n_blocks):
-
-            @pl.when(step == r)
+        d = d_ref[...].reshape(n_tensor * chunk, rows)
+        for i in range(len(blocks)):
+
+            @pl.when(step == i)
             def _():
-                w = jnp.concatenate([w_refs[2 * r][...], w_refs[2 * r + 1][...]], 0)
-                out_ref[...] = jnp.dot(d_ref[...], w, preferred_element_type=F32).astype(BF16)
+                w = jnp.concatenate([w_refs[2 * i][...], w_refs[2 * i + 1][...]], 0)
+                out = jnp.dot(d, w, preferred_element_type=F32).astype(BF16)
+                out_ref[...] = out.reshape(n_tensor, chunk, width)
+
+    return pl.pallas_call(
+        body,
+        grid=(len(blocks),),
+        in_specs=[pl.BlockSpec(d_slots.shape, lambda i: (0, 0, 0))]
+        + [pl.BlockSpec((half, width), lambda i: (0, 0))] * (2 * len(blocks)),
+        out_specs=pl.BlockSpec((n_tensor, chunk, width), lambda i: (0, 0, i)),
+        out_shape=jax.ShapeDtypeStruct((n_tensor, chunk, len(blocks) * width), BF16),
+        name="hidden_share",
+    )(d_slots, *[parts[s][r] for r in blocks for s in range(2)])
+
+
+def hidden_grad(d_own, d_rest, parts, others, where, blocks, into):
+    n_tensor = len(d_rest) + 1
+    chunk, rows = d_own.shape
+    half, width = parts[0][0].shape
+    n_blocks = len(parts[0])
+    per = n_tensor + 1
+
+    def body(where_ref, *rest):
+        d_refs = rest[:n_tensor]
+        w_refs = rest[n_tensor : n_tensor + per * len(blocks)]
+        out_ref = rest[-1]
+        step = pl.program_id(0)
+        for i in range(len(blocks)):
+
+            @pl.when(step == i)
+            def _():
+                mine = w_refs[per * i : per * (i + 1)]
+                w = jnp.concatenate([mine[0][...], mine[1][...]], 0)
+                total = jnp.dot(d_refs[0][...], w, preferred_element_type=F32)
+                for k in range(1, n_tensor):
+                    total += jnp.dot(d_refs[k][...], mine[k + 1][...], preferred_element_type=F32)
+                out_ref[...] = total.astype(BF16)
 
     fixed = lambda i, where_ref: (0, 0)
+
+    def column(i, where_ref):
+        r = blocks[-1]
+        for at in range(len(blocks) - 2, -1, -1):
+            r = jnp.where(i == at, blocks[at], r)
+        return (0, where_ref[0] ^ r)
+
+    operands = [d_own, *d_rest]
+    specs = [pl.BlockSpec((chunk, rows), fixed)] * n_tensor
+    for r in blocks:
+        operands += [parts[0][r], parts[1][r]] + [others[r, k] for k in range(1, n_tensor)]
+        specs += [pl.BlockSpec((half, width), fixed)] * 2 + [pl.BlockSpec((rows, width), fixed)] * (n_tensor - 1)
+    aliases = {}
+    if into is not None:
+        operands.append(into)
+        specs.append(pl.BlockSpec(memory_space=pl.ANY))
+        aliases = {len(operands): 0}
     return pl.pallas_call(
         body,
         grid_spec=pltpu.PrefetchScalarGridSpec(
             num_scalar_prefetch=1,
-            grid=(n_blocks,),
-            in_specs=[pl.BlockSpec(d_raw.shape, fixed)] + [pl.BlockSpec((half, width), fixed)] * (2 * n_blocks),
-            out_specs=pl.BlockSpec((tok, width), lambda i, where_ref: (0, where_ref[0] ^ i)),
+            grid=(len(blocks),),
+            in_specs=specs,
+            out_specs=pl.BlockSpec((chunk, width), column),
         ),
-        out_shape=jax.ShapeDtypeStruct((tok, n_blocks * width), BF16),
+        out_shape=jax.ShapeDtypeStruct((chunk, n_blocks * width), BF16),
+        input_output_aliases=aliases,
         name="hidden_grad",
-    )(where, d_raw, *[parts[s][r] for r in range(n_blocks) for s in range(2)])
+    )(where, *operands)
+
+
+def add_shares(shares, where, blocks, width, into):
+    chunk = shares[0].shape[0]
+
+    def body(where_ref, *rest):
+        total = rest[0][...].astype(F32)
+        for ref in rest[1 : len(shares)]:
+            total += ref[...].astype(F32)
+        rest[-1][...] = total.astype(BF16)
+
+    def column(i, where_ref):
+        r = blocks[-1]
+        for at in range(len(blocks) - 2, -1, -1):
+            r = jnp.where(i == at, blocks[at], r)
+        return (0, where_ref[0] ^ r)
+
+    return pl.pallas_call(
+        body,
+        grid_spec=pltpu.PrefetchScalarGridSpec(
+            num_scalar_prefetch=1,
+            grid=(len(blocks),),
+            in_specs=[pl.BlockSpec((chunk, width), lambda i, where_ref: (0, i))] * len(shares)
+            + [pl.BlockSpec(memory_space=pl.ANY)],
+            out_specs=pl.BlockSpec((chunk, width), column),
+        ),
+        out_shape=jax.ShapeDtypeStruct(into.shape, BF16),
+        input_output_aliases={len(shares) + 1: 0},
+        name="add_shares",
+    )(where, *shares, into)
 
 
 def scatter_sum(keep, sent, n_dp):
@@ -173,14 +279,23 @@
     return jnp.concatenate(sides, 0)
 
 
-def local(hidden, weight, qk_scale, cotangent, n_dp):
-    where = lax.axis_index("dp").astype(jnp.int32).reshape(1)
+def local(hidden, weight, qk_scale, cotangent, n_dp, n_tensor):
+    width = weight.shape[1]
+    where = jnp.stack([lax.axis_index("dp"), lax.axis_index("tensor")]).astype(jnp.int32)
     parts = gather_blocks(weight, n_dp)
-    keys_values, d_raw, d_t = project(hidden, parts, qk_scale, cotangent, where)
+    others = gather_others(weight, n_tensor, n_dp)
+    keys_values, d_slots, d_t = project(hidden, parts, qk_scale, cotangent, where, n_tensor)
+    near = [0, 1]
+    linked = sorted({r for r, k in others} - set(near))
+    far = [r for r in range(n_dp) if r not in near and r not in linked]
     sent = weight_grad(d_t, hidden, where, n_dp, 1, BF16)
-    input_share = hidden_grad(d_raw, parts, where)
+    share = hidden_share(d_slots, parts, far)
     keep = weight_grad(d_t, hidden, where, n_dp, 0, F32)
-    input_grad = lax.psum_scatter(input_share, "tensor", scatter_dimension=0, tiled=True)
+    d_rest = [shift(d_slots[k], k, n_tensor) for k in range(1, n_tensor)]
+    shares = [share[0]] + [shift(share[k], k, n_tensor) for k in range(1, n_tensor)]
+    input_grad = hidden_grad(d_slots[0], d_rest, parts, others, where, near, None)
+    input_grad = hidden_grad(d_slots[0], d_rest, parts, others, where, linked, input_grad)
+    input_grad = add_shares(shares, where, far, width, input_grad)
     grad = scatter_sum(keep, sent, n_dp)
     w = weight.astype(F32)
     sums = jnp.stack([jnp.sum(grad * w, 1), jnp.sum(w * w, 1), jnp.sum(grad * grad, 1)])
@@ -201,9 +316,9 @@
 def solution(mesh):
     in_specs = (P("dp", None), P("tensor", "dp"), P("tensor", None), P("dp", "tensor"))
     out_specs = (P("dp", "tensor"), P(("dp", "tensor"), None), P("tensor", "dp"))
-    n_dp = mesh.shape["dp"]
+    n_dp, n_tensor = mesh.shape["dp"], mesh.shape["tensor"]
 
     def body(hidden, weight, qk_scale, cotangent):
-        return local(hidden, weight, qk_scale, cotangent, n_dp)
+        return local(hidden, weight, qk_scale, cotangent, n_dp, n_tensor)
 
     return jax.shard_map(body, mesh=mesh, in_specs=in_specs, out_specs=out_specs, check_vma=False)

time: 206 us -> 188 us (0.913)
  waiting for transfers between devices: 136 us -> 88.9 us
  starting transfers between devices: 17.6 us -> 42.6 us
  between operations: 14.3 us -> 1.08 us
  Pallas kernels: 30.9 us -> 41.1 us
  local copies, waits for them, and re-layouts: 1.27 us -> 7.59 us
    reduce_scatter x1 -> x0, waiting for transfers between devices: 96.5 us -> none  [local(): lax.psum_scatter(input_share, 'tensor', scatter_dimension=0, tiled=True)]
    ppermute x0 -> x10, waiting for transfers between devices: none -> 49.7 us  [shift(): lax.ppermute(x, 'tensor', [(i, (i - by) % n_tensor) for i in range(n_tens...]
    ppermute x0 -> x10, starting transfers between devices: none -> 15.9 us  [shift(): lax.ppermute(x, 'tensor', [(i, (i - by) % n_tensor) for i in range(n_tens...]
    ppermute x22 -> x37, starting transfers between devices: 17.5 us -> 26.7 us  [swap(): return lax.ppermute(x, 'dp', [(i, i ^ bit) for i in range(n_dp)])]
    pallas_call x0 -> x2, Pallas kernels: none -> 6.2 us  [the longest x1 3.18 us: hidden_share(): pl.pallas_call(body, grid=(len(blocks),), in_specs=[pl.BlockSpec(d_slots....]
    squeeze x0 -> x2, local copies, waits for them, and re-layouts: none -> 3.53 us  [the longest x1 2.89 us: local(): share[k]]
    pallas_call x1 -> x2, Pallas kernels: 8.67 us -> 11.8 us  [hidden_grad(): pl.pallas_call(body, grid_spec=pltpu.PrefetchScalarGridSpec(num_scalar_pr...]
    ppermute x22 -> x37, waiting for transfers between devices: 39.6 us -> 39.2 us  [swap(): return lax.ppermute(x, 'dp', [(i, i ^ bit) for i in range(n_dp)])]
  transfers between devices with their start and end apart: 23 -> 47, of which waited for: 14 -> 17; matrix products, arithmetic and copies ran while one was open for 3% -> 5% of each run, Pallas kernels for 5% -> 13%
where the time goes in v2:
time: 188 us; the launch traced here: 187 us
  waiting for transfers between devices  88.9 us (47%)
  starting transfers between devices  42.6 us (23%)
  Pallas kernels  41.1 us (22%)
  local copies, waits for them, and re-layouts  7.59 us (4%)
  other arithmetic  5.94 us (3%)
    ppermute x10, waiting for transfers between devices, shift(): lax.ppermute(x, 'tensor', [(i, (i - by) % n_tensor) for i in range(n_tens...  49.7 us
    ppermute x37, waiting for transfers between devices, swap(): return lax.ppermute(x, 'dp', [(i, i ^ bit) for i in range(n_dp)])  39.2 us
    ppermute x37, starting transfers between devices, swap(): return lax.ppermute(x, 'dp', [(i, i ^ bit) for i in range(n_dp)])  26.7 us
    ppermute x10, starting transfers between devices, shift(): lax.ppermute(x, 'tensor', [(i, (i - by) % n_tensor) for i in range(n_tens...  15.9 us
    pallas_call x2, Pallas kernels, weight_grad(): pl.pallas_call(body, grid_spec=pltpu.PrefetchScalarGridSpec(num_scalar_pr...  12.1 us
    pallas_call x2, Pallas kernels, hidden_grad(): pl.pallas_call(body, grid_spec=pltpu.PrefetchScalarGridSpec(num_scalar_pr...  11.8 us
    pallas_call x1, Pallas kernels, project(): pl.pallas_call(body, grid_spec=pltpu.PrefetchScalarGridSpec(num_scalar_pr...  11 us
  transfers between devices with their start and end apart: 47, of which 17 were waited for; matrix products, arithmetic and copies ran while one was open for 5% of the time, Pallas kernels for 13%

profile of v2, /device:TPU:0, one launch (start us, length us, event | category | flops | bytes accessed | tf_op | source)
XLA Modules:
  0.0 187.2 jit_solution(12694172534930356402)
XLA Ops:
  1.7 3.0 %collective-permute-start.2 = (bf16[128,1024]{1,0:T(8,128)(2,1)S(1)}, bf16[128,1024]{1,0:T(8,128)(2,1)S(1)}, u32[]{:S(2)}, u32[]{:S(2)}) collective-permute-start(bf16[128,1024]{1,0:T(8,128)(2,1)S(1)} %get-tuple-element.21.rest_0_.rest_4_), channel_id=1, source_target_pairs={{0,8},{4,12},{8,0},{12,4},{16,24},{20,28},{24,16},{28,20},{1,9},{5... | collective-permute-start | bytes 786440 | tf_op jit(solution)/shard_map/ppermute | solution.py:17
  4.8 1.5 collective-permute-start.7
  6.9 5.0 %collective-permute-done.2.rest_4_ = bf16[128,1024]{1,0:T(8,128)(2,1)S(1)} collective-permute-done((bf16[128,1024]{1,0:T(8,128)(2,1)S(1)}, bf16[128,1024]{1,0:T(8,128)(2,1)S(1)}, u32[]{:S(2)}, u32[]{:S(2)}) %collective-permute-start.2) | collective-permute-done | bytes 262176 | tf_op jit(solution)/shard_map/ppermute | solution.py:17
  11.9 2.0 %collective-permute-done.7.rest_9_.rest_15_ = bf16[128,1024]{1,0:T(8,128)(2,1)S(1)} collective-permute-done((bf16[128,1024]{1,0:T(8,128)(2,1)S(1)}, bf16[128,1024]{1,0:T(8,128)(2,1)S(1)}, u32[]{:S(2)}, u32[]{:S(2)}) %collective-permute-start.7) | collective-permute-done | bytes 262176 | tf_op jit(solution)/shard_map/ppermute | solution.py:17
  16.7 1.7 collective-permute-start.11
  20.1 3.6 %collective-permute-done.10.rest_12_.rest_0_ = bf16[128,1024]{1,0:T(8,128)(2,1)S(1)} collective-permute-done((bf16[128,1024]{1,0:T(8,128)(2,1)S(1)}, bf16[128,1024]{1,0:T(8,128)(2,1)S(1)}, u32[]{:S(2)}, u32[]{:S(2)}) %collective-permute-start.10) | collective-permute-done | bytes 262176 | tf_op jit(solution)/shard_map/ppermute | solution.py:17
  26.4 11.0 %project.1 = (bf16[512,256]{1,0:T(8,128)(2,1)}, bf16[4,128,256]{2,1,0:T(8,128)(2,1)}, bf16[256,512]{1,0:T(8,128)(2,1)}) custom-call(s32[2]{0:T(128)} %pad_add_fusion.where_ref, bf16[512,8192]{1,0:T(8,128)(2,1)} %h_ref.5, f32[1,128]{1,0:T(1,128)} %s_ref.1, bf16[512,256]{1,0:T(8,128)(2,1)} %c_ref.1, bf16[128,1024]{1,0:T(8,128)(2,1)} %copy-done.2, ...), custom_call_target="tpu_custom_call" | custom-call | tf_op jit(solution)/shard_map/project/pallas_call | solution.py:78
  37.4 5.9 %weight_grad_odd.1 = bf16[4,256,1024]{2,1,0:T(8,128)(2,1)} custom-call(s32[2]{0:T(128)} %pad_add_fusion.where_ref, bf16[256,512]{1,0:T(8,128)(2,1)} %get-tuple-element.8.d_ref, bf16[512,8192]{1,0:T(8,128)(2,1)} %h_ref.5), custom_call_target="tpu_custom_call" | custom-call | tf_op jit(solution)/shard_map/weight_grad_odd/pallas_call | solution.py:112
  43.4 3.6 %collective-permute-start.20 = (bf16[256,1024]{1,0:T(8,128)(2,1)S(1)}, bf16[256,1024]{1,0:T(8,128)(2,1)S(1)}, u32[]{:S(2)}, u32[]{:S(2)}) collective-permute-start(bf16[256,1024]{1,0:T(8,128)(2,1)S(1)} %copy-done), channel_id=1, source_target_pairs={{0,3},{1,0},{2,1},{3,2},{4,7},{5,4},{6,5},{7,6},{8,11},{9,8},{10,9... | collective-permute-start | bytes 1572872 | tf_op jit(solution)/shard_map/ppermute | solution.py:129
  47.0 6.3 %weight_grad_even.1 = f32[4,256,1024]{2,1,0:T(8,128)} custom-call(s32[2]{0:T(128)} %pad_add_fusion.where_ref, bf16[256,512]{1,0:T(8,128)(2,1)} %get-tuple-element.8.d_ref, bf16[512,8192]{1,0:T(8,128)(2,1)} %h_ref.5), custom_call_target="tpu_custom_call" | custom-call | tf_op jit(solution)/shard_map/weight_grad_even/pallas_call | solution.py:112
  53.3 2.9 %convert_add_fusion = f32[4,256,1024]{2,1,0:T(8,128)S(1)} fusion(f32[4,256,1024]{2,1,0:T(8,128)} %weight_grad_even.1, bf16[4,256,1024]{2,1,0:T(8,128)(2,1)S(1)} %collective-permute-done.39), kind=kLoop, calls=%fused_computation | loop fusion | flops 2097152 | bytes 10485760 | tf_op jit(solution)/shard_map/add | solution.py:263
  58.1 1.6 collective-permute-start.42
  59.7 4.1 %collective-permute-start.22 = (bf16[128,1024]{1,0:T(8,128)(2,1)S(1)}, bf16[128,1024]{1,0:T(8,128)(2,1)S(1)}, u32[]{:S(2)}, u32[]{:S(2)}) collective-permute-start(bf16[128,1024]{1,0:T(8,128)(2,1)S(1)} %slice.107), channel_id=1, source_target_pairs={{0,3},{1,0},{2,1},{3,2},{4,7},{5,4},{6,5},{7,6},{8,11},{9,8},{10,9... | collective-permute-start | bytes 786440 | tf_op jit(solution)/shard_map/ppermute | solution.py:129
  63.8 7.9 %collective-permute-done.23.rest_8_ = bf16[256,1024]{1,0:T(8,128)(2,1)} collective-permute-done((bf16[256,1024]{1,0:T(8,128)(2,1)S(1)}, bf16[256,1024]{1,0:T(8,128)(2,1)}, u32[]{:S(2)}, u32[]{:S(2)}) %collective-permute-start.23) | collective-permute-done | bytes 524320 | tf_op jit(solution)/shard_map/ppermute | solution.py:129
  72.6 1.6 collective-permute-start.24
  74.9 2.3 %collective-permute-start.17 = (bf16[128,256]{1,0:T(8,128)(2,1)S(1)}, bf16[128,256]{1,0:T(8,128)(2,1)S(1)}, u32[]{:S(2)}, u32[]{:S(2)}) collective-permute-start(bf16[128,256]{1,0:T(8,128)(2,1)S(1)} %get-tuple-element.24), channel_id=1, source_target_pairs={{0,3},{1,0},{2,1},{3,2},{4,7},{5,4},{6,5},{7,6},{8,11},{9,8},{10,9... | collective-permute-start | bytes 196616 | tf_op jit(solution)/shard_map/ppermute | solution.py:129
  77.6 1.6 collective-permute-start.41
  79.1 4.4 %collective-permute-done.24 = bf16[128,1024]{1,0:T(8,128)(2,1)S(1)} collective-permute-done((bf16[128,1024]{1,0:T(8,128)(2,1)S(1)}, bf16[128,1024]{1,0:T(8,128)(2,1)S(1)}, u32[]{:S(2)}, u32[]{:S(2)}) %collective-permute-start.24) | collective-permute-done | bytes 262176 | tf_op jit(solution)/shard_map/ppermute | solution.py:129
  86.9 5.5 %collective-permute-done.19.rest_3_ = bf16[128,256]{1,0:T(8,128)(2,1)S(1)} collective-permute-done((bf16[128,256]{1,0:T(8,128)(2,1)S(1)}, bf16[128,256]{1,0:T(8,128)(2,1)S(1)}, u32[]{:S(2)}, u32[]{:S(2)}) %collective-permute-start.19) | collective-permute-done | bytes 65568 | tf_op jit(solution)/shard_map/ppermute | solution.py:129
  93.9 1.6 collective-permute-start.30
  96.7 1.7 collective-permute-done.21.rest_6_
  98.5 16.3 %collective-permute-done.43 = bf16[128,1024]{1,0:T(8,128)(2,1)S(1)} collective-permute-done((bf16[128,1024]{1,0:T(8,128)(2,1)S(1)}, bf16[128,1024]{1,0:T(8,128)(2,1)S(1)}, u32[]{:S(2)}, u32[]{:S(2)}) %collective-permute-start.43) | collective-permute-done | bytes 262176 | tf_op jit(solution)/shard_map/ppermute | solution.py:17
  116.3 1.6 collective-permute-start.31
  119.0 3.2 %hidden_share.1 = bf16[4,128,2048]{2,1,0:T(8,128)(2,1)} custom-call(bf16[4,128,256]{2,1,0:T(8,128)(2,1)} %get-tuple-element.7.d_ref, bf16[128,1024]{1,0:T(8,128)(2,1)} %copy-done.13, bf16[128,1024]{1,0:T(8,128)(2,1)} %copy-done.14, bf16[128,1024]{1,0:T(8,128)(2,1)} %copy-done.15, bf16[128,1024]{1,0:T(8,128)(2,1)} %collective-permute-done.13.rest_15_.rest_3_), custom_call_target="tpu_custom_call" | custom-call | tf_op jit(solution)/shard_map/hidden_share/pallas_call | solution.py:166
  122.3 6.1 %collective-permute-done.25.rest_7_ = bf16[256,1024]{1,0:T(8,128)(2,1)} collective-permute-done((bf16[256,1024]{1,0:T(8,128)(2,1)S(1)}, bf16[256,1024]{1,0:T(8,128)(2,1)}, u32[]{:S(2)}, u32[]{:S(2)}) %collective-permute-start.25) | collective-permute-done | bytes 524320 | tf_op jit(solution)/shard_map/ppermute | solution.py:17
  130.5 2.9 %slice_bitcast_fusion.6 = (bf16[128,2048]{1,0:T(8,128)(2,1)}, bf16[128,2048]{1,0:T(8,128)(2,1)}, bf16[128,2048]{1,0:T(8,128)(2,1)}, bf16[128,2048]{1,0:T(8,128)(2,1)}) fusion(bf16[4,128,2048]{2,1,0:T(8,128)(2,1)} %hidden_share.1), kind=kLoop, calls=%fused_computation.25 | loop fusion | bytes 4194304 | tf_op jit(solution)/shard_map/squeeze | solution.py:295
  136.2 1.9 %collective-permute-start.16 = (bf16[128,2048]{1,0:T(8,128)(2,1)}, bf16[128,2048]{1,0:T(8,128)(2,1)}, u32[]{:S(2)}, u32[]{:S(2)}) collective-permute-start(bf16[128,2048]{1,0:T(8,128)(2,1)} %get-tuple-element.16), channel_id=1, source_target_pairs={{0,1},{1,2},{2,3},{3,0},{4,5},{5,6},{6,7},{7,4},{8,9},{9,10},{10,1... | collective-permute-start | bytes 1572872 | tf_op jit(solution)/shard_map/ppermute | solution.py:129
  138.1 1.6 collective-permute-start.46
  139.7 4.6 %hidden_grad.2.rest_24_ = bf16[128,8192]{1,0:T(8,128)(2,1)} custom-call(s32[2]{0:T(128)} %pad_add_fusion.where_ref, bf16[128,256]{1,0:T(8,128)(2,1)} %get-tuple-element.25.rest_0_, bf16[128,256]{1,0:T(8,128)(2,1)} %copy-done.27, bf16[128,256]{1,0:T(8,128)(2,1)} %copy-done.28, bf16[128,256]{1,0:T(8,128)(2,1)} %copy-done.29, bf16[128,1024]{1,0:T(8,128)(2,1)} %copy-done.2, ...), custom_call_target="tpu_custom_call" | custom-call | tf_op jit(solution)/shard_map/hidden_grad/pallas_call | solution.py:218
  144.4 7.1 %hidden_grad.3.rest_4_ = bf16[128,8192]{1,0:T(8,128)(2,1)} custom-call(s32[2]{0:T(128)} %pad_add_fusion.where_ref, bf16[128,256]{1,0:T(8,128)(2,1)} %get-tuple-element.25.rest_0_, bf16[128,256]{1,0:T(8,128)(2,1)} %copy-done.27, bf16[128,256]{1,0:T(8,128)(2,1)} %copy-done.28, bf16[128,256]{1,0:T(8,128)(2,1)} %copy-done.29, ...), custom_call_target="tpu_custom_call", output_to_operand_aliasing={{}: (25, {})} | custom-call | tf_op jit(solution)/shard_map/hidden_grad/pallas_call | solution.py:218
  151.5 30.6 %collective-permute-done.15.rest_2_ = bf16[128,2048]{1,0:T(8,128)(2,1)S(1)} collective-permute-done((bf16[128,2048]{1,0:T(8,128)(2,1)}, bf16[128,2048]{1,0:T(8,128)(2,1)S(1)}, u32[]{:S(2)}, u32[]{:S(2)}) %collective-permute-start.15) | collective-permute-done | bytes 524320 | tf_op jit(solution)/shard_map/ppermute | solution.py:129
  182.9 3.0 %add_shares.1 = bf16[128,8192]{1,0:T(8,128)(2,1)} custom-call(s32[2]{0:T(128)} %pad_add_fusion.where_ref, bf16[128,2048]{1,0:T(8,128)(2,1)} %get-tuple-element.19.rest_0_, bf16[128,2048]{1,0:T(8,128)(2,1)} %copy-done.23, bf16[128,2048]{1,0:T(8,128)(2,1)} %copy-done.24, ...), custom_call_target="tpu_custom_call", output_to_operand_aliasing={{}: (5, {})} | custom-call | tf_op jit(solution)/shard_map/add_shares/pallas_call | solution.py:247
  (154 shorter events, 28.4 us)
Async XLA Ops:
  1.7 10.2 %collective-permute-start.2 = (bf16[128,1024]{1,0:T(8,128)(2,1)S(1)}, bf16[128,1024]{1,0:T(8,128)(2,1)S(1)}, u32[]{:S(2)}, u32[]{:S(2)}) collective-permute-start(bf16[128,1024]{1,0:T(8,128)(2,1)S(1)} %get-tuple-element.21.rest_0_.rest_4_), channel_id=1, source_target_pairs={{0,8},{4,12},{8,0},{12,4},{16,24},{20,28},{24,16},{28,20},{1,9},{5... | collective-permute-start | bytes 786440 | tf_op jit(solution)/shard_map/ppermute | solution.py:17
  4.8 9.2 %collective-permute-start.7 = (bf16[128,1024]{1,0:T(8,128)(2,1)S(1)}, bf16[128,1024]{1,0:T(8,128)(2,1)S(1)}, u32[]{:S(2)}, u32[]{:S(2)}) collective-permute-start(bf16[128,1024]{1,0:T(8,128)(2,1)S(1)} %get-tuple-element.20.rest_1_.rest_5_), channel_id=1, source_target_pairs={{0,16},{4,20},{8,24},{12,28},{16,0},{20,4},{24,8},{28,12},{1,17},{... | collective-permute-start | bytes 786440 | tf_op jit(solution)/shard_map/ppermute | solution.py:17
  6.3 10.4 %collective-permute-start.3 = (bf16[128,1024]{1,0:T(8,128)(2,1)S(1)}, bf16[128,1024]{1,0:T(8,128)(2,1)S(1)}, u32[]{:S(2)}, u32[]{:S(2)}) collective-permute-start(bf16[128,1024]{1,0:T(8,128)(2,1)S(1)} %get-tuple-element.20.rest_1_.rest_5_), channel_id=1, source_target_pairs={{0,8},{4,12},{8,0},{12,4},{16,24},{20,28},{24,16},{28,20},{1,9},{5... | collective-permute-start | bytes 786440 | tf_op jit(solution)/shard_map/ppermute | solution.py:17
  6.8 12.7 %collective-permute-start.6 = (bf16[128,1024]{1,0:T(8,128)(2,1)S(1)}, bf16[128,1024]{1,0:T(8,128)(2,1)S(1)}, u32[]{:S(2)}, u32[]{:S(2)}) collective-permute-start(bf16[128,1024]{1,0:T(8,128)(2,1)S(1)} %get-tuple-element.21.rest_0_.rest_4_), channel_id=1, source_target_pairs={{0,16},{4,20},{8,24},{12,28},{16,0},{20,4},{24,8},{28,12},{1,17},{... | collective-permute-start | bytes 786440 | tf_op jit(solution)/shard_map/ppermute | solution.py:17
  6.9 12.7 %collective-permute-start = (bf16[128,1024]{1,0:T(8,128)(2,1)S(1)}, bf16[128,1024]{1,0:T(8,128)(2,1)S(1)}, u32[]{:S(2)}, u32[]{:S(2)}) collective-permute-start(bf16[128,1024]{1,0:T(8,128)(2,1)S(1)} %get-tuple-element.21.rest_0_.rest_4_), channel_id=1, source_target_pairs={{0,4},{4,0},{8,12},{12,8},{16,20},{20,16},{24,28},{28,24},{1,5},{5... | collective-permute-start | bytes 786440 | tf_op jit(solution)/shard_map/ppermute | solution.py:17
  13.9 9.8 %collective-permute-start.10 = (bf16[128,1024]{1,0:T(8,128)(2,1)S(1)}, bf16[128,1024]{1,0:T(8,128)(2,1)S(1)}, u32[]{:S(2)}, u32[]{:S(2)}) collective-permute-start(bf16[128,1024]{1,0:T(8,128)(2,1)S(1)} %collective-permute-done.2.rest_4_), channel_id=1, source_target_pairs={{0,16},{4,20},{8,24},{12,28},{16,0},{20,4},{24,8},{28,12},{1,17},{... | collective-permute-start | bytes 786440 | tf_op jit(solution)/shard_map/ppermute | solution.py:17
  43.3 10.0 %collective-permute-start.39 = (bf16[4,256,1024]{2,1,0:T(8,128)(2,1)}, bf16[4,256,1024]{2,1,0:T(8,128)(2,1)S(1)}, u32[]{:S(2)}, u32[]{:S(2)}) collective-permute-start(bf16[4,256,1024]{2,1,0:T(8,128)(2,1)} %weight_grad_odd.1), channel_id=1, source_target_pairs={{0,4},{4,0},{8,12},{12,8},{16,20},{20,16},{24,28},{28,24},{1,5},{5... | collective-permute-start | bytes 6291464 | tf_op jit(solution)/shard_map/ppermute | solution.py:17
  43.4 16.2 %collective-permute-start.20 = (bf16[256,1024]{1,0:T(8,128)(2,1)S(1)}, bf16[256,1024]{1,0:T(8,128)(2,1)S(1)}, u32[]{:S(2)}, u32[]{:S(2)}) collective-permute-start(bf16[256,1024]{1,0:T(8,128)(2,1)S(1)} %copy-done), channel_id=1, source_target_pairs={{0,3},{1,0},{2,1},{3,2},{4,7},{5,4},{6,5},{7,6},{8,11},{9,8},{10,9... | collective-permute-start | bytes 1572872 | tf_op jit(solution)/shard_map/ppermute | solution.py:129
  47.0 24.6 %collective-permute-start.23 = (bf16[256,1024]{1,0:T(8,128)(2,1)S(1)}, bf16[256,1024]{1,0:T(8,128)(2,1)}, u32[]{:S(2)}, u32[]{:S(2)}) collective-permute-start(bf16[256,1024]{1,0:T(8,128)(2,1)S(1)} %copy-done), channel_id=1, source_target_pairs={{0,1},{1,2},{2,3},{3,0},{4,5},{5,6},{6,7},{7,4},{8,9},{9,10},{10,1... | collective-permute-start | bytes 1572872 | tf_op jit(solution)/shard_map/ppermute | solution.py:129
  56.6 18.3 %collective-permute-start.40 = (bf16[2,128,1024]{2,1,0:T(8,128)(2,1)S(1)}, bf16[2,128,1024]{2,1,0:T(8,128)(2,1)S(1)}, u32[]{:S(2)}, u32[]{:S(2)}) collective-permute-start(bf16[2,128,1024]{2,1,0:T(8,128)(2,1)S(1)} %slice_bitcast_fusion.5), channel_id=1, source_target_pairs={{0,8},{4,12},{8,0},{12,4},{16,24},{20,28},{24,16},{28,20},{1,9},{5... | collective-permute-start | bytes 1572872 | tf_op jit(solution)/shard_map/ppermute | solution.py:17
  58.1 19.1 %collective-permute-start.42 = (bf16[2,128,1024]{2,1,0:T(8,128)(2,1)S(1)}, bf16[2,128,1024]{2,1,0:T(8,128)(2,1)S(1)}, u32[]{:S(2)}, u32[]{:S(2)}) collective-permute-start(bf16[2,128,1024]{2,1,0:T(8,128)(2,1)S(1)} %slice_bitcast_fusion.3), channel_id=1, source_target_pairs={{0,16},{4,20},{8,24},{12,28},{16,0},{20,4},{24,8},{28,12},{1,17},{... | collective-permute-start | bytes 1572872 | tf_op jit(solution)/shard_map/ppermute | solution.py:17
  59.7 17.9 %collective-permute-start.22 = (bf16[128,1024]{1,0:T(8,128)(2,1)S(1)}, bf16[128,1024]{1,0:T(8,128)(2,1)S(1)}, u32[]{:S(2)}, u32[]{:S(2)}) collective-permute-start(bf16[128,1024]{1,0:T(8,128)(2,1)S(1)} %slice.107), channel_id=1, source_target_pairs={{0,3},{1,0},{2,1},{3,2},{4,7},{5,4},{6,5},{7,6},{8,11},{9,8},{10,9... | collective-permute-start | bytes 786440 | tf_op jit(solution)/shard_map/ppermute | solution.py:129
  72.6 10.9 %collective-permute-start.24 = (bf16[128,1024]{1,0:T(8,128)(2,1)S(1)}, bf16[128,1024]{1,0:T(8,128)(2,1)S(1)}, u32[]{:S(2)}, u32[]{:S(2)}) collective-permute-start(bf16[128,1024]{1,0:T(8,128)(2,1)S(1)} %slice.108), channel_id=1, source_target_pairs={{0,1},{1,2},{2,3},{3,0},{4,5},{5,6},{6,7},{7,4},{8,9},{9,10},{10,1... | collective-permute-start | bytes 786440 | tf_op jit(solution)/shard_map/ppermute | solution.py:129
  74.2 19.6 %collective-permute-start.36 = (bf16[256,1024]{1,0:T(8,128)(2,1)S(1)}, bf16[256,1024]{1,0:T(8,128)(2,1)S(1)}, u32[]{:S(2)}, u32[]{:S(2)}) collective-permute-start(bf16[256,1024]{1,0:T(8,128)(2,1)S(1)} %collective-permute-done.20.rest_6_), channel_id=1, source_target_pairs={{0,4},{4,0},{8,12},{12,8},{16,20},{20,16},{24,28},{28,24},{1,5},{5... | collective-permute-start | bytes 1572872 | tf_op jit(solution)/shard_map/ppermute | solution.py:17
  77.6 17.9 %collective-permute-start.41 = (bf16[128,1024]{1,0:T(8,128)(2,1)S(1)}, bf16[128,1024]{1,0:T(8,128)(2,1)S(1)}, u32[]{:S(2)}, u32[]{:S(2)}) collective-permute-start(bf16[128,1024]{1,0:T(8,128)(2,1)S(1)} %fusion.10), channel_id=1, source_target_pairs={{0,16},{4,20},{8,24},{12,28},{16,0},{20,4},{24,8},{28,12},{1,17},{... | collective-permute-start | bytes 786440 | tf_op jit(solution)/shard_map/ppermute | solution.py:17
  83.6 12.5 %collective-permute-start.38 = (bf16[256,1024]{1,0:T(8,128)(2,1)}, bf16[256,1024]{1,0:T(8,128)(2,1)S(1)}, u32[]{:S(2)}, u32[]{:S(2)}) collective-permute-start(bf16[256,1024]{1,0:T(8,128)(2,1)} %collective-permute-done.23.rest_8_), channel_id=1, source_target_pairs={{0,4},{4,0},{8,12},{12,8},{16,20},{20,16},{24,28},{28,24},{1,5},{5... | collective-permute-start | bytes 1572872 | tf_op jit(solution)/shard_map/ppermute | solution.py:17
  83.6 14.9 %collective-permute-start.21 = (bf16[256,1024]{1,0:T(8,128)(2,1)S(1)}, bf16[256,1024]{1,0:T(8,128)(2,1)S(1)}, u32[]{:S(2)}, u32[]{:S(2)}) collective-permute-start(bf16[256,1024]{1,0:T(8,128)(2,1)S(1)} %collective-permute-done.20.rest_6_), channel_id=1, source_target_pairs={{0,8},{4,12},{8,0},{12,4},{16,24},{20,28},{24,16},{28,20},{1,9},{5... | collective-permute-start | bytes 1572872 | tf_op jit(solution)/shard_map/ppermute | solution.py:17
  92.4 23.9 %collective-permute-start.26 = (bf16[256,1024]{1,0:T(8,128)(2,1)}, bf16[256,1024]{1,0:T(8,128)(2,1)S(1)}, u32[]{:S(2)}, u32[]{:S(2)}) collective-permute-start(bf16[256,1024]{1,0:T(8,128)(2,1)} %collective-permute-done.23.rest_8_), channel_id=1, source_target_pairs={{0,8},{4,12},{8,0},{12,4},{16,24},{20,28},{24,16},{28,20},{1,9},{5... | collective-permute-start | bytes 1572872 | tf_op jit(solution)/shard_map/ppermute | solution.py:17
  93.9 24.0 %collective-permute-start.30 = (bf16[256,1024]{1,0:T(8,128)(2,1)S(1)}, bf16[256,1024]{1,0:T(8,128)(2,1)}, u32[]{:S(2)}, u32[]{:S(2)}) collective-permute-start(bf16[256,1024]{1,0:T(8,128)(2,1)S(1)} %collective-permute-done.20.rest_6_), channel_id=1, source_target_pairs={{0,16},{4,20},{8,24},{12,28},{16,0},{20,4},{24,8},{28,12},{1,17},{... | collective-permute-start | bytes 1572872 | tf_op jit(solution)/shard_map/ppermute | solution.py:17
  95.5 19.3 %collective-permute-start.43 = (bf16[128,1024]{1,0:T(8,128)(2,1)S(1)}, bf16[128,1024]{1,0:T(8,128)(2,1)S(1)}, u32[]{:S(2)}, u32[]{:S(2)}) collective-permute-start(bf16[128,1024]{1,0:T(8,128)(2,1)S(1)} %fusion.11), channel_id=1, source_target_pairs={{0,8},{4,12},{8,0},{12,4},{16,24},{20,28},{24,16},{28,20},{1,9},{5... | collective-permute-start | bytes 786440 | tf_op jit(solution)/shard_map/ppermute | solution.py:17
  96.1 22.3 %collective-permute-start.32 = (bf16[256,1024]{1,0:T(8,128)(2,1)}, bf16[256,1024]{1,0:T(8,128)(2,1)}, u32[]{:S(2)}, u32[]{:S(2)}) collective-permute-start(bf16[256,1024]{1,0:T(8,128)(2,1)} %collective-permute-done.23.rest_8_), channel_id=1, source_target_pairs={{0,16},{4,20},{8,24},{12,28},{16,0},{20,4},{24,8},{28,12},{1,17},{... | collective-permute-start | bytes 1572872 | tf_op jit(solution)/shard_map/ppermute | solution.py:17
  98.5 23.7 %collective-permute-start.37 = (bf16[256,1024]{1,0:T(8,128)(2,1)S(1)}, bf16[256,1024]{1,0:T(8,128)(2,1)}, u32[]{:S(2)}, u32[]{:S(2)}) collective-permute-start(bf16[256,1024]{1,0:T(8,128)(2,1)S(1)} %constant_dynamic-update-slice_fusion.rest_7_), channel_id=1, source_target_pairs={{0,4},{4,0},{8,12},{12,8},{16,20},{20,16},{24,28},{28,24},{1,5},{5... | collective-permute-start | bytes 1572872 | tf_op jit(solution)/shard_map/ppermute | solution.py:17
  114.8 13.6 %collective-permute-start.25 = (bf16[256,1024]{1,0:T(8,128)(2,1)S(1)}, bf16[256,1024]{1,0:T(8,128)(2,1)}, u32[]{:S(2)}, u32[]{:S(2)}) collective-permute-start(bf16[256,1024]{1,0:T(8,128)(2,1)S(1)} %constant_dynamic-update-slice_fusion.rest_7_), channel_id=1, source_target_pairs={{0,8},{4,12},{8,0},{12,4},{16,24},{20,28},{24,16},{28,20},{1,9},{5... | collective-permute-start | bytes 1572872 | tf_op jit(solution)/shard_map/ppermute | solution.py:17
  116.3 13.4 %collective-permute-start.31 = (bf16[256,1024]{1,0:T(8,128)(2,1)S(1)}, bf16[256,1024]{1,0:T(8,128)(2,1)}, u32[]{:S(2)}, u32[]{:S(2)}) collective-permute-start(bf16[256,1024]{1,0:T(8,128)(2,1)S(1)} %constant_dynamic-update-slice_fusion.rest_7_), channel_id=1, source_target_pairs={{0,16},{4,20},{8,24},{12,28},{16,0},{20,4},{24,8},{28,12},{1,17},{... | collective-permute-start | bytes 1572872 | tf_op jit(solution)/shard_map/ppermute | solution.py:17
  117.9 11.8 %collective-permute-start.27 = (bf16[256,1024]{1,0:T(8,128)(2,1)S(1)}, bf16[256,1024]{1,0:T(8,128)(2,1)}, u32[]{:S(2)}, u32[]{:S(2)}) collective-permute-start(bf16[256,1024]{1,0:T(8,128)(2,1)S(1)} %collective-permute-done.21.rest_6_), channel_id=1, source_target_pairs={{0,4},{4,0},{8,12},{12,8},{16,20},{20,16},{24,28},{28,24},{1,5},{5... | collective-permute-start | bytes 1572872 | tf_op jit(solution)/shard_map/ppermute | solution.py:17
  118.4 10.0 %collective-permute-start.44 = (f32[3,256]{1,0:T(4,128)S(1)}, f32[3,256]{1,0:T(4,128)S(1)}, u32[]{:S(2)}, u32[]{:S(2)}) collective-permute-start(f32[3,256]{1,0:T(4,128)S(1)} %pad_maximum_fusion.1), channel_id=1, source_target_pairs={{0,4},{4,0},{8,12},{12,8},{16,20},{20,16},{24,28},{28,24},{1,5},{5... | collective-permute-start | bytes 9224 | tf_op jit(solution)/shard_map/ppermute | solution.py:17
  122.2 11.3 %collective-permute-start.29 = (bf16[256,1024]{1,0:T(8,128)(2,1)S(1)}, bf16[256,1024]{1,0:T(8,128)(2,1)S(1)}, u32[]{:S(2)}, u32[]{:S(2)}) collective-permute-start(bf16[256,1024]{1,0:T(8,128)(2,1)S(1)} %copy-done.20), channel_id=1, source_target_pairs={{0,4},{4,0},{8,12},{12,8},{16,20},{20,16},{24,28},{28,24},{1,5},{5... | collective-permute-start | bytes 1572872 | tf_op jit(solution)/shard_map/ppermute | solution.py:17
  134.3 17.2 %collective-permute-start.14 = (bf16[128,2048]{1,0:T(8,128)(2,1)}, bf16[128,2048]{1,0:T(8,128)(2,1)S(1)}, u32[]{:S(2)}, u32[]{:S(2)}) collective-permute-start(bf16[128,2048]{1,0:T(8,128)(2,1)} %get-tuple-element.18), channel_id=1, source_target_pairs={{0,3},{1,0},{2,1},{3,2},{4,7},{5,4},{6,5},{7,6},{8,11},{9,8},{10,9... | collective-permute-start | bytes 1572872 | tf_op jit(solution)/shard_map/ppermute | solution.py:129
  135.1 9.3 %collective-permute-start.34 = (bf16[256,1024]{1,0:T(8,128)(2,1)}, bf16[256,1024]{1,0:T(8,128)(2,1)}, u32[]{:S(2)}, u32[]{:S(2)}) collective-permute-start(bf16[256,1024]{1,0:T(8,128)(2,1)} %collective-permute-done.31.rest_17_), channel_id=1, source_target_pairs={{0,4},{4,0},{8,12},{12,8},{16,20},{20,16},{24,28},{28,24},{1,5},{5... | collective-permute-start | bytes 1572872 | tf_op jit(solution)/shard_map/ppermute | solution.py:17
  135.1 47.0 %collective-permute-start.15 = (bf16[128,2048]{1,0:T(8,128)(2,1)}, bf16[128,2048]{1,0:T(8,128)(2,1)S(1)}, u32[]{:S(2)}, u32[]{:S(2)}) collective-permute-start(bf16[128,2048]{1,0:T(8,128)(2,1)} %get-tuple-element.17), channel_id=1, source_target_pairs={{0,2},{1,3},{2,0},{3,1},{4,6},{5,7},{6,4},{7,5},{8,10},{9,11},{10,... | collective-permute-start | bytes 1572872 | tf_op jit(solution)/shard_map/ppermute | solution.py:129
  136.2 46.0 %collective-permute-start.16 = (bf16[128,2048]{1,0:T(8,128)(2,1)}, bf16[128,2048]{1,0:T(8,128)(2,1)}, u32[]{:S(2)}, u32[]{:S(2)}) collective-permute-start(bf16[128,2048]{1,0:T(8,128)(2,1)} %get-tuple-element.16), channel_id=1, source_target_pairs={{0,1},{1,2},{2,3},{3,0},{4,5},{5,6},{6,7},{7,4},{8,9},{9,10},{10,1... | collective-permute-start | bytes 1572872 | tf_op jit(solution)/shard_map/ppermute | solution.py:129
  138.1 47.8 %collective-permute-start.46 = (f32[3,256]{1,0:T(4,128)S(1)}, f32[3,256]{1,0:T(4,128)S(1)}, u32[]{:S(2)}, u32[]{:S(2)}) collective-permute-start(f32[3,256]{1,0:T(4,128)S(1)} %fusion.15), channel_id=1, source_target_pairs={{0,16},{4,20},{8,24},{12,28},{16,0},{20,4},{24,8},{28,12},{1,17},{... | collective-permute-start | bytes 9224 | tf_op jit(solution)/shard_map/ppermute | solution.py:17
  (45 other events, 478.2 us)

commit v3 on v2

--- a/solution.py
+++ b/solution.py
@@ -17,7 +17,7 @@
     return lax.ppermute(x, "dp", [(i, i ^ bit) for i in range(n_dp)])
 
 
-def gather_blocks(w, n_dp):
+def gather_links(w, n_dp):
     bits = [1 << i for i in range(1, n_dp.bit_length() - 1)]
     half = w.shape[0] // 2
     parts = []
@@ -25,9 +25,12 @@
         have = {0: rows}
         for bit in order:
             have.update({r ^ bit: swap(x, bit, n_dp) for r, x in list(have.items())})
-        have.update({r ^ 1: swap(x, 1, n_dp) for r, x in list(have.items())})
         parts.append(have)
     return parts
+
+
+def add_core(have, n_dp):
+    return {**have, **{r ^ 1: swap(x, 1, n_dp) for r, x in have.items()}}
 
 
 def project(hidden, parts, qk_scale, cotangent, where, n_tensor):
@@ -129,24 +132,6 @@
     return lax.ppermute(x, "tensor", [(i, (i - by) % n_tensor) for i in range(n_tensor)])
 
 
-def gather_others(w, n_tensor, n_dp):
-    half = w.shape[0] // 2
-    slots = {1: shift(w, 1, n_tensor), n_tensor - 1: shift(w, -1, n_tensor)}
-    for k in range(2, n_tensor - 1):
-        low = shift(slots[1][:half], k - 1, n_tensor)
-        high = shift(slots[n_tensor - 1][half:], k + 1, n_tensor)
-        slots[k] = jnp.concatenate([low, high], 0)
-    rest = {}
-    bit = 2
-    while bit < n_dp:
-        for k, x in slots.items():
-            rest[bit, k] = swap(x, bit, n_dp)
-        bit *= 2
-    rest.update({(0, k): x for k, x in slots.items()})
-    rest.update({(r ^ 1, k): swap(x, 1, n_dp) for (r, k), x in list(rest.items())})
-    return rest
-
-
 def hidden_share(d_slots, parts, blocks):
     n_tensor, chunk, rows = d_slots.shape
     half, width = parts[0][0].shape
@@ -174,16 +159,15 @@
     )(d_slots, *[parts[s][r] for r in blocks for s in range(2)])
 
 
-def hidden_grad(d_own, d_rest, parts, others, where, blocks, into):
-    n_tensor = len(d_rest) + 1
-    chunk, rows = d_own.shape
+def hidden_grad(d_own, d_pair, d_mid, parts, pair, mid, where, blocks, into):
+    chunk = d_own.shape[0]
     half, width = parts[0][0].shape
     n_blocks = len(parts[0])
-    per = n_tensor + 1
+    per = 4
 
     def body(where_ref, *rest):
-        d_refs = rest[:n_tensor]
-        w_refs = rest[n_tensor : n_tensor + per * len(blocks)]
+        d_refs = rest[:3]
+        w_refs = rest[3 : 3 + per * len(blocks)]
         out_ref = rest[-1]
         step = pl.program_id(0)
         for i in range(len(blocks)):
@@ -193,7 +177,7 @@
                 mine = w_refs[per * i : per * (i + 1)]
                 w = jnp.concatenate([mine[0][...], mine[1][...]], 0)
                 total = jnp.dot(d_refs[0][...], w, preferred_element_type=F32)
-                for k in range(1, n_tensor):
+                for k in (1, 2):
                     total += jnp.dot(d_refs[k][...], mine[k + 1][...], preferred_element_type=F32)
                 out_ref[...] = total.astype(BF16)
 
@@ -205,11 +189,10 @@
             r = jnp.where(i == at, blocks[at], r)
         return (0, where_ref[0] ^ r)
 
-    operands = [d_own, *d_rest]
-    specs = [pl.BlockSpec((chunk, rows), fixed)] * n_tensor
+    operands = [d_own, d_pair, d_mid]
     for r in blocks:
-        operands += [parts[0][r], parts[1][r]] + [others[r, k] for k in range(1, n_tensor)]
-        specs += [pl.BlockSpec((half, width), fixed)] * 2 + [pl.BlockSpec((rows, width), fixed)] * (n_tensor - 1)
+        operands += [parts[0][r], parts[1][r], pair[r], mid[r]]
+    specs = [pl.BlockSpec(x.shape, fixed) for x in operands]
     aliases = {}
     if into is not None:
         operands.append(into)
@@ -259,44 +242,62 @@
     )(where, *shares, into)
 
 
-def scatter_sum(keep, sent, n_dp):
-    total = keep + swap(sent, 1, n_dp).astype(F32)
-    count = n_dp.bit_length() - 2
-    rows, width = keep.shape[1:]
-    total = total.reshape((2,) * count + (rows, width))
-    half = rows // 2
-    sides = []
-    for at, order in ((0, list(range(count))), (half, list(range(count))[::-1])):
-        part = lax.slice_in_dim(total, at, at + half, axis=count)
-        left = list(range(count))[::-1]
-        for b in order:
-            axis = left.index(b)
-            left.remove(b)
-            go = lax.index_in_dim(part, 1, axis, keepdims=False).astype(BF16)
-            stay = lax.index_in_dim(part, 0, axis, keepdims=False)
-            part = stay + swap(go, 2 << b, n_dp).astype(F32)
-        sides.append(part)
-    return jnp.concatenate(sides, 0)
+def halve(part, axis, bit, n_dp):
+    go = lax.index_in_dim(part, 1, axis, keepdims=False).astype(BF16)
+    stay = lax.index_in_dim(part, 0, axis, keepdims=False)
+    return stay + swap(go, bit, n_dp).astype(F32)
 
 
 def local(hidden, weight, qk_scale, cotangent, n_dp, n_tensor):
     width = weight.shape[1]
+    half = weight.shape[0] // 2
     where = jnp.stack([lax.axis_index("dp"), lax.axis_index("tensor")]).astype(jnp.int32)
-    parts = gather_blocks(weight, n_dp)
-    others = gather_others(weight, n_tensor, n_dp)
+    ahead = shift(weight, 1, n_tensor)
+    behind = shift(weight, -1, n_tensor)
+    parts = gather_links(weight, n_dp)
+    parts, ahead, behind = lax.optimization_barrier((parts, ahead, behind))
+    pair = {0: jnp.concatenate([ahead, behind], 0)}
+    low, high = shift(ahead[:half], 1, n_tensor), shift(behind[half:], -1, n_tensor)
+    bits = [1 << i for i in range(1, n_dp.bit_length() - 1)]
+    pair.update({bit: swap(pair[0], bit, n_dp) for bit in bits})
+    parts = [add_core(have, n_dp) for have in parts]
     keys_values, d_slots, d_t = project(hidden, parts, qk_scale, cotangent, where, n_tensor)
     near = [0, 1]
-    linked = sorted({r for r, k in others} - set(near))
+    linked = [r for bit in bits for r in (bit, bit ^ 1)]
     far = [r for r in range(n_dp) if r not in near and r not in linked]
+    share = hidden_share(d_slots, parts, far)
+    d_t, share, low, high = lax.optimization_barrier((d_t, share, low, high))
+    shares = [share[0]] + [shift(share[k], k, n_tensor) for k in range(1, n_tensor)]
+    mid = {0: jnp.concatenate([low, high], 0)}
+    mid.update({bit: swap(mid[0], bit, n_dp) for bit in bits})
     sent = weight_grad(d_t, hidden, where, n_dp, 1, BF16)
-    share = hidden_share(d_slots, parts, far)
+    d_rest = [shift(d_slots[k], k, n_tensor) for k in range(1, n_tensor)]
+    d_t, sent, pair, d_rest = lax.optimization_barrier((d_t, sent, pair, d_rest))
+    pair = add_core(pair, n_dp)
     keep = weight_grad(d_t, hidden, where, n_dp, 0, F32)
-    d_rest = [shift(d_slots[k], k, n_tensor) for k in range(1, n_tensor)]
-    shares = [share[0]] + [shift(share[k], k, n_tensor) for k in range(1, n_tensor)]
-    input_grad = hidden_grad(d_slots[0], d_rest, parts, others, where, near, None)
-    input_grad = hidden_grad(d_slots[0], d_rest, parts, others, where, linked, input_grad)
+    total = keep + swap(sent, 1, n_dp).astype(F32)
+    total, mid_links = lax.optimization_barrier((total, mid))
+    mid = add_core(mid_links, n_dp)
+    count = len(bits)
+    total = total.reshape((2,) * count + total.shape[1:])
+    sides = [total[..., :half, :], total[..., half:, :]]
+    orders = [list(range(count)), list(range(count))[::-1]]
+    left = [list(range(count))[::-1], list(range(count))[::-1]]
+    for step in range(count):
+        if step == count - 1:
+            sides, shares[1], shares[-1] = lax.optimization_barrier((sides, shares[1], shares[-1]))
+        for at in range(2):
+            b = orders[at][step]
+            axis = left[at].index(b)
+            left[at].remove(b)
+            sides[at] = halve(sides[at], axis, bits[b], n_dp)
+    grad = jnp.concatenate(sides, 0)
+    grad, shares[2] = lax.optimization_barrier((grad, shares[2]))
+    d_pair = jnp.concatenate([d_rest[0], d_rest[-1]], 1)
+    d_all = (d_slots[0], d_pair, d_rest[1], parts, pair, mid, where)
+    input_grad = hidden_grad(*d_all, near, None)
+    input_grad = hidden_grad(*d_all, linked, input_grad)
     input_grad = add_shares(shares, where, far, width, input_grad)
-    grad = scatter_sum(keep, sent, n_dp)
     w = weight.astype(F32)
     sums = jnp.stack([jnp.sum(grad * w, 1), jnp.sum(w * w, 1), jnp.sum(grad * grad, 1)])
     bit = 1

time: 188 us -> 165 us (0.88)
  waiting for transfers between devices: 88.9 us -> 72.8 us
  starting transfers between devices: 42.6 us -> 35.4 us
    ppermute x10, waiting for transfers between devices: 49.7 us -> 41.4 us  [shift(): lax.ppermute(x, 'tensor', [(i, (i - by) % n_tensor) for i in range(n_tens...]
    ppermute x37 -> x32, waiting for transfers between devices: 39.2 us -> 31.5 us  [swap(): return lax.ppermute(x, 'dp', [(i, i ^ bit) for i in range(n_dp)])]
    ppermute x37 -> x32, starting transfers between devices: 26.7 us -> 20.1 us  [swap(): return lax.ppermute(x, 'dp', [(i, i ^ bit) for i in range(n_dp)])]
    squeeze x1, local copies, waits for them, and re-layouts: 2.89 us -> 0.98 us  [local(): share[k]]
  transfers between devices with their start and end apart: 47 -> 42, of which waited for: 17 -> 20; matrix products, arithmetic and copies ran while one was open for 5% -> 6% of each run, Pallas kernels for 13% -> 25%
where the time goes in v3:
time: 165 us; the launch traced here: 164 us
  waiting for transfers between devices  72.8 us (44%)
  Pallas kernels  41 us (25%)
  starting transfers between devices  35.4 us (21%)
  local copies, waits for them, and re-layouts  7.58 us (5%)
  other arithmetic  6.68 us (4%)
    ppermute x10, waiting for transfers between devices, shift(): lax.ppermute(x, 'tensor', [(i, (i - by) % n_tensor) for i in range(n_tens...  41.4 us
    ppermute x32, waiting for transfers between devices, swap(): return lax.ppermute(x, 'dp', [(i, i ^ bit) for i in range(n_dp)])  31.5 us
    ppermute x32, starting transfers between devices, swap(): return lax.ppermute(x, 'dp', [(i, i ^ bit) for i in range(n_dp)])  20.1 us
    ppermute x10, starting transfers between devices, shift(): lax.ppermute(x, 'tensor', [(i, (i - by) % n_tensor) for i in range(n_tens...  15.2 us
    pallas_call x2, Pallas kernels, weight_grad(): pl.pallas_call(body, grid_spec=pltpu.PrefetchScalarGridSpec(num_scalar_pr...  12 us
    pallas_call x2, Pallas kernels, hidden_grad(): pl.pallas_call(body, grid_spec=pltpu.PrefetchScalarGridSpec(num_scalar_pr...  11.7 us
    pallas_call x1, Pallas kernels, project(): pl.pallas_call(body, grid_spec=pltpu.PrefetchScalarGridSpec(num_scalar_pr...  11 us
    add x1, other arithmetic, local(): total = keep + swap(sent, 1, n_dp).astype(F32)  3.55 us
  transfers between devices with their start and end apart: 42, of which 20 were waited for; matrix products, arithmetic and copies ran while one was open for 6% of the time, Pallas kernels for 25%

profile of v3, /device:TPU:0, one launch (start us, length us, event | category | flops | bytes accessed | tf_op | source)
XLA Modules:
  0.0 164.4 jit_solution(15561285552770469263)
XLA Ops:
  1.7 3.0 %collective-permute-start = (bf16[128,1024]{1,0:T(8,128)(2,1)S(1)}, bf16[128,1024]{1,0:T(8,128)(2,1)S(1)}, u32[]{:S(2)}, u32[]{:S(2)}) collective-permute-start(bf16[128,1024]{1,0:T(8,128)(2,1)S(1)} %get-tuple-element.38.rest_0_.rest_3_), channel_id=1, source_target_pairs={{0,8},{4,12},{8,0},{12,4},{16,24},{20,28},{24,16},{28,20},{1,9},{5... | collective-permute-start | bytes 786440 | tf_op jit(solution)/shard_map/ppermute | solution.py:17
  4.8 1.5 collective-permute-start.4
  6.8 3.6 %collective-permute-start.6 = (bf16[256,1024]{1,0:T(8,128)(2,1)}, bf16[256,1024]{1,0:T(8,128)(2,1)S(1)}, u32[]{:S(2)}, u32[]{:S(2)}) collective-permute-start(bf16[256,1024]{1,0:T(8,128)(2,1)} %param.5), channel_id=1, source_target_pairs={{0,3},{1,0},{2,1},{3,2},{4,7},{5,4},{6,5},{7,6},{8,11},{9,8},{10,9... | collective-permute-start | bytes 1572872 | tf_op jit(solution)/shard_map/ppermute | solution.py:132
  11.1 1.7 %collective-permute-start.3 = (bf16[128,1024]{1,0:T(8,128)(2,1)S(1)}, bf16[128,1024]{1,0:T(8,128)(2,1)S(1)}, u32[]{:S(2)}, u32[]{:S(2)}) collective-permute-start(bf16[128,1024]{1,0:T(8,128)(2,1)S(1)} %get-tuple-element.39.rest_1_.rest_4_), channel_id=1, source_target_pairs={{0,8},{4,12},{8,0},{12,4},{16,24},{20,28},{24,16},{28,20},{1,9},{5... | collective-permute-start | bytes 786440 | tf_op jit(solution)/shard_map/ppermute | solution.py:17
  13.9 1.5 collective-permute-start.2
  15.5 4.1 %collective-permute-done.1.rest_8_.rest_11_ = bf16[128,1024]{1,0:T(8,128)(2,1)S(1)} collective-permute-done((bf16[128,1024]{1,0:T(8,128)(2,1)S(1)}, bf16[128,1024]{1,0:T(8,128)(2,1)S(1)}, u32[]{:S(2)}, u32[]{:S(2)}) %collective-permute-start.1) | collective-permute-done | bytes 262176 | tf_op jit(solution)/shard_map/ppermute | solution.py:17
  19.6 4.1 %collective-permute-done.2.rest_12_.rest_0_ = bf16[128,1024]{1,0:T(8,128)(2,1)S(1)} collective-permute-done((bf16[128,1024]{1,0:T(8,128)(2,1)S(1)}, bf16[128,1024]{1,0:T(8,128)(2,1)S(1)}, u32[]{:S(2)}, u32[]{:S(2)}) %collective-permute-start.2) | collective-permute-done | bytes 262176 | tf_op jit(solution)/shard_map/ppermute | solution.py:17
  23.8 2.3 %collective-permute-done.5.rest_13_.rest_1_ = bf16[128,1024]{1,0:T(8,128)(2,1)} collective-permute-done((bf16[128,1024]{1,0:T(8,128)(2,1)S(1)}, bf16[128,1024]{1,0:T(8,128)(2,1)}, u32[]{:S(2)}, u32[]{:S(2)}) %collective-permute-start.5) | collective-permute-done | bytes 262176 | tf_op jit(solution)/shard_map/ppermute | solution.py:17
  26.0 7.0 %collective-permute-done.7 = bf16[256,1024]{1,0:T(8,128)(2,1)S(1)} collective-permute-done((bf16[256,1024]{1,0:T(8,128)(2,1)}, bf16[256,1024]{1,0:T(8,128)(2,1)S(1)}, u32[]{:S(2)}, u32[]{:S(2)}) %collective-permute-start.7) | collective-permute-done | bytes 524320 | tf_op jit(solution)/shard_map/ppermute | solution.py:132
  34.3 1.5 collective-permute-start.19
  40.2 1.7 %collective-permute-start.16 = (bf16[128,1024]{1,0:T(8,128)(2,1)}, bf16[128,1024]{1,0:T(8,128)(2,1)S(1)}, u32[]{:S(2)}, u32[]{:S(2)}) collective-permute-start(bf16[128,1024]{1,0:T(8,128)(2,1)} %slice.81), channel_id=1, source_target_pairs={{0,3},{1,0},{2,1},{3,2},{4,7},{5,4},{6,5},{7,6},{8,11},{9,8},{10,9... | collective-permute-start | bytes 786440 | tf_op jit(solution)/shard_map/ppermute | solution.py:132
  42.9 11.0 %project.1 = (bf16[512,256]{1,0:T(8,128)(2,1)}, bf16[4,128,256]{2,1,0:T(8,128)(2,1)}, bf16[256,512]{1,0:T(8,128)(2,1)}) custom-call(s32[2]{0:T(128)} %pad_add_fusion.where_ref, bf16[512,8192]{1,0:T(8,128)(2,1)} %h_ref.5, f32[1,128]{1,0:T(1,128)} %s_ref.1, bf16[512,256]{1,0:T(8,128)(2,1)} %c_ref.1, bf16[128,1024]{1,0:T(8,128)(2,1)} %copy-done.4, ...), custom_call_target="tpu_custom_call" | custom-call | tf_op jit(solution)/shard_map/project/pallas_call | solution.py:81
  54.0 1.6 slice_bitcast_fusion.8
  55.5 3.5 %collective-permute-start.20 = (bf16[128,256]{1,0:T(8,128)(2,1)S(1)}, bf16[128,256]{1,0:T(8,128)(2,1)S(1)}, u32[]{:S(2)}, u32[]{:S(2)}) collective-permute-start(bf16[128,256]{1,0:T(8,128)(2,1)S(1)} %get-tuple-element.89), channel_id=1, source_target_pairs={{0,3},{1,0},{2,1},{3,2},{4,7},{5,4},{6,5},{7,6},{8,11},{9,8},{10,9... | collective-permute-start | bytes 196616 | tf_op jit(solution)/shard_map/ppermute | solution.py:132
  59.7 3.2 %hidden_share.1 = bf16[4,128,2048]{2,1,0:T(8,128)(2,1)} custom-call(bf16[4,128,256]{2,1,0:T(8,128)(2,1)} %get-tuple-element.48.d_ref, bf16[128,1024]{1,0:T(8,128)(2,1)} %copy-done.15, bf16[128,1024]{1,0:T(8,128)(2,1)} %collective-permute-done.5.rest_13_.rest_1_, bf16[128,1024]{1,0:T(8,128)(2,1)} %copy-done.16, ...), custom_call_target="tpu_custom_call" | custom-call | tf_op jit(solution)/shard_map/hidden_share/pallas_call | solution.py:151
  62.9 5.7 %weight_grad_odd.1 = bf16[4,256,1024]{2,1,0:T(8,128)(2,1)} custom-call(s32[2]{0:T(128)} %pad_add_fusion.where_ref, bf16[256,512]{1,0:T(8,128)(2,1)} %get-tuple-element.53.d_ref, bf16[512,8192]{1,0:T(8,128)(2,1)} %h_ref.5), custom_call_target="tpu_custom_call" | custom-call | tf_op jit(solution)/shard_map/weight_grad_odd/pallas_call | solution.py:115
  68.8 1.6 collective-permute-start.24
  70.9 6.3 %weight_grad_even.1 = f32[4,256,1024]{2,1,0:T(8,128)} custom-call(s32[2]{0:T(128)} %pad_add_fusion.where_ref, bf16[256,512]{1,0:T(8,128)(2,1)} %get-tuple-element.53.d_ref, bf16[512,8192]{1,0:T(8,128)(2,1)} %h_ref.5), custom_call_target="tpu_custom_call" | custom-call | tf_op jit(solution)/shard_map/weight_grad_even/pallas_call | solution.py:115
  77.1 3.6 %convert_add_fusion = f32[4,256,1024]{2,1,0:T(8,128)S(1)} fusion(f32[4,256,1024]{2,1,0:T(8,128)} %weight_grad_even.1, bf16[4,256,1024]{2,1,0:T(8,128)(2,1)} %collective-permute-done.23), kind=kLoop, calls=%fused_computation | loop fusion | flops 2097152 | bytes 10485760 | tf_op jit(solution)/shard_map/add | solution.py:278
  80.7 2.6 %collective-permute-done.24.rest_6_ = bf16[256,1024]{1,0:T(8,128)(2,1)} collective-permute-done((bf16[256,1024]{1,0:T(8,128)(2,1)S(1)}, bf16[256,1024]{1,0:T(8,128)(2,1)}, u32[]{:S(2)}, u32[]{:S(2)}) %collective-permute-start.24) | collective-permute-done | bytes 524320 | tf_op jit(solution)/shard_map/ppermute | solution.py:17
  87.1 3.3 %collective-permute-start.28 = (bf16[128,2048]{1,0:T(8,128)(2,1)S(1)}, bf16[128,2048]{1,0:T(8,128)(2,1)S(1)}, u32[]{:S(2)}, u32[]{:S(2)}) collective-permute-start(bf16[128,2048]{1,0:T(8,128)(2,1)S(1)} %get-tuple-element.82), channel_id=1, source_target_pairs={{0,3},{1,0},{2,1},{3,2},{4,7},{5,4},{6,5},{7,6},{8,11},{9,8},{10,9... | collective-permute-start | bytes 1572872 | tf_op jit(solution)/shard_map/ppermute | solution.py:132
  90.4 7.8 %collective-permute-done.26 = bf16[2,128,1024]{2,1,0:T(8,128)(2,1)S(1)} collective-permute-done((bf16[2,128,1024]{2,1,0:T(8,128)(2,1)S(1)}, bf16[2,128,1024]{2,1,0:T(8,128)(2,1)S(1)}, u32[]{:S(2)}, u32[]{:S(2)}) %collective-permute-start.26) | collective-permute-done | bytes 524320 | tf_op jit(solution)/shard_map/ppermute | solution.py:17
  98.8 3.9 %collective-permute-done.28.rest_1_ = bf16[128,2048]{1,0:T(8,128)(2,1)S(1)} collective-permute-done((bf16[128,2048]{1,0:T(8,128)(2,1)S(1)}, bf16[128,2048]{1,0:T(8,128)(2,1)S(1)}, u32[]{:S(2)}, u32[]{:S(2)}) %collective-permute-start.28) | collective-permute-done | bytes 524320 | tf_op jit(solution)/shard_map/ppermute | solution.py:132
  102.7 10.7 %collective-permute-done.29.rest_3_ = bf16[128,2048]{1,0:T(8,128)(2,1)S(1)} collective-permute-done((bf16[128,2048]{1,0:T(8,128)(2,1)S(1)}, bf16[128,2048]{1,0:T(8,128)(2,1)S(1)}, u32[]{:S(2)}, u32[]{:S(2)}) %collective-permute-start.29) | collective-permute-done | bytes 524320 | tf_op jit(solution)/shard_map/ppermute | solution.py:132
  114.4 1.5 collective-permute-start.31
  116.0 2.2 %collective-permute-start.32 = (bf16[128,2048]{1,0:T(8,128)(2,1)S(1)}, bf16[128,2048]{1,0:T(8,128)(2,1)S(1)}, u32[]{:S(2)}, u32[]{:S(2)}) collective-permute-start(bf16[128,2048]{1,0:T(8,128)(2,1)S(1)} %get-tuple-element.80), channel_id=1, source_target_pairs={{0,2},{1,3},{2,0},{3,1},{4,6},{5,7},{6,4},{7,5},{8,10},{9,11},{10,... | collective-permute-start | bytes 1572872 | tf_op jit(solution)/shard_map/ppermute | solution.py:132
  118.7 1.5 collective-permute-done.30
  121.1 19.7 %collective-permute-done.32.rest_2_ = bf16[128,2048]{1,0:T(8,128)(2,1)S(1)} collective-permute-done((bf16[128,2048]{1,0:T(8,128)(2,1)S(1)}, bf16[128,2048]{1,0:T(8,128)(2,1)S(1)}, u32[]{:S(2)}, u32[]{:S(2)}) %collective-permute-start.32) | collective-permute-done | bytes 524320 | tf_op jit(solution)/shard_map/ppermute | solution.py:132
  143.1 3.0 %collective-permute-done.40 = f32[3,256]{1,0:T(4,128)S(1)} collective-permute-done((f32[3,256]{1,0:T(4,128)S(1)}, f32[3,256]{1,0:T(4,128)S(1)}, u32[]{:S(2)}, u32[]{:S(2)}) %collective-permute-start.40) | collective-permute-done | bytes 3104 | tf_op jit(solution)/shard_map/ppermute | solution.py:17
  147.6 4.6 %hidden_grad.2.rest_19_ = bf16[128,8192]{1,0:T(8,128)(2,1)} custom-call(s32[2]{0:T(128)} %pad_add_fusion.where_ref, bf16[128,256]{1,0:T(8,128)(2,1)} %get-tuple-element.86.rest_0_, bf16[128,512]{1,0:T(8,128)(2,1)} %copy-done.17, bf16[128,256]{1,0:T(8,128)(2,1)} %copy-done.23, bf16[128,1024]{1,0:T(8,128)(2,1)} %copy-done.4, bf16[128,1024]{1,0:T(8,128)(2,1)} %copy-done.3, ...), custom_call_target="tpu_custom_call" | custom-call | tf_op jit(solution)/shard_map/hidden_grad/pallas_call | solution.py:201
  153.1 7.1 %hidden_grad.3.rest_4_ = bf16[128,8192]{1,0:T(8,128)(2,1)} custom-call(s32[2]{0:T(128)} %pad_add_fusion.where_ref, bf16[128,256]{1,0:T(8,128)(2,1)} %get-tuple-element.86.rest_0_, bf16[128,512]{1,0:T(8,128)(2,1)} %copy-done.17, bf16[128,256]{1,0:T(8,128)(2,1)} %copy-done.23, bf16[128,1024]{1,0:T(8,128)(2,1)} %copy-done.6, ...), custom_call_target="tpu_custom_call", output_to_operand_aliasing={{}: (20, {})} | custom-call | tf_op jit(solution)/shard_map/hidden_grad/pallas_call | solution.py:201
  160.2 3.0 %add_shares.1 = bf16[128,8192]{1,0:T(8,128)(2,1)} custom-call(s32[2]{0:T(128)} %pad_add_fusion.where_ref, bf16[128,2048]{1,0:T(8,128)(2,1)} %get-tuple-element.83.rest_0_, bf16[128,2048]{1,0:T(8,128)(2,1)} %copy-done.18, bf16[128,2048]{1,0:T(8,128)(2,1)} %copy-done.20, bf16[128,2048]{1,0:T(8,128)(2,1)} %copy-done.19, ...), custom_call_target="tpu_custom_call", output_to_operand_aliasing={{}: (5, {})} | custom-call | tf_op jit(solution)/shard_map/add_shares/pallas_call | solution.py:230
  (137 shorter events, 23.8 us)
Async XLA Ops:
  1.7 9.3 %collective-permute-start = (bf16[128,1024]{1,0:T(8,128)(2,1)S(1)}, bf16[128,1024]{1,0:T(8,128)(2,1)S(1)}, u32[]{:S(2)}, u32[]{:S(2)}) collective-permute-start(bf16[128,1024]{1,0:T(8,128)(2,1)S(1)} %get-tuple-element.38.rest_0_.rest_3_), channel_id=1, source_target_pairs={{0,8},{4,12},{8,0},{12,4},{16,24},{20,28},{24,16},{28,20},{1,9},{5... | collective-permute-start | bytes 786440 | tf_op jit(solution)/shard_map/ppermute | solution.py:17
  4.8 9.2 %collective-permute-start.4 = (bf16[128,1024]{1,0:T(8,128)(2,1)S(1)}, bf16[128,1024]{1,0:T(8,128)(2,1)S(1)}, u32[]{:S(2)}, u32[]{:S(2)}) collective-permute-start(bf16[128,1024]{1,0:T(8,128)(2,1)S(1)} %get-tuple-element.39.rest_1_.rest_4_), channel_id=1, source_target_pairs={{0,16},{4,20},{8,24},{12,28},{16,0},{20,4},{24,8},{28,12},{1,17},{... | collective-permute-start | bytes 786440 | tf_op jit(solution)/shard_map/ppermute | solution.py:17
  6.3 13.3 %collective-permute-start.1 = (bf16[128,1024]{1,0:T(8,128)(2,1)S(1)}, bf16[128,1024]{1,0:T(8,128)(2,1)S(1)}, u32[]{:S(2)}, u32[]{:S(2)}) collective-permute-start(bf16[128,1024]{1,0:T(8,128)(2,1)S(1)} %get-tuple-element.38.rest_0_.rest_3_), channel_id=1, source_target_pairs={{0,16},{4,20},{8,24},{12,28},{16,0},{20,4},{24,8},{28,12},{1,17},{... | collective-permute-start | bytes 786440 | tf_op jit(solution)/shard_map/ppermute | solution.py:17
  6.8 19.2 %collective-permute-start.6 = (bf16[256,1024]{1,0:T(8,128)(2,1)}, bf16[256,1024]{1,0:T(8,128)(2,1)S(1)}, u32[]{:S(2)}, u32[]{:S(2)}) collective-permute-start(bf16[256,1024]{1,0:T(8,128)(2,1)} %param.5), channel_id=1, source_target_pairs={{0,3},{1,0},{2,1},{3,2},{4,7},{5,4},{6,5},{7,6},{8,11},{9,8},{10,9... | collective-permute-start | bytes 1572872 | tf_op jit(solution)/shard_map/ppermute | solution.py:132
  10.4 22.7 %collective-permute-start.7 = (bf16[256,1024]{1,0:T(8,128)(2,1)}, bf16[256,1024]{1,0:T(8,128)(2,1)S(1)}, u32[]{:S(2)}, u32[]{:S(2)}) collective-permute-start(bf16[256,1024]{1,0:T(8,128)(2,1)} %param.5), channel_id=1, source_target_pairs={{0,1},{1,2},{2,3},{3,0},{4,5},{5,6},{6,7},{7,4},{8,9},{9,10},{10,1... | collective-permute-start | bytes 1572872 | tf_op jit(solution)/shard_map/ppermute | solution.py:132
  11.1 8.6 %collective-permute-start.3 = (bf16[128,1024]{1,0:T(8,128)(2,1)S(1)}, bf16[128,1024]{1,0:T(8,128)(2,1)S(1)}, u32[]{:S(2)}, u32[]{:S(2)}) collective-permute-start(bf16[128,1024]{1,0:T(8,128)(2,1)S(1)} %get-tuple-element.39.rest_1_.rest_4_), channel_id=1, source_target_pairs={{0,8},{4,12},{8,0},{12,4},{16,24},{20,28},{24,16},{28,20},{1,9},{5... | collective-permute-start | bytes 786440 | tf_op jit(solution)/shard_map/ppermute | solution.py:17
  13.9 9.8 %collective-permute-start.2 = (bf16[128,1024]{1,0:T(8,128)(2,1)S(1)}, bf16[128,1024]{1,0:T(8,128)(2,1)S(1)}, u32[]{:S(2)}, u32[]{:S(2)}) collective-permute-start(bf16[128,1024]{1,0:T(8,128)(2,1)S(1)} %collective-permute-done.rest_4_.rest_3_), channel_id=1, source_target_pairs={{0,16},{4,20},{8,24},{12,28},{16,0},{20,4},{24,8},{28,12},{1,17},{... | collective-permute-start | bytes 786440 | tf_op jit(solution)/shard_map/ppermute | solution.py:17
  19.5 6.5 %collective-permute-start.5 = (bf16[128,1024]{1,0:T(8,128)(2,1)S(1)}, bf16[128,1024]{1,0:T(8,128)(2,1)}, u32[]{:S(2)}, u32[]{:S(2)}) collective-permute-start(bf16[128,1024]{1,0:T(8,128)(2,1)S(1)} %collective-permute-done.4.rest_9_.rest_12_), channel_id=1, source_target_pairs={{0,8},{4,12},{8,0},{12,4},{16,24},{20,28},{24,16},{28,20},{1,9},{5... | collective-permute-start | bytes 786440 | tf_op jit(solution)/shard_map/ppermute | solution.py:17
  33.7 35.0 %collective-permute-start.18 = (bf16[512,1024]{1,0:T(8,128)(2,1)S(1)}, bf16[512,1024]{1,0:T(8,128)(2,1)}, u32[]{:S(2)}, u32[]{:S(2)}) collective-permute-start(bf16[512,1024]{1,0:T(8,128)(2,1)S(1)} %constant_dynamic-update-slice_fusion.rest_5_), channel_id=1, source_target_pairs={{0,8},{4,12},{8,0},{12,4},{16,24},{20,28},{24,16},{28,20},{1,9},{5... | collective-permute-start | bytes 3145736 | tf_op jit(solution)/shard_map/ppermute | solution.py:17
  34.3 34.4 %collective-permute-start.19 = (bf16[512,1024]{1,0:T(8,128)(2,1)S(1)}, bf16[512,1024]{1,0:T(8,128)(2,1)}, u32[]{:S(2)}, u32[]{:S(2)}) collective-permute-start(bf16[512,1024]{1,0:T(8,128)(2,1)S(1)} %constant_dynamic-update-slice_fusion.rest_5_), channel_id=1, source_target_pairs={{0,16},{4,20},{8,24},{12,28},{16,0},{20,4},{24,8},{28,12},{1,17},{... | collective-permute-start | bytes 3145736 | tf_op jit(solution)/shard_map/ppermute | solution.py:17
  40.2 18.8 %collective-permute-start.16 = (bf16[128,1024]{1,0:T(8,128)(2,1)}, bf16[128,1024]{1,0:T(8,128)(2,1)S(1)}, u32[]{:S(2)}, u32[]{:S(2)}) collective-permute-start(bf16[128,1024]{1,0:T(8,128)(2,1)} %slice.81), channel_id=1, source_target_pairs={{0,3},{1,0},{2,1},{3,2},{4,7},{5,4},{6,5},{7,6},{8,11},{9,8},{10,9... | collective-permute-start | bytes 786440 | tf_op jit(solution)/shard_map/ppermute | solution.py:132
  42.0 17.1 %collective-permute-start.17 = (bf16[128,1024]{1,0:T(8,128)(2,1)}, bf16[128,1024]{1,0:T(8,128)(2,1)S(1)}, u32[]{:S(2)}, u32[]{:S(2)}) collective-permute-start(bf16[128,1024]{1,0:T(8,128)(2,1)} %slice.82), channel_id=1, source_target_pairs={{0,1},{1,2},{2,3},{3,0},{4,5},{5,6},{6,7},{7,4},{8,9},{9,10},{10,1... | collective-permute-start | bytes 786440 | tf_op jit(solution)/shard_map/ppermute | solution.py:132
  55.5 13.1 %collective-permute-start.20 = (bf16[128,256]{1,0:T(8,128)(2,1)S(1)}, bf16[128,256]{1,0:T(8,128)(2,1)S(1)}, u32[]{:S(2)}, u32[]{:S(2)}) collective-permute-start(bf16[128,256]{1,0:T(8,128)(2,1)S(1)} %get-tuple-element.89), channel_id=1, source_target_pairs={{0,3},{1,0},{2,1},{3,2},{4,7},{5,4},{6,5},{7,6},{8,11},{9,8},{10,9... | collective-permute-start | bytes 196616 | tf_op jit(solution)/shard_map/ppermute | solution.py:132
  59.1 9.6 %collective-permute-start.21 = (bf16[128,256]{1,0:T(8,128)(2,1)S(1)}, bf16[128,256]{1,0:T(8,128)(2,1)S(1)}, u32[]{:S(2)}, u32[]{:S(2)}) collective-permute-start(bf16[128,256]{1,0:T(8,128)(2,1)S(1)} %get-tuple-element.88), channel_id=1, source_target_pairs={{0,2},{1,3},{2,0},{3,1},{4,6},{5,7},{6,4},{7,5},{8,10},{9,11},{10,... | collective-permute-start | bytes 196616 | tf_op jit(solution)/shard_map/ppermute | solution.py:132
  59.1 9.6 %collective-permute-start.22 = (bf16[128,256]{1,0:T(8,128)(2,1)S(1)}, bf16[128,256]{1,0:T(8,128)(2,1)S(1)}, u32[]{:S(2)}, u32[]{:S(2)}) collective-permute-start(bf16[128,256]{1,0:T(8,128)(2,1)S(1)} %get-tuple-element.87), channel_id=1, source_target_pairs={{0,1},{1,2},{2,3},{3,0},{4,5},{5,6},{6,7},{7,4},{8,9},{9,10},{10,1... | collective-permute-start | bytes 196616 | tf_op jit(solution)/shard_map/ppermute | solution.py:132
  68.7 8.5 %collective-permute-start.23 = (bf16[4,256,1024]{2,1,0:T(8,128)(2,1)}, bf16[4,256,1024]{2,1,0:T(8,128)(2,1)}, u32[]{:S(2)}, u32[]{:S(2)}) collective-permute-start(bf16[4,256,1024]{2,1,0:T(8,128)(2,1)} %weight_grad_odd.1), channel_id=1, source_target_pairs={{0,4},{4,0},{8,12},{12,8},{16,20},{20,16},{24,28},{28,24},{1,5},{5... | collective-permute-start | bytes 6291464 | tf_op jit(solution)/shard_map/ppermute | solution.py:17
  68.8 14.5 %collective-permute-start.24 = (bf16[256,1024]{1,0:T(8,128)(2,1)S(1)}, bf16[256,1024]{1,0:T(8,128)(2,1)}, u32[]{:S(2)}, u32[]{:S(2)}) collective-permute-start(bf16[256,1024]{1,0:T(8,128)(2,1)S(1)} %constant_dynamic-update-slice_fusion.2.rest_6_), channel_id=1, source_target_pairs={{0,8},{4,12},{8,0},{12,4},{16,24},{20,28},{24,16},{28,20},{1,9},{5... | collective-permute-start | bytes 1572872 | tf_op jit(solution)/shard_map/ppermute | solution.py:17
  70.4 14.1 %collective-permute-start.25 = (bf16[256,1024]{1,0:T(8,128)(2,1)S(1)}, bf16[256,1024]{1,0:T(8,128)(2,1)}, u32[]{:S(2)}, u32[]{:S(2)}) collective-permute-start(bf16[256,1024]{1,0:T(8,128)(2,1)S(1)} %constant_dynamic-update-slice_fusion.2.rest_6_), channel_id=1, source_target_pairs={{0,16},{4,20},{8,24},{12,28},{16,0},{20,4},{24,8},{28,12},{1,17},{... | collective-permute-start | bytes 1572872 | tf_op jit(solution)/shard_map/ppermute | solution.py:17
  84.9 13.2 %collective-permute-start.26 = (bf16[2,128,1024]{2,1,0:T(8,128)(2,1)S(1)}, bf16[2,128,1024]{2,1,0:T(8,128)(2,1)S(1)}, u32[]{:S(2)}, u32[]{:S(2)}) collective-permute-start(bf16[2,128,1024]{2,1,0:T(8,128)(2,1)S(1)} %slice_bitcast_fusion.3), channel_id=1, source_target_pairs={{0,8},{4,12},{8,0},{12,4},{16,24},{20,28},{24,16},{28,20},{1,9},{5... | collective-permute-start | bytes 1572872 | tf_op jit(solution)/shard_map/ppermute | solution.py:17
  85.5 12.9 %collective-permute-start.27 = (bf16[2,128,1024]{2,1,0:T(8,128)(2,1)S(1)}, bf16[2,128,1024]{2,1,0:T(8,128)(2,1)S(1)}, u32[]{:S(2)}, u32[]{:S(2)}) collective-permute-start(bf16[2,128,1024]{2,1,0:T(8,128)(2,1)S(1)} %slice_bitcast_fusion.2), channel_id=1, source_target_pairs={{0,16},{4,20},{8,24},{12,28},{16,0},{20,4},{24,8},{28,12},{1,17},{... | collective-permute-start | bytes 1572872 | tf_op jit(solution)/shard_map/ppermute | solution.py:17
  87.1 15.6 %collective-permute-start.28 = (bf16[128,2048]{1,0:T(8,128)(2,1)S(1)}, bf16[128,2048]{1,0:T(8,128)(2,1)S(1)}, u32[]{:S(2)}, u32[]{:S(2)}) collective-permute-start(bf16[128,2048]{1,0:T(8,128)(2,1)S(1)} %get-tuple-element.82), channel_id=1, source_target_pairs={{0,3},{1,0},{2,1},{3,2},{4,7},{5,4},{6,5},{7,6},{8,11},{9,8},{10,9... | collective-permute-start | bytes 1572872 | tf_op jit(solution)/shard_map/ppermute | solution.py:132
  90.4 23.0 %collective-permute-start.29 = (bf16[128,2048]{1,0:T(8,128)(2,1)S(1)}, bf16[128,2048]{1,0:T(8,128)(2,1)S(1)}, u32[]{:S(2)}, u32[]{:S(2)}) collective-permute-start(bf16[128,2048]{1,0:T(8,128)(2,1)S(1)} %get-tuple-element.81), channel_id=1, source_target_pairs={{0,1},{1,2},{2,3},{3,0},{4,5},{5,6},{6,7},{7,4},{8,9},{9,10},{10,1... | collective-permute-start | bytes 1572872 | tf_op jit(solution)/shard_map/ppermute | solution.py:132
  113.4 6.7 %collective-permute-start.30 = (bf16[128,1024]{1,0:T(8,128)(2,1)S(1)}, bf16[128,1024]{1,0:T(8,128)(2,1)S(1)}, u32[]{:S(2)}, u32[]{:S(2)}) collective-permute-start(bf16[128,1024]{1,0:T(8,128)(2,1)S(1)} %fusion.8), channel_id=1, source_target_pairs={{0,16},{4,20},{8,24},{12,28},{16,0},{20,4},{24,8},{28,12},{1,17},{... | collective-permute-start | bytes 786440 | tf_op jit(solution)/shard_map/ppermute | solution.py:17
  114.4 6.4 %collective-permute-start.31 = (bf16[128,1024]{1,0:T(8,128)(2,1)S(1)}, bf16[128,1024]{1,0:T(8,128)(2,1)S(1)}, u32[]{:S(2)}, u32[]{:S(2)}) collective-permute-start(bf16[128,1024]{1,0:T(8,128)(2,1)S(1)} %fusion.9), channel_id=1, source_target_pairs={{0,8},{4,12},{8,0},{12,4},{16,24},{20,28},{24,16},{28,20},{1,9},{5... | collective-permute-start | bytes 786440 | tf_op jit(solution)/shard_map/ppermute | solution.py:17
  116.0 24.8 %collective-permute-start.32 = (bf16[128,2048]{1,0:T(8,128)(2,1)S(1)}, bf16[128,2048]{1,0:T(8,128)(2,1)S(1)}, u32[]{:S(2)}, u32[]{:S(2)}) collective-permute-start(bf16[128,2048]{1,0:T(8,128)(2,1)S(1)} %get-tuple-element.80), channel_id=1, source_target_pairs={{0,2},{1,3},{2,0},{3,1},{4,6},{5,7},{6,4},{7,5},{8,10},{9,11},{10,... | collective-permute-start | bytes 1572872 | tf_op jit(solution)/shard_map/ppermute | solution.py:132
  118.2 24.9 %collective-permute-start.37 = (bf16[512,1024]{1,0:T(8,128)(2,1)S(1)}, bf16[512,1024]{1,0:T(8,128)(2,1)S(1)}, u32[]{:S(2)}, u32[]{:S(2)}) collective-permute-start(bf16[512,1024]{1,0:T(8,128)(2,1)S(1)} %constant_dynamic-update-slice_fusion.rest_5_), channel_id=1, source_target_pairs={{0,4},{4,0},{8,12},{12,8},{16,20},{20,16},{24,28},{28,24},{1,5},{5... | collective-permute-start | bytes 3145736 | tf_op jit(solution)/shard_map/ppermute | solution.py:17
  118.2 34.1 %collective-permute-start.33 = (bf16[512,1024]{1,0:T(8,128)(2,1)}, bf16[512,1024]{1,0:T(8,128)(2,1)}, u32[]{:S(2)}, u32[]{:S(2)}) collective-permute-start(bf16[512,1024]{1,0:T(8,128)(2,1)} %collective-permute-done.18.rest_5_), channel_id=1, source_target_pairs={{0,4},{4,0},{8,12},{12,8},{16,20},{20,16},{24,28},{28,24},{1,5},{5... | collective-permute-start | bytes 3145736 | tf_op jit(solution)/shard_map/ppermute | solution.py:17
  120.1 32.1 %collective-permute-start.35 = (bf16[512,1024]{1,0:T(8,128)(2,1)}, bf16[512,1024]{1,0:T(8,128)(2,1)}, u32[]{:S(2)}, u32[]{:S(2)}) collective-permute-start(bf16[512,1024]{1,0:T(8,128)(2,1)} %collective-permute-done.19.rest_13_), channel_id=1, source_target_pairs={{0,4},{4,0},{8,12},{12,8},{16,20},{20,16},{24,28},{28,24},{1,5},{5... | collective-permute-start | bytes 3145736 | tf_op jit(solution)/shard_map/ppermute | solution.py:17
  141.3 4.9 %collective-permute-start.38 = (bf16[256,1024]{1,0:T(8,128)(2,1)S(1)}, bf16[256,1024]{1,0:T(8,128)(2,1)S(1)}, u32[]{:S(2)}, u32[]{:S(2)}) collective-permute-start(bf16[256,1024]{1,0:T(8,128)(2,1)S(1)} %constant_dynamic-update-slice_fusion.2.rest_6_), channel_id=1, source_target_pairs={{0,4},{4,0},{8,12},{12,8},{16,20},{20,16},{24,28},{28,24},{1,5},{5... | collective-permute-start | bytes 1572872 | tf_op jit(solution)/shard_map/ppermute | solution.py:17
  143.1 9.2 %collective-permute-start.34 = (bf16[256,1024]{1,0:T(8,128)(2,1)}, bf16[256,1024]{1,0:T(8,128)(2,1)S(1)}, u32[]{:S(2)}, u32[]{:S(2)}) collective-permute-start(bf16[256,1024]{1,0:T(8,128)(2,1)} %collective-permute-done.24.rest_6_), channel_id=1, source_target_pairs={{0,4},{4,0},{8,12},{12,8},{16,20},{20,16},{24,28},{28,24},{1,5},{5... | collective-permute-start | bytes 1572872 | tf_op jit(solution)/shard_map/ppermute | solution.py:17
  146.1 6.1 %collective-permute-start.36 = (bf16[256,1024]{1,0:T(8,128)(2,1)}, bf16[256,1024]{1,0:T(8,128)(2,1)}, u32[]{:S(2)}, u32[]{:S(2)}) collective-permute-start(bf16[256,1024]{1,0:T(8,128)(2,1)} %collective-permute-done.25.rest_14_), channel_id=1, source_target_pairs={{0,4},{4,0},{8,12},{12,8},{16,20},{20,16},{24,28},{28,24},{1,5},{5... | collective-permute-start | bytes 1572872 | tf_op jit(solution)/shard_map/ppermute | solution.py:17
  146.2 17.0 %collective-permute-start.41 = (f32[3,256]{1,0:T(4,128)S(1)}, f32[3,256]{1,0:T(4,128)S(1)}, u32[]{:S(2)}, u32[]{:S(2)}) collective-permute-start(f32[3,256]{1,0:T(4,128)S(1)} %fusion.13), channel_id=1, source_target_pairs={{0,16},{4,20},{8,24},{12,28},{16,0},{20,4},{24,8},{28,12},{1,17},{... | collective-permute-start | bytes 9224 | tf_op jit(solution)/shard_map/ppermute | solution.py:17
  (34 other events, 463.4 us)

commit v4 on v3

--- a/solution.py
+++ b/solution.py
@@ -254,30 +254,38 @@
     where = jnp.stack([lax.axis_index("dp"), lax.axis_index("tensor")]).astype(jnp.int32)
     ahead = shift(weight, 1, n_tensor)
     behind = shift(weight, -1, n_tensor)
-    parts = gather_links(weight, n_dp)
+    parts = [add_core(have, n_dp) for have in gather_links(weight, n_dp)]
     parts, ahead, behind = lax.optimization_barrier((parts, ahead, behind))
     pair = {0: jnp.concatenate([ahead, behind], 0)}
     low, high = shift(ahead[:half], 1, n_tensor), shift(behind[half:], -1, n_tensor)
     bits = [1 << i for i in range(1, n_dp.bit_length() - 1)]
     pair.update({bit: swap(pair[0], bit, n_dp) for bit in bits})
-    parts = [add_core(have, n_dp) for have in parts]
     keys_values, d_slots, d_t = project(hidden, parts, qk_scale, cotangent, where, n_tensor)
     near = [0, 1]
     linked = [r for bit in bits for r in (bit, bit ^ 1)]
     far = [r for r in range(n_dp) if r not in near and r not in linked]
     share = hidden_share(d_slots, parts, far)
     d_t, share, low, high = lax.optimization_barrier((d_t, share, low, high))
-    shares = [share[0]] + [shift(share[k], k, n_tensor) for k in range(1, n_tensor)]
+    cut = share.shape[2] // 2
+    via_ahead = shift(share[2, :, :cut], 1, n_tensor)
+    via_behind = shift(share[2, :, cut:], -1, n_tensor)
     mid = {0: jnp.concatenate([low, high], 0)}
     mid.update({bit: swap(mid[0], bit, n_dp) for bit in bits})
     sent = weight_grad(d_t, hidden, where, n_dp, 1, BF16)
     d_rest = [shift(d_slots[k], k, n_tensor) for k in range(1, n_tensor)]
-    d_t, sent, pair, d_rest = lax.optimization_barrier((d_t, sent, pair, d_rest))
+    due = (d_t, sent, pair, d_rest, via_ahead, via_behind)
+    d_t, sent, pair, d_rest, via_ahead, via_behind = lax.optimization_barrier(due)
+    to_ahead = jnp.concatenate([share[1, :, :cut] + via_ahead, share[1, :, cut:]], 1)
+    to_behind = jnp.concatenate([share[-1, :, :cut], share[-1, :, cut:] + via_behind], 1)
+    from_ahead, from_behind = shift(to_ahead, 1, n_tensor), shift(to_behind, -1, n_tensor)
     pair = add_core(pair, n_dp)
     keep = weight_grad(d_t, hidden, where, n_dp, 0, F32)
     total = keep + swap(sent, 1, n_dp).astype(F32)
-    total, mid_links = lax.optimization_barrier((total, mid))
-    mid = add_core(mid_links, n_dp)
+    total, mid, from_ahead, from_behind = lax.optimization_barrier((total, mid, from_ahead, from_behind))
+    mid = add_core(mid, n_dp)
+    d_pair = jnp.concatenate([d_rest[0], d_rest[-1]], 1)
+    d_all = (d_slots[0], d_pair, d_rest[1], parts, pair, mid, where)
+    input_grad = hidden_grad(*d_all, near, None)
     count = len(bits)
     total = total.reshape((2,) * count + total.shape[1:])
     sides = [total[..., :half, :], total[..., half:, :]]
@@ -285,19 +293,16 @@
     left = [list(range(count))[::-1], list(range(count))[::-1]]
     for step in range(count):
         if step == count - 1:
-            sides, shares[1], shares[-1] = lax.optimization_barrier((sides, shares[1], shares[-1]))
+            sides, input_grad = lax.optimization_barrier((sides, input_grad))
         for at in range(2):
             b = orders[at][step]
             axis = left[at].index(b)
             left[at].remove(b)
             sides[at] = halve(sides[at], axis, bits[b], n_dp)
+    input_grad = hidden_grad(*d_all, linked, input_grad)
+    sides, input_grad = lax.optimization_barrier((sides, input_grad))
     grad = jnp.concatenate(sides, 0)
-    grad, shares[2] = lax.optimization_barrier((grad, shares[2]))
-    d_pair = jnp.concatenate([d_rest[0], d_rest[-1]], 1)
-    d_all = (d_slots[0], d_pair, d_rest[1], parts, pair, mid, where)
-    input_grad = hidden_grad(*d_all, near, None)
-    input_grad = hidden_grad(*d_all, linked, input_grad)
-    input_grad = add_shares(shares, where, far, width, input_grad)
+    input_grad = add_shares([share[0], from_ahead, from_behind], where, far, width, input_grad)
     w = weight.astype(F32)
     sums = jnp.stack([jnp.sum(grad * w, 1), jnp.sum(w * w, 1), jnp.sum(grad * grad, 1)])
     bit = 1

time: 165 us -> 178 us (1.079)
  local copies, waits for them, and re-layouts: 7.58 us -> 14.2 us
  other arithmetic: 6.68 us -> 12.3 us
  starting transfers between devices: 35.4 us -> 40.9 us
  waiting for transfers between devices: 72.8 us -> 67.8 us
    ppermute x10 -> x11, starting transfers between devices: 15.2 us -> 20.6 us  [shift(): lax.ppermute(x, 'tensor', [(i, (i - by) % n_tensor) for i in range(n_tens...]
    ppermute x32, waiting for transfers between devices: 31.5 us -> 26.8 us  [swap(): return lax.ppermute(x, 'dp', [(i, i ^ bit) for i in range(n_dp)])]
    add x3, other arithmetic: 0.48 us -> 3.5 us  [halve(): return stay + swap(go, bit, n_dp).astype(F32)]
    convert_element_type x4, local copies, waits for them, and re-layouts: 0.13 us -> 2.58 us  [halve(): go = lax.index_in_dim(part, 1, axis, keepdims=False).astype(BF16)]
    squeeze x1 -> x2, local copies, waits for them, and re-layouts: 0.98 us -> 3.08 us  [the longest x1 2.26 us: local(): share[-1, :, :cut]]
    ppermute x10 -> x11, waiting for transfers between devices: 41.4 us -> 41 us  [shift(): lax.ppermute(x, 'tensor', [(i, (i - by) % n_tensor) for i in range(n_tens...]
  transfers between devices with their start and end apart: 42 -> 43, of which waited for: 20 -> 20; matrix products, arithmetic and copies ran while one was open for 6% -> 12% of each run, Pallas kernels for 25% -> 23%
where the time goes in v4:
time: 178 us; the launch traced here: 177 us
  waiting for transfers between devices  67.8 us (38%)
  Pallas kernels  41 us (23%)
  starting transfers between devices  40.9 us (23%)
  local copies, waits for them, and re-layouts  14.2 us (8%)
  other arithmetic  12.3 us (7%)
    ppermute x11, waiting for transfers between devices, shift(): lax.ppermute(x, 'tensor', [(i, (i - by) % n_tensor) for i in range(n_tens...  41 us
    ppermute x32, waiting for transfers between devices, swap(): return lax.ppermute(x, 'dp', [(i, i ^ bit) for i in range(n_dp)])  26.8 us
    ppermute x11, starting transfers between devices, shift(): lax.ppermute(x, 'tensor', [(i, (i - by) % n_tensor) for i in range(n_tens...  20.6 us
    ppermute x32, starting transfers between devices, swap(): return lax.ppermute(x, 'dp', [(i, i ^ bit) for i in range(n_dp)])  20.2 us
    pallas_call x2, Pallas kernels, weight_grad(): pl.pallas_call(body, grid_spec=pltpu.PrefetchScalarGridSpec(num_scalar_pr...  12 us
    pallas_call x2, Pallas kernels, hidden_grad(): pl.pallas_call(body, grid_spec=pltpu.PrefetchScalarGridSpec(num_scalar_pr...  11.7 us
    pallas_call x1, Pallas kernels, project(): pl.pallas_call(body, grid_spec=pltpu.PrefetchScalarGridSpec(num_scalar_pr...  11 us
  transfers between devices with their start and end apart: 43, of which 20 were waited for; matrix products, arithmetic and copies ran while one was open for 12% of the time, Pallas kernels for 23%

profile of v4, /device:TPU:0, one launch (start us, length us, event | category | flops | bytes accessed | tf_op | source)
XLA Modules:
  0.0 177.2 jit_solution(7797446607297143550)
XLA Ops:
  1.7 3.1 %collective-permute-start.10 = (bf16[128,1024]{1,0:T(8,128)(2,1)S(1)}, bf16[128,1024]{1,0:T(8,128)(2,1)S(1)}, u32[]{:S(2)}, u32[]{:S(2)}) collective-permute-start(bf16[128,1024]{1,0:T(8,128)(2,1)S(1)} %get-tuple-element.51.rest_1_.rest_4_), channel_id=1, source_target_pairs={{0,16},{4,20},{8,24},{12,28},{16,0},{20,4},{24,8},{28,12},{1,17},{... | collective-permute-start | bytes 786440 | tf_op jit(solution)/shard_map/ppermute | solution.py:17
  6.9 5.0 %collective-permute-done.10.rest_9_.rest_12_ = bf16[128,1024]{1,0:T(8,128)(2,1)S(1)} collective-permute-done((bf16[128,1024]{1,0:T(8,128)(2,1)S(1)}, bf16[128,1024]{1,0:T(8,128)(2,1)S(1)}, u32[]{:S(2)}, u32[]{:S(2)}) %collective-permute-start.10) | collective-permute-done | bytes 262176 | tf_op jit(solution)/shard_map/ppermute | solution.py:17
  11.9 2.0 %collective-permute-done.1.rest_4_.rest_3_ = bf16[128,1024]{1,0:T(8,128)(2,1)S(1)} collective-permute-done((bf16[128,1024]{1,0:T(8,128)(2,1)S(1)}, bf16[128,1024]{1,0:T(8,128)(2,1)S(1)}, u32[]{:S(2)}, u32[]{:S(2)}) %collective-permute-start.1) | collective-permute-done | bytes 262176 | tf_op jit(solution)/shard_map/ppermute | solution.py:17
  16.7 1.7 collective-permute-start.5
  19.6 3.6 %collective-permute-start.14 = (bf16[256,1024]{1,0:T(8,128)(2,1)}, bf16[256,1024]{1,0:T(8,128)(2,1)S(1)}, u32[]{:S(2)}, u32[]{:S(2)}) collective-permute-start(bf16[256,1024]{1,0:T(8,128)(2,1)} %param.5), channel_id=1, source_target_pairs={{0,3},{1,0},{2,1},{3,2},{4,7},{5,4},{6,5},{7,6},{8,11},{9,8},{10,9... | collective-permute-start | bytes 1572872 | tf_op jit(solution)/shard_map/ppermute | solution.py:132
  26.3 9.5 %collective-permute-done.14 = bf16[256,1024]{1,0:T(8,128)(2,1)S(1)} collective-permute-done((bf16[256,1024]{1,0:T(8,128)(2,1)}, bf16[256,1024]{1,0:T(8,128)(2,1)S(1)}, u32[]{:S(2)}, u32[]{:S(2)}) %collective-permute-start.14) | collective-permute-done | bytes 524320 | tf_op jit(solution)/shard_map/ppermute | solution.py:132
  35.8 8.6 %collective-permute-done.15 = bf16[256,1024]{1,0:T(8,128)(2,1)S(1)} collective-permute-done((bf16[256,1024]{1,0:T(8,128)(2,1)}, bf16[256,1024]{1,0:T(8,128)(2,1)S(1)}, u32[]{:S(2)}, u32[]{:S(2)}) %collective-permute-start.15) | collective-permute-done | bytes 524320 | tf_op jit(solution)/shard_map/ppermute | solution.py:132
  45.3 1.6 collective-permute-start.18
  48.2 1.8 %collective-permute-start.16 = (bf16[128,1024]{1,0:T(8,128)(2,1)}, bf16[128,1024]{1,0:T(8,128)(2,1)S(1)}, u32[]{:S(2)}, u32[]{:S(2)}) collective-permute-start(bf16[128,1024]{1,0:T(8,128)(2,1)} %slice.90), channel_id=1, source_target_pairs={{0,3},{1,0},{2,1},{3,2},{4,7},{5,4},{6,5},{7,6},{8,11},{9,8},{10,9... | collective-permute-start | bytes 786440 | tf_op jit(solution)/shard_map/ppermute | solution.py:132
  50.8 11.0 %project.1 = (bf16[512,256]{1,0:T(8,128)(2,1)}, bf16[4,128,256]{2,1,0:T(8,128)(2,1)}, bf16[256,512]{1,0:T(8,128)(2,1)}) custom-call(s32[2]{0:T(128)} %pad_add_fusion.where_ref, bf16[512,8192]{1,0:T(8,128)(2,1)} %h_ref.5, f32[1,128]{1,0:T(1,128)} %s_ref.1, bf16[512,256]{1,0:T(8,128)(2,1)} %c_ref.1, bf16[128,1024]{1,0:T(8,128)(2,1)} %copy-done.5, ...), custom_call_target="tpu_custom_call" | custom-call | tf_op jit(solution)/shard_map/project/pallas_call | solution.py:81
  61.8 3.3 %hidden_share.1 = bf16[4,128,2048]{2,1,0:T(8,128)(2,1)} custom-call(bf16[4,128,256]{2,1,0:T(8,128)(2,1)} %get-tuple-element.68.d_ref, bf16[128,1024]{1,0:T(8,128)(2,1)} %copy-done.16, bf16[128,1024]{1,0:T(8,128)(2,1)} %copy-done.15, bf16[128,1024]{1,0:T(8,128)(2,1)} %collective-permute-done.6.rest_14_.rest_2_, bf16[128,1024]{1,0:T(8,128)(2,1)} %copy-done.17), custom_call_target="tpu_custom_call" | custom-call | tf_op jit(solution)/shard_map/hidden_share/pallas_call | solution.py:151
  65.1 2.3 %slice_bitcast_fusion.5 = (bf16[128,1024]{1,0:T(8,128)(2,1)}, bf16[128,1024]{1,0:T(8,128)(2,1)S(1)}, bf16[128,1024]{1,0:T(8,128)(2,1)}, bf16[128,1024]{1,0:T(8,128)(2,1)}) fusion(bf16[4,128,2048]{2,1,0:T(8,128)(2,1)} %hidden_share.1), kind=kLoop, calls=%fused_computation.29 | loop fusion | bytes 2097152 | tf_op jit(solution)/shard_map/squeeze | solution.py:279
  67.4 3.5 %collective-permute-start.23 = (bf16[128,1024]{1,0:T(8,128)(2,1)}, bf16[128,1024]{1,0:T(8,128)(2,1)}, u32[]{:S(2)}, u32[]{:S(2)}) collective-permute-start(bf16[128,1024]{1,0:T(8,128)(2,1)} %get-tuple-element.107), channel_id=1, source_target_pairs={{0,3},{1,0},{2,1},{3,2},{4,7},{5,4},{6,5},{7,6},{8,11},{9,8},{10,9... | collective-permute-start | bytes 786440 | tf_op jit(solution)/shard_map/ppermute | solution.py:132
  71.6 3.8 %collective-permute-start.20 = (bf16[128,256]{1,0:T(8,128)(2,1)S(1)}, bf16[128,256]{1,0:T(8,128)(2,1)S(1)}, u32[]{:S(2)}, u32[]{:S(2)}) collective-permute-start(bf16[128,256]{1,0:T(8,128)(2,1)S(1)} %get-tuple-element.115), channel_id=1, source_target_pairs={{0,3},{1,0},{2,1},{3,2},{4,7},{5,4},{6,5},{7,6},{8,11},{9,8},{10,9... | collective-permute-start | bytes 196616 | tf_op jit(solution)/shard_map/ppermute | solution.py:132
  75.4 6.4 %collective-permute-done.20 = bf16[128,256]{1,0:T(8,128)(2,1)S(1)} collective-permute-done((bf16[128,256]{1,0:T(8,128)(2,1)S(1)}, bf16[128,256]{1,0:T(8,128)(2,1)S(1)}, u32[]{:S(2)}, u32[]{:S(2)}) %collective-permute-start.20) | collective-permute-done | bytes 65568 | tf_op jit(solution)/shard_map/ppermute | solution.py:132
  82.9 4.1 %collective-permute-done.21.rest_2_ = bf16[128,256]{1,0:T(8,128)(2,1)S(1)} collective-permute-done((bf16[128,256]{1,0:T(8,128)(2,1)S(1)}, bf16[128,256]{1,0:T(8,128)(2,1)S(1)}, u32[]{:S(2)}, u32[]{:S(2)}) %collective-permute-start.21) | collective-permute-done | bytes 65568 | tf_op jit(solution)/shard_map/ppermute | solution.py:132
  87.0 2.7 %collective-permute-start.22 = (bf16[128,256]{1,0:T(8,128)(2,1)}, bf16[128,256]{1,0:T(8,128)(2,1)}, u32[]{:S(2)}, u32[]{:S(2)}) collective-permute-start(bf16[128,256]{1,0:T(8,128)(2,1)} %get-tuple-element.113), channel_id=1, source_target_pairs={{0,1},{1,2},{2,3},{3,0},{4,5},{5,6},{6,7},{7,4},{8,9},{9,10},{10,1... | collective-permute-start | bytes 196616 | tf_op jit(solution)/shard_map/ppermute | solution.py:132
  89.7 5.7 %weight_grad_odd.1 = bf16[4,256,1024]{2,1,0:T(8,128)(2,1)} custom-call(s32[2]{0:T(128)} %pad_add_fusion.where_ref, bf16[256,512]{1,0:T(8,128)(2,1)} %get-tuple-element.73.d_ref, bf16[512,8192]{1,0:T(8,128)(2,1)} %h_ref.5), custom_call_target="tpu_custom_call" | custom-call | tf_op jit(solution)/shard_map/weight_grad_odd/pallas_call | solution.py:115
  95.6 1.7 constant_dynamic-update-slice_fusion.3
  97.3 1.7 constant_dynamic-update-slice_fusion.2.rest_6_
  103.9 3.7 %collective-permute-start.28 = (bf16[128,2048]{1,0:T(8,128)(2,1)}, bf16[128,2048]{1,0:T(8,128)(2,1)}, u32[]{:S(2)}, u32[]{:S(2)}) collective-permute-start(bf16[128,2048]{1,0:T(8,128)(2,1)} %pad_maximum_fusion), channel_id=1, source_target_pairs={{0,3},{1,0},{2,1},{3,2},{4,7},{5,4},{6,5},{7,6},{8,11},{9,8},{10,9... | collective-permute-start | bytes 1572872 | tf_op jit(solution)/shard_map/ppermute | solution.py:132
  107.6 6.3 %weight_grad_even.1 = f32[4,256,1024]{2,1,0:T(8,128)} custom-call(s32[2]{0:T(128)} %pad_add_fusion.where_ref, bf16[256,512]{1,0:T(8,128)(2,1)} %get-tuple-element.73.d_ref, bf16[512,8192]{1,0:T(8,128)(2,1)} %h_ref.5), custom_call_target="tpu_custom_call" | custom-call | tf_op jit(solution)/shard_map/weight_grad_even/pallas_call | solution.py:115
  113.9 3.6 %convert_add_fusion = f32[4,256,1024]{2,1,0:T(8,128)S(1)} fusion(f32[4,256,1024]{2,1,0:T(8,128)} %weight_grad_even.1, bf16[4,256,1024]{2,1,0:T(8,128)(2,1)} %collective-permute-done.25), kind=kLoop, calls=%fused_computation | loop fusion | flops 2097152 | bytes 10485760 | tf_op jit(solution)/shard_map/add | solution.py:283
  117.5 2.4 %collective-permute-done.29.rest_2_ = bf16[128,2048]{1,0:T(8,128)(2,1)} collective-permute-done((bf16[128,2048]{1,0:T(8,128)(2,1)}, bf16[128,2048]{1,0:T(8,128)(2,1)}, u32[]{:S(2)}, u32[]{:S(2)}) %collective-permute-start.29) | collective-permute-done | bytes 524320 | tf_op jit(solution)/shard_map/ppermute | solution.py:132
  119.9 10.0 %collective-permute-done.28.rest_1_ = bf16[128,2048]{1,0:T(8,128)(2,1)} collective-permute-done((bf16[128,2048]{1,0:T(8,128)(2,1)}, bf16[128,2048]{1,0:T(8,128)(2,1)}, u32[]{:S(2)}, u32[]{:S(2)}) %collective-permute-start.28) | collective-permute-done | bytes 524320 | tf_op jit(solution)/shard_map/ppermute | solution.py:132
  133.9 10.1 %collective-permute-done.30 = bf16[2,128,1024]{2,1,0:T(8,128)(2,1)S(1)} collective-permute-done((bf16[2,128,1024]{2,1,0:T(8,128)(2,1)S(1)}, bf16[2,128,1024]{2,1,0:T(8,128)(2,1)S(1)}, u32[]{:S(2)}, u32[]{:S(2)}) %collective-permute-start.30) | collective-permute-done | bytes 524320 | tf_op jit(solution)/shard_map/ppermute | solution.py:17
  147.5 4.6 %hidden_grad.2.rest_19_ = bf16[128,8192]{1,0:T(8,128)(2,1)} custom-call(s32[2]{0:T(128)} %pad_add_fusion.where_ref, bf16[128,256]{1,0:T(8,128)(2,1)} %get-tuple-element.112.rest_0_, bf16[128,512]{1,0:T(8,128)(2,1)} %copy-done.21, bf16[128,256]{1,0:T(8,128)(2,1)} %copy-done.23, bf16[128,1024]{1,0:T(8,128)(2,1)} %copy-done.5, bf16[128,1024]{1,0:T(8,128)(2,1)} %copy-done.4, ...), custom_call_target="tpu_custom_call" | custom-call | tf_op jit(solution)/shard_map/hidden_grad/pallas_call | solution.py:201
  152.1 1.8 %fusion.9 = bf16[128,1024]{1,0:T(8,128)(2,1)} fusion(f32[2,128,1024]{2,1,0:T(8,128)} %get-tuple-element.88), kind=kLoop, calls=%fused_computation.26 | loop fusion | bytes 524288 | tf_op jit(solution)/shard_map/convert_element_type | solution.py:246
  155.8 7.1 %hidden_grad.3.rest_3_ = bf16[128,8192]{1,0:T(8,128)(2,1)} custom-call(s32[2]{0:T(128)} %pad_add_fusion.where_ref, bf16[128,256]{1,0:T(8,128)(2,1)} %get-tuple-element.112.rest_0_, bf16[128,512]{1,0:T(8,128)(2,1)} %copy-done.21, bf16[128,256]{1,0:T(8,128)(2,1)} %copy-done.23, bf16[128,1024]{1,0:T(8,128)(2,1)} %copy-done.7, ...), custom_call_target="tpu_custom_call", output_to_operand_aliasing={{}: (20, {})} | custom-call | tf_op jit(solution)/shard_map/hidden_grad/pallas_call | solution.py:201
  168.3 2.3 %collective-permute-done.41 = f32[3,256]{1,0:T(4,128)S(1)} collective-permute-done((f32[3,256]{1,0:T(4,128)S(1)}, f32[3,256]{1,0:T(4,128)S(1)}, u32[]{:S(2)}, u32[]{:S(2)}) %collective-permute-start.41) | collective-permute-done | bytes 3104 | tf_op jit(solution)/shard_map/ppermute | solution.py:17
  170.5 1.6 collective-permute-start.42
  173.0 3.0 %add_shares.1 = bf16[128,8192]{1,0:T(8,128)(2,1)} custom-call(s32[2]{0:T(128)} %pad_add_fusion.where_ref, bf16[128,2048]{1,0:T(8,128)(2,1)} %slice_bitcast_fusion.4.rest_0_, bf16[128,2048]{1,0:T(8,128)(2,1)} %collective-permute-done.28.rest_1_, bf16[128,2048]{1,0:T(8,128)(2,1)} %collective-permute-done.29.rest_2_, ...), custom_call_target="tpu_custom_call", output_to_operand_aliasing={{}: (4, {})} | custom-call | tf_op jit(solution)/shard_map/add_shares/pallas_call | solution.py:230
  (148 shorter events, 36.7 us)
Async XLA Ops:
  1.7 10.2 %collective-permute-start.10 = (bf16[128,1024]{1,0:T(8,128)(2,1)S(1)}, bf16[128,1024]{1,0:T(8,128)(2,1)S(1)}, u32[]{:S(2)}, u32[]{:S(2)}) collective-permute-start(bf16[128,1024]{1,0:T(8,128)(2,1)S(1)} %get-tuple-element.51.rest_1_.rest_4_), channel_id=1, source_target_pairs={{0,16},{4,20},{8,24},{12,28},{16,0},{20,4},{24,8},{28,12},{1,17},{... | collective-permute-start | bytes 786440 | tf_op jit(solution)/shard_map/ppermute | solution.py:17
  4.8 9.2 %collective-permute-start.1 = (bf16[128,1024]{1,0:T(8,128)(2,1)S(1)}, bf16[128,1024]{1,0:T(8,128)(2,1)S(1)}, u32[]{:S(2)}, u32[]{:S(2)}) collective-permute-start(bf16[128,1024]{1,0:T(8,128)(2,1)S(1)} %get-tuple-element.50.rest_0_.rest_3_), channel_id=1, source_target_pairs={{0,8},{4,12},{8,0},{12,4},{16,24},{20,28},{24,16},{28,20},{1,9},{5... | collective-permute-start | bytes 786440 | tf_op jit(solution)/shard_map/ppermute | solution.py:17
  6.3 10.4 %collective-permute-start.3 = (bf16[128,1024]{1,0:T(8,128)(2,1)S(1)}, bf16[128,1024]{1,0:T(8,128)(2,1)S(1)}, u32[]{:S(2)}, u32[]{:S(2)}) collective-permute-start(bf16[128,1024]{1,0:T(8,128)(2,1)S(1)} %get-tuple-element.50.rest_0_.rest_3_), channel_id=1, source_target_pairs={{0,16},{4,20},{8,24},{12,28},{16,0},{20,4},{24,8},{28,12},{1,17},{... | collective-permute-start | bytes 786440 | tf_op jit(solution)/shard_map/ppermute | solution.py:17
  6.8 12.8 %collective-permute-start.8 = (bf16[128,1024]{1,0:T(8,128)(2,1)S(1)}, bf16[128,1024]{1,0:T(8,128)(2,1)S(1)}, u32[]{:S(2)}, u32[]{:S(2)}) collective-permute-start(bf16[128,1024]{1,0:T(8,128)(2,1)S(1)} %get-tuple-element.51.rest_1_.rest_4_), channel_id=1, source_target_pairs={{0,8},{4,12},{8,0},{12,4},{16,24},{20,28},{24,16},{28,20},{1,9},{5... | collective-permute-start | bytes 786440 | tf_op jit(solution)/shard_map/ppermute | solution.py:17
  6.9 16.3 %collective-permute-start = (bf16[128,1024]{1,0:T(8,128)(2,1)S(1)}, bf16[128,1024]{1,0:T(8,128)(2,1)S(1)}, u32[]{:S(2)}, u32[]{:S(2)}) collective-permute-start(bf16[128,1024]{1,0:T(8,128)(2,1)S(1)} %get-tuple-element.50.rest_0_.rest_3_), channel_id=1, source_target_pairs={{0,4},{4,0},{8,12},{12,8},{16,20},{20,16},{24,28},{28,24},{1,5},{5... | collective-permute-start | bytes 786440 | tf_op jit(solution)/shard_map/ppermute | solution.py:17
  11.9 11.3 %collective-permute-start.7 = (bf16[128,1024]{1,0:T(8,128)(2,1)S(1)}, bf16[128,1024]{1,0:T(8,128)(2,1)}, u32[]{:S(2)}, u32[]{:S(2)}) collective-permute-start(bf16[128,1024]{1,0:T(8,128)(2,1)S(1)} %get-tuple-element.51.rest_1_.rest_4_), channel_id=1, source_target_pairs={{0,4},{4,0},{8,12},{12,8},{16,20},{20,16},{24,28},{28,24},{1,5},{5... | collective-permute-start | bytes 786440 | tf_op jit(solution)/shard_map/ppermute | solution.py:17
  14.0 9.8 %collective-permute-start.12 = (bf16[128,1024]{1,0:T(8,128)(2,1)S(1)}, bf16[128,1024]{1,0:T(8,128)(2,1)S(1)}, u32[]{:S(2)}, u32[]{:S(2)}) collective-permute-start(bf16[128,1024]{1,0:T(8,128)(2,1)S(1)} %collective-permute-done.10.rest_9_.rest_12_), channel_id=1, source_target_pairs={{0,8},{4,12},{8,0},{12,4},{16,24},{20,28},{24,16},{28,20},{1,9},{5... | collective-permute-start | bytes 786440 | tf_op jit(solution)/shard_map/ppermute | solution.py:17
  19.6 16.2 %collective-permute-start.14 = (bf16[256,1024]{1,0:T(8,128)(2,1)}, bf16[256,1024]{1,0:T(8,128)(2,1)S(1)}, u32[]{:S(2)}, u32[]{:S(2)}) collective-permute-start(bf16[256,1024]{1,0:T(8,128)(2,1)} %param.5), channel_id=1, source_target_pairs={{0,3},{1,0},{2,1},{3,2},{4,7},{5,4},{6,5},{7,6},{8,11},{9,8},{10,9... | collective-permute-start | bytes 1572872 | tf_op jit(solution)/shard_map/ppermute | solution.py:132
  23.2 21.3 %collective-permute-start.15 = (bf16[256,1024]{1,0:T(8,128)(2,1)}, bf16[256,1024]{1,0:T(8,128)(2,1)S(1)}, u32[]{:S(2)}, u32[]{:S(2)}) collective-permute-start(bf16[256,1024]{1,0:T(8,128)(2,1)} %param.5), channel_id=1, source_target_pairs={{0,1},{1,2},{2,3},{3,0},{4,5},{5,6},{6,7},{7,4},{8,9},{9,10},{10,1... | collective-permute-start | bytes 1572872 | tf_op jit(solution)/shard_map/ppermute | solution.py:132
  25.3 19.1 %collective-permute-start.13 = (bf16[128,1024]{1,0:T(8,128)(2,1)S(1)}, bf16[128,1024]{1,0:T(8,128)(2,1)S(1)}, u32[]{:S(2)}, u32[]{:S(2)}) collective-permute-start(bf16[128,1024]{1,0:T(8,128)(2,1)S(1)} %collective-permute-done.12.rest_13_.rest_1_), channel_id=1, source_target_pairs={{0,4},{4,0},{8,12},{12,8},{16,20},{20,16},{24,28},{28,24},{1,5},{5... | collective-permute-start | bytes 786440 | tf_op jit(solution)/shard_map/ppermute | solution.py:17
  25.7 19.5 %collective-permute-start.6 = (bf16[128,1024]{1,0:T(8,128)(2,1)S(1)}, bf16[128,1024]{1,0:T(8,128)(2,1)}, u32[]{:S(2)}, u32[]{:S(2)}) collective-permute-start(bf16[128,1024]{1,0:T(8,128)(2,1)S(1)} %collective-permute-done.5.rest_12_.rest_0_), channel_id=1, source_target_pairs={{0,4},{4,0},{8,12},{12,8},{16,20},{20,16},{24,28},{28,24},{1,5},{5... | collective-permute-start | bytes 786440 | tf_op jit(solution)/shard_map/ppermute | solution.py:17
  45.3 50.2 %collective-permute-start.18 = (bf16[512,1024]{1,0:T(8,128)(2,1)S(1)}, bf16[512,1024]{1,0:T(8,128)(2,1)}, u32[]{:S(2)}, u32[]{:S(2)}) collective-permute-start(bf16[512,1024]{1,0:T(8,128)(2,1)S(1)} %constant_dynamic-update-slice_fusion.rest_5_), channel_id=1, source_target_pairs={{0,8},{4,12},{8,0},{12,4},{16,24},{20,28},{24,16},{28,20},{1,9},{5... | collective-permute-start | bytes 3145736 | tf_op jit(solution)/shard_map/ppermute | solution.py:17
  46.9 48.6 %collective-permute-start.19 = (bf16[512,1024]{1,0:T(8,128)(2,1)S(1)}, bf16[512,1024]{1,0:T(8,128)(2,1)}, u32[]{:S(2)}, u32[]{:S(2)}) collective-permute-start(bf16[512,1024]{1,0:T(8,128)(2,1)S(1)} %constant_dynamic-update-slice_fusion.rest_5_), channel_id=1, source_target_pairs={{0,16},{4,20},{8,24},{12,28},{16,0},{20,4},{24,8},{28,12},{1,17},{... | collective-permute-start | bytes 3145736 | tf_op jit(solution)/shard_map/ppermute | solution.py:17
  48.2 16.9 %collective-permute-start.16 = (bf16[128,1024]{1,0:T(8,128)(2,1)}, bf16[128,1024]{1,0:T(8,128)(2,1)S(1)}, u32[]{:S(2)}, u32[]{:S(2)}) collective-permute-start(bf16[128,1024]{1,0:T(8,128)(2,1)} %slice.90), channel_id=1, source_target_pairs={{0,3},{1,0},{2,1},{3,2},{4,7},{5,4},{6,5},{7,6},{8,11},{9,8},{10,9... | collective-permute-start | bytes 786440 | tf_op jit(solution)/shard_map/ppermute | solution.py:132
  50.0 15.1 %collective-permute-start.17 = (bf16[128,1024]{1,0:T(8,128)(2,1)S(1)}, bf16[128,1024]{1,0:T(8,128)(2,1)S(1)}, u32[]{:S(2)}, u32[]{:S(2)}) collective-permute-start(bf16[128,1024]{1,0:T(8,128)(2,1)S(1)} %slice.91), channel_id=1, source_target_pairs={{0,1},{1,2},{2,3},{3,0},{4,5},{5,6},{6,7},{7,4},{8,9},{9,10},{10,1... | collective-permute-start | bytes 786440 | tf_op jit(solution)/shard_map/ppermute | solution.py:132
  67.4 28.1 %collective-permute-start.23 = (bf16[128,1024]{1,0:T(8,128)(2,1)}, bf16[128,1024]{1,0:T(8,128)(2,1)}, u32[]{:S(2)}, u32[]{:S(2)}) collective-permute-start(bf16[128,1024]{1,0:T(8,128)(2,1)} %get-tuple-element.107), channel_id=1, source_target_pairs={{0,3},{1,0},{2,1},{3,2},{4,7},{5,4},{6,5},{7,6},{8,11},{9,8},{10,9... | collective-permute-start | bytes 786440 | tf_op jit(solution)/shard_map/ppermute | solution.py:132
  70.9 24.6 %collective-permute-start.24 = (bf16[128,1024]{1,0:T(8,128)(2,1)}, bf16[128,1024]{1,0:T(8,128)(2,1)}, u32[]{:S(2)}, u32[]{:S(2)}) collective-permute-start(bf16[128,1024]{1,0:T(8,128)(2,1)} %get-tuple-element.106), channel_id=1, source_target_pairs={{0,1},{1,2},{2,3},{3,0},{4,5},{5,6},{6,7},{7,4},{8,9},{9,10},{10,1... | collective-permute-start | bytes 786440 | tf_op jit(solution)/shard_map/ppermute | solution.py:132
  71.6 10.3 %collective-permute-start.20 = (bf16[128,256]{1,0:T(8,128)(2,1)S(1)}, bf16[128,256]{1,0:T(8,128)(2,1)S(1)}, u32[]{:S(2)}, u32[]{:S(2)}) collective-permute-start(bf16[128,256]{1,0:T(8,128)(2,1)S(1)} %get-tuple-element.115), channel_id=1, source_target_pairs={{0,3},{1,0},{2,1},{3,2},{4,7},{5,4},{6,5},{7,6},{8,11},{9,8},{10,9... | collective-permute-start | bytes 196616 | tf_op jit(solution)/shard_map/ppermute | solution.py:132
  95.5 18.4 %collective-permute-start.25 = (bf16[4,256,1024]{2,1,0:T(8,128)(2,1)}, bf16[4,256,1024]{2,1,0:T(8,128)(2,1)}, u32[]{:S(2)}, u32[]{:S(2)}) collective-permute-start(bf16[4,256,1024]{2,1,0:T(8,128)(2,1)} %weight_grad_odd.1), channel_id=1, source_target_pairs={{0,4},{4,0},{8,12},{12,8},{16,20},{20,16},{24,28},{28,24},{1,5},{5... | collective-permute-start | bytes 6291464 | tf_op jit(solution)/shard_map/ppermute | solution.py:17
  98.9 18.6 %collective-permute-start.26 = (bf16[256,1024]{1,0:T(8,128)(2,1)}, bf16[256,1024]{1,0:T(8,128)(2,1)}, u32[]{:S(2)}, u32[]{:S(2)}) collective-permute-start(bf16[256,1024]{1,0:T(8,128)(2,1)} %constant_dynamic-update-slice_fusion.2.rest_6_), channel_id=1, source_target_pairs={{0,8},{4,12},{8,0},{12,4},{16,24},{20,28},{24,16},{28,20},{1,9},{5... | collective-permute-start | bytes 1572872 | tf_op jit(solution)/shard_map/ppermute | solution.py:17
  99.5 18.0 %collective-permute-start.27 = (bf16[256,1024]{1,0:T(8,128)(2,1)}, bf16[256,1024]{1,0:T(8,128)(2,1)}, u32[]{:S(2)}, u32[]{:S(2)}) collective-permute-start(bf16[256,1024]{1,0:T(8,128)(2,1)} %constant_dynamic-update-slice_fusion.2.rest_6_), channel_id=1, source_target_pairs={{0,16},{4,20},{8,24},{12,28},{16,0},{20,4},{24,8},{28,12},{1,17},{... | collective-permute-start | bytes 1572872 | tf_op jit(solution)/shard_map/ppermute | solution.py:17
  102.9 17.0 %collective-permute-start.29 = (bf16[128,2048]{1,0:T(8,128)(2,1)}, bf16[128,2048]{1,0:T(8,128)(2,1)}, u32[]{:S(2)}, u32[]{:S(2)}) collective-permute-start(bf16[128,2048]{1,0:T(8,128)(2,1)} %pad_maximum_fusion.1), channel_id=1, source_target_pairs={{0,1},{1,2},{2,3},{3,0},{4,5},{5,6},{6,7},{7,4},{8,9},{9,10},{10,1... | collective-permute-start | bytes 1572872 | tf_op jit(solution)/shard_map/ppermute | solution.py:132
  103.9 26.0 %collective-permute-start.28 = (bf16[128,2048]{1,0:T(8,128)(2,1)}, bf16[128,2048]{1,0:T(8,128)(2,1)}, u32[]{:S(2)}, u32[]{:S(2)}) collective-permute-start(bf16[128,2048]{1,0:T(8,128)(2,1)} %pad_maximum_fusion), channel_id=1, source_target_pairs={{0,3},{1,0},{2,1},{3,2},{4,7},{5,4},{6,5},{7,6},{8,11},{9,8},{10,9... | collective-permute-start | bytes 1572872 | tf_op jit(solution)/shard_map/ppermute | solution.py:132
  113.9 19.1 %collective-permute-start.32 = (bf16[512,1024]{1,0:T(8,128)(2,1)S(1)}, bf16[512,1024]{1,0:T(8,128)(2,1)S(1)}, u32[]{:S(2)}, u32[]{:S(2)}) collective-permute-start(bf16[512,1024]{1,0:T(8,128)(2,1)S(1)} %constant_dynamic-update-slice_fusion.rest_5_), channel_id=1, source_target_pairs={{0,4},{4,0},{8,12},{12,8},{16,20},{20,16},{24,28},{28,24},{1,5},{5... | collective-permute-start | bytes 3145736 | tf_op jit(solution)/shard_map/ppermute | solution.py:17
  130.2 13.7 %collective-permute-start.30 = (bf16[2,128,1024]{2,1,0:T(8,128)(2,1)S(1)}, bf16[2,128,1024]{2,1,0:T(8,128)(2,1)S(1)}, u32[]{:S(2)}, u32[]{:S(2)}) collective-permute-start(bf16[2,128,1024]{2,1,0:T(8,128)(2,1)S(1)} %slice_bitcast_fusion.3), channel_id=1, source_target_pairs={{0,8},{4,12},{8,0},{12,4},{16,24},{20,28},{24,16},{28,20},{1,9},{5... | collective-permute-start | bytes 1572872 | tf_op jit(solution)/shard_map/ppermute | solution.py:17
  131.8 13.5 %collective-permute-start.31 = (bf16[2,128,1024]{2,1,0:T(8,128)(2,1)S(1)}, bf16[2,128,1024]{2,1,0:T(8,128)(2,1)S(1)}, u32[]{:S(2)}, u32[]{:S(2)}) collective-permute-start(bf16[2,128,1024]{2,1,0:T(8,128)(2,1)S(1)} %slice_bitcast_fusion.2), channel_id=1, source_target_pairs={{0,16},{4,20},{8,24},{12,28},{16,0},{20,4},{24,8},{28,12},{1,17},{... | collective-permute-start | bytes 1572872 | tf_op jit(solution)/shard_map/ppermute | solution.py:17
  132.4 22.9 %collective-permute-start.36 = (bf16[512,1024]{1,0:T(8,128)(2,1)}, bf16[512,1024]{1,0:T(8,128)(2,1)}, u32[]{:S(2)}, u32[]{:S(2)}) collective-permute-start(bf16[512,1024]{1,0:T(8,128)(2,1)} %collective-permute-done.18.rest_5_), channel_id=1, source_target_pairs={{0,4},{4,0},{8,12},{12,8},{16,20},{20,16},{24,28},{28,24},{1,5},{5... | collective-permute-start | bytes 3145736 | tf_op jit(solution)/shard_map/ppermute | solution.py:17
  132.4 23.4 %collective-permute-start.38 = (bf16[512,1024]{1,0:T(8,128)(2,1)}, bf16[512,1024]{1,0:T(8,128)(2,1)}, u32[]{:S(2)}, u32[]{:S(2)}) collective-permute-start(bf16[512,1024]{1,0:T(8,128)(2,1)} %collective-permute-done.19.rest_13_), channel_id=1, source_target_pairs={{0,4},{4,0},{8,12},{12,8},{16,20},{20,16},{24,28},{28,24},{1,5},{5... | collective-permute-start | bytes 3145736 | tf_op jit(solution)/shard_map/ppermute | solution.py:17
  132.9 13.7 %collective-permute-start.33 = (bf16[256,1024]{1,0:T(8,128)(2,1)}, bf16[256,1024]{1,0:T(8,128)(2,1)S(1)}, u32[]{:S(2)}, u32[]{:S(2)}) collective-permute-start(bf16[256,1024]{1,0:T(8,128)(2,1)} %constant_dynamic-update-slice_fusion.2.rest_6_), channel_id=1, source_target_pairs={{0,4},{4,0},{8,12},{12,8},{16,20},{20,16},{24,28},{28,24},{1,5},{5... | collective-permute-start | bytes 1572872 | tf_op jit(solution)/shard_map/ppermute | solution.py:17
  144.0 11.8 %collective-permute-start.37 = (bf16[256,1024]{1,0:T(8,128)(2,1)}, bf16[256,1024]{1,0:T(8,128)(2,1)}, u32[]{:S(2)}, u32[]{:S(2)}) collective-permute-start(bf16[256,1024]{1,0:T(8,128)(2,1)} %collective-permute-done.26.rest_6_), channel_id=1, source_target_pairs={{0,4},{4,0},{8,12},{12,8},{16,20},{20,16},{24,28},{28,24},{1,5},{5... | collective-permute-start | bytes 1572872 | tf_op jit(solution)/shard_map/ppermute | solution.py:17
  145.3 10.5 %collective-permute-start.39 = (bf16[256,1024]{1,0:T(8,128)(2,1)}, bf16[256,1024]{1,0:T(8,128)(2,1)}, u32[]{:S(2)}, u32[]{:S(2)}) collective-permute-start(bf16[256,1024]{1,0:T(8,128)(2,1)} %collective-permute-done.27.rest_14_), channel_id=1, source_target_pairs={{0,4},{4,0},{8,12},{12,8},{16,20},{20,16},{24,28},{28,24},{1,5},{5... | collective-permute-start | bytes 1572872 | tf_op jit(solution)/shard_map/ppermute | solution.py:17
  153.8 9.1 %collective-permute-start.35 = (bf16[128,1024]{1,0:T(8,128)(2,1)}, bf16[128,1024]{1,0:T(8,128)(2,1)S(1)}, u32[]{:S(2)}, u32[]{:S(2)}) collective-permute-start(bf16[128,1024]{1,0:T(8,128)(2,1)} %fusion.9), channel_id=1, source_target_pairs={{0,8},{4,12},{8,0},{12,4},{16,24},{20,28},{24,16},{28,20},{1,9},{5... | collective-permute-start | bytes 786440 | tf_op jit(solution)/shard_map/ppermute | solution.py:17
  (37 other events, 580.9 us)

commit v5 on v4

--- a/solution.py
+++ b/solution.py
@@ -254,10 +254,15 @@
     where = jnp.stack([lax.axis_index("dp"), lax.axis_index("tensor")]).astype(jnp.int32)
     ahead = shift(weight, 1, n_tensor)
     behind = shift(weight, -1, n_tensor)
-    parts = [add_core(have, n_dp) for have in gather_links(weight, n_dp)]
-    parts, ahead, behind = lax.optimization_barrier((parts, ahead, behind))
+    parts = gather_links(weight, n_dp)
+    last = n_dp - 2
+    final = [have[last] for have in parts]
+    parts = [add_core({r: x for r, x in have.items() if r != last}, n_dp) for have in parts]
+    final, ahead, behind = lax.optimization_barrier((final, ahead, behind))
+    for have, x in zip(parts, final):
+        have.update(add_core({last: x}, n_dp))
     pair = {0: jnp.concatenate([ahead, behind], 0)}
-    low, high = shift(ahead[:half], 1, n_tensor), shift(behind[half:], -1, n_tensor)
+    across = shift(weight, 2, n_tensor)
     bits = [1 << i for i in range(1, n_dp.bit_length() - 1)]
     pair.update({bit: swap(pair[0], bit, n_dp) for bit in bits})
     keys_values, d_slots, d_t = project(hidden, parts, qk_scale, cotangent, where, n_tensor)
@@ -265,23 +270,23 @@
     linked = [r for bit in bits for r in (bit, bit ^ 1)]
     far = [r for r in range(n_dp) if r not in near and r not in linked]
     share = hidden_share(d_slots, parts, far)
-    d_t, share, low, high = lax.optimization_barrier((d_t, share, low, high))
+    d_rest = [shift(d_slots[k], k, n_tensor) for k in range(1, n_tensor)]
+    d_t, share, across, d_rest = lax.optimization_barrier((d_t, share, across, d_rest))
     cut = share.shape[2] // 2
     via_ahead = shift(share[2, :, :cut], 1, n_tensor)
     via_behind = shift(share[2, :, cut:], -1, n_tensor)
-    mid = {0: jnp.concatenate([low, high], 0)}
+    mid = {0: across}
     mid.update({bit: swap(mid[0], bit, n_dp) for bit in bits})
     sent = weight_grad(d_t, hidden, where, n_dp, 1, BF16)
-    d_rest = [shift(d_slots[k], k, n_tensor) for k in range(1, n_tensor)]
-    due = (d_t, sent, pair, d_rest, via_ahead, via_behind)
-    d_t, sent, pair, d_rest, via_ahead, via_behind = lax.optimization_barrier(due)
+    due = (d_t, sent, pair, via_ahead, via_behind)
+    d_t, sent, pair, via_ahead, via_behind = lax.optimization_barrier(due)
     to_ahead = jnp.concatenate([share[1, :, :cut] + via_ahead, share[1, :, cut:]], 1)
     to_behind = jnp.concatenate([share[-1, :, :cut], share[-1, :, cut:] + via_behind], 1)
     from_ahead, from_behind = shift(to_ahead, 1, n_tensor), shift(to_behind, -1, n_tensor)
     pair = add_core(pair, n_dp)
     keep = weight_grad(d_t, hidden, where, n_dp, 0, F32)
     total = keep + swap(sent, 1, n_dp).astype(F32)
-    total, mid, from_ahead, from_behind = lax.optimization_barrier((total, mid, from_ahead, from_behind))
+    total, mid = lax.optimization_barrier((total, mid))
     mid = add_core(mid, n_dp)
     d_pair = jnp.concatenate([d_rest[0], d_rest[-1]], 1)
     d_all = (d_slots[0], d_pair, d_rest[1], parts, pair, mid, where)
@@ -293,7 +298,8 @@
     left = [list(range(count))[::-1], list(range(count))[::-1]]
     for step in range(count):
         if step == count - 1:
-            sides, input_grad = lax.optimization_barrier((sides, input_grad))
+            due = (sides, input_grad, from_ahead, from_behind)
+            sides, input_grad, from_ahead, from_behind = lax.optimization_barrier(due)
         for at in range(2):
             b = orders[at][step]
             axis = left[at].index(b)

time: 178 us -> 150 us (0.84)
  waiting for transfers between devices: 67.8 us -> 46.2 us
  local copies, waits for them, and re-layouts: 14.2 us -> 8.58 us
  starting transfers between devices: 40.9 us -> 38.7 us
    ppermute x11 -> x10, waiting for transfers between devices: 41 us -> 24.7 us  [shift(): lax.ppermute(x, 'tensor', [(i, (i - by) % n_tensor) for i in range(n_tens...]
    ppermute x32, waiting for transfers between devices: 26.8 us -> 21.5 us  [swap(): return lax.ppermute(x, 'dp', [(i, i ^ bit) for i in range(n_dp)])]
    ppermute x11 -> x10, starting transfers between devices: 20.6 us -> 16.3 us  [shift(): lax.ppermute(x, 'tensor', [(i, (i - by) % n_tensor) for i in range(n_tens...]
    unnamed x56 -> x53, local copies, waits for them, and re-layouts: 3.36 us -> 0.18 us
    ppermute x32, starting transfers between devices: 20.2 us -> 22.5 us  [swap(): return lax.ppermute(x, 'dp', [(i, i ^ bit) for i in range(n_dp)])]
  transfers between devices with their start and end apart: 43 -> 42, of which waited for: 20 -> 14; matrix products, arithmetic and copies ran while one was open for 12% -> 12% of each run, Pallas kernels for 23% -> 28%
where the time goes in v5:
time: 150 us; the launch traced here: 149 us
  waiting for transfers between devices  46.2 us (31%)
  Pallas kernels  41.1 us (27%)
  starting transfers between devices  38.7 us (26%)
  other arithmetic  13.3 us (9%)
  local copies, waits for them, and re-layouts  8.58 us (6%)
    ppermute x10, waiting for transfers between devices, shift(): lax.ppermute(x, 'tensor', [(i, (i - by) % n_tensor) for i in range(n_tens...  24.7 us
    ppermute x32, starting transfers between devices, swap(): return lax.ppermute(x, 'dp', [(i, i ^ bit) for i in range(n_dp)])  22.5 us
    ppermute x32, waiting for transfers between devices, swap(): return lax.ppermute(x, 'dp', [(i, i ^ bit) for i in range(n_dp)])  21.5 us
    ppermute x10, starting transfers between devices, shift(): lax.ppermute(x, 'tensor', [(i, (i - by) % n_tensor) for i in range(n_tens...  16.3 us
    pallas_call x2, Pallas kernels, weight_grad(): pl.pallas_call(body, grid_spec=pltpu.PrefetchScalarGridSpec(num_scalar_pr...  12.2 us
    pallas_call x2, Pallas kernels, hidden_grad(): pl.pallas_call(body, grid_spec=pltpu.PrefetchScalarGridSpec(num_scalar_pr...  11.7 us
    pallas_call x1, Pallas kernels, project(): pl.pallas_call(body, grid_spec=pltpu.PrefetchScalarGridSpec(num_scalar_pr...  11 us
    add x1, other arithmetic, local(): total = keep + swap(sent, 1, n_dp).astype(F32)  3.55 us
  transfers between devices with their start and end apart: 42, of which 14 were waited for; matrix products, arithmetic and copies ran while one was open for 12% of the time, Pallas kernels for 28%

profile of v5, /device:TPU:0, one launch (start us, length us, event | category | flops | bytes accessed | tf_op | source)
XLA Modules:
  0.0 148.9 jit_solution(6257959103245092149)
XLA Ops:
  1.8 3.0 %collective-permute-start.2 = (bf16[128,1024]{1,0:T(8,128)(2,1)S(1)}, bf16[128,1024]{1,0:T(8,128)(2,1)S(1)}, u32[]{:S(2)}, u32[]{:S(2)}) collective-permute-start(bf16[128,1024]{1,0:T(8,128)(2,1)S(1)} %get-tuple-element.81.rest_0_.rest_3_), channel_id=1, source_target_pairs={{0,8},{4,12},{8,0},{12,4},{16,24},{20,28},{24,16},{28,20},{1,9},{5... | collective-permute-start | bytes 786440 | tf_op jit(solution)/shard_map/ppermute | solution.py:17
  4.8 1.5 %collective-permute-start.7 = (bf16[128,1024]{1,0:T(8,128)(2,1)S(1)}, bf16[128,1024]{1,0:T(8,128)(2,1)S(1)}, u32[]{:S(2)}, u32[]{:S(2)}) collective-permute-start(bf16[128,1024]{1,0:T(8,128)(2,1)S(1)} %get-tuple-element.80.rest_1_.rest_4_), channel_id=1, source_target_pairs={{0,16},{4,20},{8,24},{12,28},{16,0},{20,4},{24,8},{28,12},{1,17},{... | collective-permute-start | bytes 786440 | tf_op jit(solution)/shard_map/ppermute | solution.py:17
  6.9 4.1 %collective-permute-start.12 = (bf16[256,1024]{1,0:T(8,128)(2,1)}, bf16[256,1024]{1,0:T(8,128)(2,1)S(1)}, u32[]{:S(2)}, u32[]{:S(2)}) collective-permute-start(bf16[256,1024]{1,0:T(8,128)(2,1)} %param.5), channel_id=1, source_target_pairs={{0,3},{1,0},{2,1},{3,2},{4,7},{5,4},{6,5},{7,6},{8,11},{9,8},{10,9... | collective-permute-start | bytes 1572872 | tf_op jit(solution)/shard_map/ppermute | solution.py:132
  12.0 2.1 %collective-permute-start.13 = (bf16[256,1024]{1,0:T(8,128)(2,1)}, bf16[256,1024]{1,0:T(8,128)(2,1)S(1)}, u32[]{:S(2)}, u32[]{:S(2)}) collective-permute-start(bf16[256,1024]{1,0:T(8,128)(2,1)} %param.5), channel_id=1, source_target_pairs={{0,1},{1,2},{2,3},{3,0},{4,5},{5,6},{6,7},{7,4},{8,9},{9,10},{10,1... | collective-permute-start | bytes 1572872 | tf_op jit(solution)/shard_map/ppermute | solution.py:132
  14.1 2.6 %collective-permute-done.3.rest_5_.rest_4_ = bf16[128,1024]{1,0:T(8,128)(2,1)S(1)} collective-permute-done((bf16[128,1024]{1,0:T(8,128)(2,1)S(1)}, bf16[128,1024]{1,0:T(8,128)(2,1)S(1)}, u32[]{:S(2)}, u32[]{:S(2)}) %collective-permute-start.3) | collective-permute-done | bytes 262176 | tf_op jit(solution)/shard_map/ppermute | solution.py:17
  16.7 1.8 %collective-permute-start.10 = (bf16[128,1024]{1,0:T(8,128)(2,1)S(1)}, bf16[128,1024]{1,0:T(8,128)(2,1)}, u32[]{:S(2)}, u32[]{:S(2)}) collective-permute-start(bf16[128,1024]{1,0:T(8,128)(2,1)S(1)} %collective-permute-done.2.rest_4_.rest_3_), channel_id=1, source_target_pairs={{0,16},{4,20},{8,24},{12,28},{16,0},{20,4},{24,8},{28,12},{1,17},{... | collective-permute-start | bytes 786440 | tf_op jit(solution)/shard_map/ppermute | solution.py:17
  20.0 4.3 %collective-permute-done.10.rest_12_.rest_0_ = bf16[128,1024]{1,0:T(8,128)(2,1)} collective-permute-done((bf16[128,1024]{1,0:T(8,128)(2,1)S(1)}, bf16[128,1024]{1,0:T(8,128)(2,1)}, u32[]{:S(2)}, u32[]{:S(2)}) %collective-permute-start.10) | collective-permute-done | bytes 262176 | tf_op jit(solution)/shard_map/ppermute | solution.py:17
  26.1 7.3 %collective-permute-done.13 = bf16[256,1024]{1,0:T(8,128)(2,1)S(1)} collective-permute-done((bf16[256,1024]{1,0:T(8,128)(2,1)}, bf16[256,1024]{1,0:T(8,128)(2,1)S(1)}, u32[]{:S(2)}, u32[]{:S(2)}) %collective-permute-start.13) | collective-permute-done | bytes 524320 | tf_op jit(solution)/shard_map/ppermute | solution.py:132
  33.5 2.6 %collective-permute-start.16 = (bf16[256,1024]{1,0:T(8,128)(2,1)S(1)}, bf16[256,1024]{1,0:T(8,128)(2,1)}, u32[]{:S(2)}, u32[]{:S(2)}) collective-permute-start(bf16[256,1024]{1,0:T(8,128)(2,1)S(1)} %copy-done.1), channel_id=1, source_target_pairs={{0,2},{1,3},{2,0},{3,1},{4,6},{5,7},{6,4},{7,5},{8,10},{9,11},{10,... | collective-permute-start | bytes 1572872 | tf_op jit(solution)/shard_map/ppermute | solution.py:132
  36.6 1.6 %collective-permute-start.20 = (bf16[512,1024]{1,0:T(8,128)(2,1)S(1)}, bf16[512,1024]{1,0:T(8,128)(2,1)}, u32[]{:S(2)}, u32[]{:S(2)}) collective-permute-start(bf16[512,1024]{1,0:T(8,128)(2,1)S(1)} %constant_dynamic-update-slice_fusion.rest_5_), channel_id=1, source_target_pairs={{0,8},{4,12},{8,0},{12,4},{16,24},{20,28},{24,16},{28,20},{1,9},{5... | collective-permute-start | bytes 3145736 | tf_op jit(solution)/shard_map/ppermute | solution.py:17
  38.2 1.6 %collective-permute-start.21 = (bf16[512,1024]{1,0:T(8,128)(2,1)S(1)}, bf16[512,1024]{1,0:T(8,128)(2,1)}, u32[]{:S(2)}, u32[]{:S(2)}) collective-permute-start(bf16[512,1024]{1,0:T(8,128)(2,1)S(1)} %constant_dynamic-update-slice_fusion.rest_5_), channel_id=1, source_target_pairs={{0,16},{4,20},{8,24},{12,28},{16,0},{20,4},{24,8},{28,12},{1,17},{... | collective-permute-start | bytes 3145736 | tf_op jit(solution)/shard_map/ppermute | solution.py:17
  40.5 11.0 %project.1 = (bf16[512,256]{1,0:T(8,128)(2,1)}, bf16[4,128,256]{2,1,0:T(8,128)(2,1)}, bf16[256,512]{1,0:T(8,128)(2,1)}) custom-call(s32[2]{0:T(128)} %pad_add_fusion.where_ref, bf16[512,8192]{1,0:T(8,128)(2,1)} %h_ref.5, f32[1,128]{1,0:T(1,128)} %s_ref.1, bf16[512,256]{1,0:T(8,128)(2,1)} %c_ref.1, bf16[128,1024]{1,0:T(8,128)(2,1)} %copy-done.6, ...), custom_call_target="tpu_custom_call" | custom-call | tf_op jit(solution)/shard_map/project/pallas_call | solution.py:81
  51.5 1.6 %slice_bitcast_fusion.9 = (bf16[128,256]{1,0:T(8,128)(2,1)}, bf16[128,256]{1,0:T(8,128)(2,1)S(1)}, bf16[128,256]{1,0:T(8,128)(2,1)S(1)}, bf16[128,256]{1,0:T(8,128)(2,1)S(1)}) fusion(bf16[4,128,256]{2,1,0:T(8,128)(2,1)} %get-tuple-element.39.d_ref), kind=kLoop, calls=%fused_computation.33 | loop fusion | bytes 524288 | tf_op jit(solution)/shard_map/squeeze | solution.py:292
  56.0 6.0 %collective-permute-done.16.rest_6_ = bf16[256,1024]{1,0:T(8,128)(2,1)} collective-permute-done((bf16[256,1024]{1,0:T(8,128)(2,1)S(1)}, bf16[256,1024]{1,0:T(8,128)(2,1)}, u32[]{:S(2)}, u32[]{:S(2)}) %collective-permute-start.16) | collective-permute-done | bytes 524320 | tf_op jit(solution)/shard_map/ppermute | solution.py:132
  63.4 3.2 %hidden_share.1 = bf16[4,128,2048]{2,1,0:T(8,128)(2,1)} custom-call(bf16[4,128,256]{2,1,0:T(8,128)(2,1)} %get-tuple-element.39.d_ref, bf16[128,1024]{1,0:T(8,128)(2,1)} %collective-permute-done.10.rest_12_.rest_0_, bf16[128,1024]{1,0:T(8,128)(2,1)} %collective-permute-done.11.rest_13_.rest_1_, bf16[128,1024]{1,0:T(8,128)(2,1)} %collective-permute-done.14.rest_14_.rest_2_, ...), custom_call_target="tpu_custom_call" | custom-call | tf_op jit(solution)/shard_map/hidden_share/pallas_call | solution.py:151
  66.6 2.0 %collective-permute-done.19 = bf16[128,256]{1,0:T(8,128)(2,1)S(1)} collective-permute-done((bf16[128,256]{1,0:T(8,128)(2,1)S(1)}, bf16[128,256]{1,0:T(8,128)(2,1)S(1)}, u32[]{:S(2)}, u32[]{:S(2)}) %collective-permute-start.19) | collective-permute-done | bytes 65568 | tf_op jit(solution)/shard_map/ppermute | solution.py:132
  68.6 2.2 %slice_bitcast_fusion.5 = (bf16[128,1024]{1,0:T(8,128)(2,1)}, bf16[128,1024]{1,0:T(8,128)(2,1)}, bf16[128,1024]{1,0:T(8,128)(2,1)}, bf16[128,1024]{1,0:T(8,128)(2,1)}) fusion(bf16[4,128,2048]{2,1,0:T(8,128)(2,1)} %hidden_share.1), kind=kLoop, calls=%fused_computation.29 | loop fusion | bytes 2097152 | tf_op jit(solution)/shard_map/squeeze | solution.py:284
  70.8 2.0 %collective-permute-start.22 = (bf16[128,1024]{1,0:T(8,128)(2,1)}, bf16[128,1024]{1,0:T(8,128)(2,1)S(1)}, u32[]{:S(2)}, u32[]{:S(2)}) collective-permute-start(bf16[128,1024]{1,0:T(8,128)(2,1)} %get-tuple-element.77), channel_id=1, source_target_pairs={{0,3},{1,0},{2,1},{3,2},{4,7},{5,4},{6,5},{7,6},{8,11},{9,8},{10,9... | collective-permute-start | bytes 786440 | tf_op jit(solution)/shard_map/ppermute | solution.py:132
  72.8 5.9 %weight_grad_odd.1 = bf16[4,256,1024]{2,1,0:T(8,128)(2,1)} custom-call(s32[2]{0:T(128)} %pad_add_fusion.where_ref, bf16[256,512]{1,0:T(8,128)(2,1)} %get-tuple-element.44.d_ref, bf16[512,8192]{1,0:T(8,128)(2,1)} %h_ref.5), custom_call_target="tpu_custom_call" | custom-call | tf_op jit(solution)/shard_map/weight_grad_odd/pallas_call | solution.py:115
  79.8 5.8 %collective-permute-done.23 = bf16[128,1024]{1,0:T(8,128)(2,1)} collective-permute-done((bf16[128,1024]{1,0:T(8,128)(2,1)}, bf16[128,1024]{1,0:T(8,128)(2,1)}, u32[]{:S(2)}, u32[]{:S(2)}) %collective-permute-start.23) | collective-permute-done | bytes 262176 | tf_op jit(solution)/shard_map/ppermute | solution.py:132
  85.7 1.6 %collective-permute-start.25 = (bf16[256,1024]{1,0:T(8,128)(2,1)}, bf16[256,1024]{1,0:T(8,128)(2,1)}, u32[]{:S(2)}, u32[]{:S(2)}) collective-permute-start(bf16[256,1024]{1,0:T(8,128)(2,1)} %collective-permute-done.16.rest_6_), channel_id=1, source_target_pairs={{0,8},{4,12},{8,0},{12,4},{16,24},{20,28},{24,16},{28,20},{1,9},{5... | collective-permute-start | bytes 1572872 | tf_op jit(solution)/shard_map/ppermute | solution.py:17
  87.2 1.5 %collective-permute-start.26 = (bf16[256,1024]{1,0:T(8,128)(2,1)}, bf16[256,1024]{1,0:T(8,128)(2,1)}, u32[]{:S(2)}, u32[]{:S(2)}) collective-permute-start(bf16[256,1024]{1,0:T(8,128)(2,1)} %collective-permute-done.16.rest_6_), channel_id=1, source_target_pairs={{0,16},{4,20},{8,24},{12,28},{16,0},{20,4},{24,8},{28,12},{1,17},{... | collective-permute-start | bytes 1572872 | tf_op jit(solution)/shard_map/ppermute | solution.py:17
  89.8 1.8 %pad_maximum_fusion.1 = bf16[128,2048]{1,0:T(8,128)(2,1)} fusion(bf16[128,1024]{1,0:T(8,128)(2,1)S(1)} %get-tuple-element.78, bf16[128,1024]{1,0:T(8,128)(2,1)} %get-tuple-element.74), kind=kLoop, calls=%fused_computation.21 | loop fusion | flops 1048576 | bytes 1048576 | tf_op jit(solution)/shard_map/concatenate | solution.py:284
  92.0 6.3 %weight_grad_even.1 = f32[4,256,1024]{2,1,0:T(8,128)} custom-call(s32[2]{0:T(128)} %pad_add_fusion.where_ref, bf16[256,512]{1,0:T(8,128)(2,1)} %get-tuple-element.44.d_ref, bf16[512,8192]{1,0:T(8,128)(2,1)} %h_ref.5), custom_call_target="tpu_custom_call" | custom-call | tf_op jit(solution)/shard_map/weight_grad_even/pallas_call | solution.py:115
  98.2 3.6 %convert_add_fusion = f32[4,256,1024]{2,1,0:T(8,128)S(1)} fusion(f32[4,256,1024]{2,1,0:T(8,128)} %weight_grad_even.1, bf16[4,256,1024]{2,1,0:T(8,128)(2,1)} %collective-permute-done.24), kind=kLoop, calls=%fused_computation | loop fusion | flops 2097152 | bytes 10485760 | tf_op jit(solution)/shard_map/add | solution.py:288
  105.0 2.5 %collective-permute-done.32.rest_2_ = bf16[128,2048]{1,0:T(8,128)(2,1)} collective-permute-done((bf16[128,2048]{1,0:T(8,128)(2,1)}, bf16[128,2048]{1,0:T(8,128)(2,1)}, u32[]{:S(2)}, u32[]{:S(2)}) %collective-permute-start.32) | collective-permute-done | bytes 524320 | tf_op jit(solution)/shard_map/ppermute | solution.py:132
  108.9 7.8 %collective-permute-done.27 = bf16[2,128,1024]{2,1,0:T(8,128)(2,1)S(1)} collective-permute-done((bf16[2,128,1024]{2,1,0:T(8,128)(2,1)S(1)}, bf16[2,128,1024]{2,1,0:T(8,128)(2,1)S(1)}, u32[]{:S(2)}, u32[]{:S(2)}) %collective-permute-start.27) | collective-permute-done | bytes 524320 | tf_op jit(solution)/shard_map/ppermute | solution.py:17
  118.5 4.6 %hidden_grad.2.rest_19_ = bf16[128,8192]{1,0:T(8,128)(2,1)} custom-call(s32[2]{0:T(128)} %pad_add_fusion.where_ref, bf16[128,256]{1,0:T(8,128)(2,1)} %get-tuple-element.82.rest_0_, bf16[128,512]{1,0:T(8,128)(2,1)} %copy-done.19, bf16[128,256]{1,0:T(8,128)(2,1)} %copy-done.21, bf16[128,1024]{1,0:T(8,128)(2,1)} %copy-done.6, bf16[128,1024]{1,0:T(8,128)(2,1)} %copy-done.5, ...), custom_call_target="tpu_custom_call" | custom-call | tf_op jit(solution)/shard_map/hidden_grad/pallas_call | solution.py:201
  123.1 1.8 %fusion.9 = bf16[128,1024]{1,0:T(8,128)(2,1)} fusion(f32[2,128,1024]{2,1,0:T(8,128)} %get-tuple-element.58), kind=kLoop, calls=%fused_computation.26 | loop fusion | bytes 524288 | tf_op jit(solution)/shard_map/convert_element_type | solution.py:246
  128.2 7.1 %hidden_grad.3.rest_3_ = bf16[128,8192]{1,0:T(8,128)(2,1)} custom-call(s32[2]{0:T(128)} %pad_add_fusion.where_ref, bf16[128,256]{1,0:T(8,128)(2,1)} %get-tuple-element.82.rest_0_, bf16[128,512]{1,0:T(8,128)(2,1)} %copy-done.19, bf16[128,256]{1,0:T(8,128)(2,1)} %copy-done.21, bf16[128,1024]{1,0:T(8,128)(2,1)} %copy-done.7, ...), custom_call_target="tpu_custom_call", output_to_operand_aliasing={{}: (20, {})} | custom-call | tf_op jit(solution)/shard_map/hidden_grad/pallas_call | solution.py:201
  140.0 2.9 %collective-permute-done.40 = f32[3,256]{1,0:T(4,128)S(1)} collective-permute-done((f32[3,256]{1,0:T(4,128)S(1)}, f32[3,256]{1,0:T(4,128)S(1)}, u32[]{:S(2)}, u32[]{:S(2)}) %collective-permute-start.40) | collective-permute-done | bytes 3104 | tf_op jit(solution)/shard_map/ppermute | solution.py:17
  144.7 3.0 %add_shares.1 = bf16[128,8192]{1,0:T(8,128)(2,1)} custom-call(s32[2]{0:T(128)} %pad_add_fusion.where_ref, bf16[128,2048]{1,0:T(8,128)(2,1)} %slice_bitcast_fusion.4.rest_0_, bf16[128,2048]{1,0:T(8,128)(2,1)} %collective-permute-done.31.rest_1_, bf16[128,2048]{1,0:T(8,128)(2,1)} %collective-permute-done.32.rest_2_, ...), custom_call_target="tpu_custom_call", output_to_operand_aliasing={{}: (4, {})} | custom-call | tf_op jit(solution)/shard_map/add_shares/pallas_call | solution.py:230
  (140 shorter events, 31.4 us)
Async XLA Ops:
  1.8 10.2 %collective-permute-start.2 = (bf16[128,1024]{1,0:T(8,128)(2,1)S(1)}, bf16[128,1024]{1,0:T(8,128)(2,1)S(1)}, u32[]{:S(2)}, u32[]{:S(2)}) collective-permute-start(bf16[128,1024]{1,0:T(8,128)(2,1)S(1)} %get-tuple-element.81.rest_0_.rest_3_), channel_id=1, source_target_pairs={{0,8},{4,12},{8,0},{12,4},{16,24},{20,28},{24,16},{28,20},{1,9},{5... | collective-permute-start | bytes 786440 | tf_op jit(solution)/shard_map/ppermute | solution.py:17
  4.8 9.3 %collective-permute-start.7 = (bf16[128,1024]{1,0:T(8,128)(2,1)S(1)}, bf16[128,1024]{1,0:T(8,128)(2,1)S(1)}, u32[]{:S(2)}, u32[]{:S(2)}) collective-permute-start(bf16[128,1024]{1,0:T(8,128)(2,1)S(1)} %get-tuple-element.80.rest_1_.rest_4_), channel_id=1, source_target_pairs={{0,16},{4,20},{8,24},{12,28},{16,0},{20,4},{24,8},{28,12},{1,17},{... | collective-permute-start | bytes 786440 | tf_op jit(solution)/shard_map/ppermute | solution.py:17
  6.3 10.4 %collective-permute-start.3 = (bf16[128,1024]{1,0:T(8,128)(2,1)S(1)}, bf16[128,1024]{1,0:T(8,128)(2,1)S(1)}, u32[]{:S(2)}, u32[]{:S(2)}) collective-permute-start(bf16[128,1024]{1,0:T(8,128)(2,1)S(1)} %get-tuple-element.80.rest_1_.rest_4_), channel_id=1, source_target_pairs={{0,8},{4,12},{8,0},{12,4},{16,24},{20,28},{24,16},{28,20},{1,9},{5... | collective-permute-start | bytes 786440 | tf_op jit(solution)/shard_map/ppermute | solution.py:17
  6.9 11.6 %collective-permute-start.6 = (bf16[128,1024]{1,0:T(8,128)(2,1)S(1)}, bf16[128,1024]{1,0:T(8,128)(2,1)S(1)}, u32[]{:S(2)}, u32[]{:S(2)}) collective-permute-start(bf16[128,1024]{1,0:T(8,128)(2,1)S(1)} %get-tuple-element.81.rest_0_.rest_3_), channel_id=1, source_target_pairs={{0,16},{4,20},{8,24},{12,28},{16,0},{20,4},{24,8},{28,12},{1,17},{... | collective-permute-start | bytes 786440 | tf_op jit(solution)/shard_map/ppermute | solution.py:17
  6.9 18.6 %collective-permute-start.12 = (bf16[256,1024]{1,0:T(8,128)(2,1)}, bf16[256,1024]{1,0:T(8,128)(2,1)S(1)}, u32[]{:S(2)}, u32[]{:S(2)}) collective-permute-start(bf16[256,1024]{1,0:T(8,128)(2,1)} %param.5), channel_id=1, source_target_pairs={{0,3},{1,0},{2,1},{3,2},{4,7},{5,4},{6,5},{7,6},{8,11},{9,8},{10,9... | collective-permute-start | bytes 1572872 | tf_op jit(solution)/shard_map/ppermute | solution.py:132
  12.0 21.4 %collective-permute-start.13 = (bf16[256,1024]{1,0:T(8,128)(2,1)}, bf16[256,1024]{1,0:T(8,128)(2,1)S(1)}, u32[]{:S(2)}, u32[]{:S(2)}) collective-permute-start(bf16[256,1024]{1,0:T(8,128)(2,1)} %param.5), channel_id=1, source_target_pairs={{0,1},{1,2},{2,3},{3,0},{4,5},{5,6},{6,7},{7,4},{8,9},{9,10},{10,1... | collective-permute-start | bytes 1572872 | tf_op jit(solution)/shard_map/ppermute | solution.py:132
  16.7 7.6 %collective-permute-start.10 = (bf16[128,1024]{1,0:T(8,128)(2,1)S(1)}, bf16[128,1024]{1,0:T(8,128)(2,1)}, u32[]{:S(2)}, u32[]{:S(2)}) collective-permute-start(bf16[128,1024]{1,0:T(8,128)(2,1)S(1)} %collective-permute-done.2.rest_4_.rest_3_), channel_id=1, source_target_pairs={{0,16},{4,20},{8,24},{12,28},{16,0},{20,4},{24,8},{28,12},{1,17},{... | collective-permute-start | bytes 786440 | tf_op jit(solution)/shard_map/ppermute | solution.py:17
  20.0 13.4 %collective-permute-start.1 = (bf16[128,1024]{1,0:T(8,128)(2,1)S(1)}, bf16[128,1024]{1,0:T(8,128)(2,1)S(1)}, u32[]{:S(2)}, u32[]{:S(2)}) collective-permute-start(bf16[128,1024]{1,0:T(8,128)(2,1)S(1)} %get-tuple-element.80.rest_1_.rest_4_), channel_id=1, source_target_pairs={{0,4},{4,0},{8,12},{12,8},{16,20},{20,16},{24,28},{28,24},{1,5},{5... | collective-permute-start | bytes 786440 | tf_op jit(solution)/shard_map/ppermute | solution.py:17
  24.3 11.7 %collective-permute-start.4 = (bf16[128,1024]{1,0:T(8,128)(2,1)S(1)}, bf16[128,1024]{1,0:T(8,128)(2,1)S(1)}, u32[]{:S(2)}, u32[]{:S(2)}) collective-permute-start(bf16[128,1024]{1,0:T(8,128)(2,1)S(1)} %collective-permute-done.2.rest_4_.rest_3_), channel_id=1, source_target_pairs={{0,4},{4,0},{8,12},{12,8},{16,20},{20,16},{24,28},{28,24},{1,5},{5... | collective-permute-start | bytes 786440 | tf_op jit(solution)/shard_map/ppermute | solution.py:17
  25.5 10.7 %collective-permute-start.9 = (bf16[128,1024]{1,0:T(8,128)(2,1)S(1)}, bf16[128,1024]{1,0:T(8,128)(2,1)S(1)}, u32[]{:S(2)}, u32[]{:S(2)}) collective-permute-start(bf16[128,1024]{1,0:T(8,128)(2,1)S(1)} %collective-permute-done.7.rest_9_.rest_12_), channel_id=1, source_target_pairs={{0,4},{4,0},{8,12},{12,8},{16,20},{20,16},{24,28},{28,24},{1,5},{5... | collective-permute-start | bytes 786440 | tf_op jit(solution)/shard_map/ppermute | solution.py:17
  25.5 11.1 %collective-permute-start.5 = (bf16[128,1024]{1,0:T(8,128)(2,1)S(1)}, bf16[128,1024]{1,0:T(8,128)(2,1)S(1)}, u32[]{:S(2)}, u32[]{:S(2)}) collective-permute-start(bf16[128,1024]{1,0:T(8,128)(2,1)S(1)} %collective-permute-done.3.rest_5_.rest_4_), channel_id=1, source_target_pairs={{0,4},{4,0},{8,12},{12,8},{16,20},{20,16},{24,28},{28,24},{1,5},{5... | collective-permute-start | bytes 786440 | tf_op jit(solution)/shard_map/ppermute | solution.py:17
  33.5 28.5 %collective-permute-start.16 = (bf16[256,1024]{1,0:T(8,128)(2,1)S(1)}, bf16[256,1024]{1,0:T(8,128)(2,1)}, u32[]{:S(2)}, u32[]{:S(2)}) collective-permute-start(bf16[256,1024]{1,0:T(8,128)(2,1)S(1)} %copy-done.1), channel_id=1, source_target_pairs={{0,2},{1,3},{2,0},{3,1},{4,6},{5,7},{6,4},{7,5},{8,10},{9,11},{10,... | collective-permute-start | bytes 1572872 | tf_op jit(solution)/shard_map/ppermute | solution.py:132
  36.6 49.0 %collective-permute-start.20 = (bf16[512,1024]{1,0:T(8,128)(2,1)S(1)}, bf16[512,1024]{1,0:T(8,128)(2,1)}, u32[]{:S(2)}, u32[]{:S(2)}) collective-permute-start(bf16[512,1024]{1,0:T(8,128)(2,1)S(1)} %constant_dynamic-update-slice_fusion.rest_5_), channel_id=1, source_target_pairs={{0,8},{4,12},{8,0},{12,4},{16,24},{20,28},{24,16},{28,20},{1,9},{5... | collective-permute-start | bytes 3145736 | tf_op jit(solution)/shard_map/ppermute | solution.py:17
  38.2 47.5 %collective-permute-start.21 = (bf16[512,1024]{1,0:T(8,128)(2,1)S(1)}, bf16[512,1024]{1,0:T(8,128)(2,1)}, u32[]{:S(2)}, u32[]{:S(2)}) collective-permute-start(bf16[512,1024]{1,0:T(8,128)(2,1)S(1)} %constant_dynamic-update-slice_fusion.rest_5_), channel_id=1, source_target_pairs={{0,16},{4,20},{8,24},{12,28},{16,0},{20,4},{24,8},{28,12},{1,17},{... | collective-permute-start | bytes 3145736 | tf_op jit(solution)/shard_map/ppermute | solution.py:17
  53.1 13.5 %collective-permute-start.17 = (bf16[128,256]{1,0:T(8,128)(2,1)S(1)}, bf16[128,256]{1,0:T(8,128)(2,1)S(1)}, u32[]{:S(2)}, u32[]{:S(2)}) collective-permute-start(bf16[128,256]{1,0:T(8,128)(2,1)S(1)} %get-tuple-element.85), channel_id=1, source_target_pairs={{0,3},{1,0},{2,1},{3,2},{4,7},{5,4},{6,5},{7,6},{8,11},{9,8},{10,9... | collective-permute-start | bytes 196616 | tf_op jit(solution)/shard_map/ppermute | solution.py:132
  54.6 12.0 %collective-permute-start.18 = (bf16[128,256]{1,0:T(8,128)(2,1)S(1)}, bf16[128,256]{1,0:T(8,128)(2,1)S(1)}, u32[]{:S(2)}, u32[]{:S(2)}) collective-permute-start(bf16[128,256]{1,0:T(8,128)(2,1)S(1)} %get-tuple-element.84), channel_id=1, source_target_pairs={{0,2},{1,3},{2,0},{3,1},{4,6},{5,7},{6,4},{7,5},{8,10},{9,11},{10,... | collective-permute-start | bytes 196616 | tf_op jit(solution)/shard_map/ppermute | solution.py:132
  70.8 9.0 %collective-permute-start.22 = (bf16[128,1024]{1,0:T(8,128)(2,1)}, bf16[128,1024]{1,0:T(8,128)(2,1)S(1)}, u32[]{:S(2)}, u32[]{:S(2)}) collective-permute-start(bf16[128,1024]{1,0:T(8,128)(2,1)} %get-tuple-element.77), channel_id=1, source_target_pairs={{0,3},{1,0},{2,1},{3,2},{4,7},{5,4},{6,5},{7,6},{8,11},{9,8},{10,9... | collective-permute-start | bytes 786440 | tf_op jit(solution)/shard_map/ppermute | solution.py:132
  72.8 12.9 %collective-permute-start.23 = (bf16[128,1024]{1,0:T(8,128)(2,1)}, bf16[128,1024]{1,0:T(8,128)(2,1)}, u32[]{:S(2)}, u32[]{:S(2)}) collective-permute-start(bf16[128,1024]{1,0:T(8,128)(2,1)} %get-tuple-element.76), channel_id=1, source_target_pairs={{0,1},{1,2},{2,3},{3,0},{4,5},{5,6},{6,7},{7,4},{8,9},{9,10},{10,1... | collective-permute-start | bytes 786440 | tf_op jit(solution)/shard_map/ppermute | solution.py:132
  85.7 12.6 %collective-permute-start.24 = (bf16[4,256,1024]{2,1,0:T(8,128)(2,1)}, bf16[4,256,1024]{2,1,0:T(8,128)(2,1)}, u32[]{:S(2)}, u32[]{:S(2)}) collective-permute-start(bf16[4,256,1024]{2,1,0:T(8,128)(2,1)} %weight_grad_odd.1), channel_id=1, source_target_pairs={{0,4},{4,0},{8,12},{12,8},{16,20},{20,16},{24,28},{28,24},{1,5},{5... | collective-permute-start | bytes 6291464 | tf_op jit(solution)/shard_map/ppermute | solution.py:17
  85.7 16.1 %collective-permute-start.25 = (bf16[256,1024]{1,0:T(8,128)(2,1)}, bf16[256,1024]{1,0:T(8,128)(2,1)}, u32[]{:S(2)}, u32[]{:S(2)}) collective-permute-start(bf16[256,1024]{1,0:T(8,128)(2,1)} %collective-permute-done.16.rest_6_), channel_id=1, source_target_pairs={{0,8},{4,12},{8,0},{12,4},{16,24},{20,28},{24,16},{28,20},{1,9},{5... | collective-permute-start | bytes 1572872 | tf_op jit(solution)/shard_map/ppermute | solution.py:17
  87.2 14.6 %collective-permute-start.26 = (bf16[256,1024]{1,0:T(8,128)(2,1)}, bf16[256,1024]{1,0:T(8,128)(2,1)}, u32[]{:S(2)}, u32[]{:S(2)}) collective-permute-start(bf16[256,1024]{1,0:T(8,128)(2,1)} %collective-permute-done.16.rest_6_), channel_id=1, source_target_pairs={{0,16},{4,20},{8,24},{12,28},{16,0},{20,4},{24,8},{28,12},{1,17},{... | collective-permute-start | bytes 1572872 | tf_op jit(solution)/shard_map/ppermute | solution.py:17
  91.6 15.8 %collective-permute-start.32 = (bf16[128,2048]{1,0:T(8,128)(2,1)}, bf16[128,2048]{1,0:T(8,128)(2,1)}, u32[]{:S(2)}, u32[]{:S(2)}) collective-permute-start(bf16[128,2048]{1,0:T(8,128)(2,1)} %pad_maximum_fusion.1), channel_id=1, source_target_pairs={{0,1},{1,2},{2,3},{3,0},{4,5},{5,6},{6,7},{7,4},{8,9},{9,10},{10,1... | collective-permute-start | bytes 1572872 | tf_op jit(solution)/shard_map/ppermute | solution.py:132
  98.2 10.1 %collective-permute-start.29 = (bf16[512,1024]{1,0:T(8,128)(2,1)S(1)}, bf16[512,1024]{1,0:T(8,128)(2,1)S(1)}, u32[]{:S(2)}, u32[]{:S(2)}) collective-permute-start(bf16[512,1024]{1,0:T(8,128)(2,1)S(1)} %constant_dynamic-update-slice_fusion.rest_5_), channel_id=1, source_target_pairs={{0,4},{4,0},{8,12},{12,8},{16,20},{20,16},{24,28},{28,24},{1,5},{5... | collective-permute-start | bytes 3145736 | tf_op jit(solution)/shard_map/ppermute | solution.py:17
  102.8 13.9 %collective-permute-start.27 = (bf16[2,128,1024]{2,1,0:T(8,128)(2,1)S(1)}, bf16[2,128,1024]{2,1,0:T(8,128)(2,1)S(1)}, u32[]{:S(2)}, u32[]{:S(2)}) collective-permute-start(bf16[2,128,1024]{2,1,0:T(8,128)(2,1)S(1)} %slice_bitcast_fusion.3), channel_id=1, source_target_pairs={{0,8},{4,12},{8,0},{12,4},{16,24},{20,28},{24,16},{28,20},{1,9},{5... | collective-permute-start | bytes 1572872 | tf_op jit(solution)/shard_map/ppermute | solution.py:17
  103.4 13.6 %collective-permute-start.28 = (bf16[2,128,1024]{2,1,0:T(8,128)(2,1)S(1)}, bf16[2,128,1024]{2,1,0:T(8,128)(2,1)S(1)}, u32[]{:S(2)}, u32[]{:S(2)}) collective-permute-start(bf16[2,128,1024]{2,1,0:T(8,128)(2,1)S(1)} %slice_bitcast_fusion.2), channel_id=1, source_target_pairs={{0,16},{4,20},{8,24},{12,28},{16,0},{20,4},{24,8},{28,12},{1,17},{... | collective-permute-start | bytes 1572872 | tf_op jit(solution)/shard_map/ppermute | solution.py:17
  107.4 15.7 %collective-permute-start.31 = (bf16[128,2048]{1,0:T(8,128)(2,1)}, bf16[128,2048]{1,0:T(8,128)(2,1)}, u32[]{:S(2)}, u32[]{:S(2)}) collective-permute-start(bf16[128,2048]{1,0:T(8,128)(2,1)} %pad_maximum_fusion), channel_id=1, source_target_pairs={{0,3},{1,0},{2,1},{3,2},{4,7},{5,4},{6,5},{7,6},{8,11},{9,8},{10,9... | collective-permute-start | bytes 1572872 | tf_op jit(solution)/shard_map/ppermute | solution.py:132
  108.3 18.7 %collective-permute-start.35 = (bf16[512,1024]{1,0:T(8,128)(2,1)}, bf16[512,1024]{1,0:T(8,128)(2,1)}, u32[]{:S(2)}, u32[]{:S(2)}) collective-permute-start(bf16[512,1024]{1,0:T(8,128)(2,1)} %collective-permute-done.20.rest_5_), channel_id=1, source_target_pairs={{0,4},{4,0},{8,12},{12,8},{16,20},{20,16},{24,28},{28,24},{1,5},{5... | collective-permute-start | bytes 3145736 | tf_op jit(solution)/shard_map/ppermute | solution.py:17
  108.3 19.9 %collective-permute-start.37 = (bf16[512,1024]{1,0:T(8,128)(2,1)}, bf16[512,1024]{1,0:T(8,128)(2,1)}, u32[]{:S(2)}, u32[]{:S(2)}) collective-permute-start(bf16[512,1024]{1,0:T(8,128)(2,1)} %collective-permute-done.21.rest_13_), channel_id=1, source_target_pairs={{0,4},{4,0},{8,12},{12,8},{16,20},{20,16},{24,28},{28,24},{1,5},{5... | collective-permute-start | bytes 3145736 | tf_op jit(solution)/shard_map/ppermute | solution.py:17
  116.7 11.5 %collective-permute-start.36 = (bf16[256,1024]{1,0:T(8,128)(2,1)}, bf16[256,1024]{1,0:T(8,128)(2,1)}, u32[]{:S(2)}, u32[]{:S(2)}) collective-permute-start(bf16[256,1024]{1,0:T(8,128)(2,1)} %collective-permute-done.25.rest_6_), channel_id=1, source_target_pairs={{0,4},{4,0},{8,12},{12,8},{16,20},{20,16},{24,28},{28,24},{1,5},{5... | collective-permute-start | bytes 1572872 | tf_op jit(solution)/shard_map/ppermute | solution.py:17
  117.0 11.2 %collective-permute-start.38 = (bf16[256,1024]{1,0:T(8,128)(2,1)}, bf16[256,1024]{1,0:T(8,128)(2,1)}, u32[]{:S(2)}, u32[]{:S(2)}) collective-permute-start(bf16[256,1024]{1,0:T(8,128)(2,1)} %collective-permute-done.26.rest_14_), channel_id=1, source_target_pairs={{0,4},{4,0},{8,12},{12,8},{16,20},{20,16},{24,28},{28,24},{1,5},{5... | collective-permute-start | bytes 1572872 | tf_op jit(solution)/shard_map/ppermute | solution.py:17
  124.9 10.4 %collective-permute-start.34 = (bf16[128,1024]{1,0:T(8,128)(2,1)}, bf16[128,1024]{1,0:T(8,128)(2,1)S(1)}, u32[]{:S(2)}, u32[]{:S(2)}) collective-permute-start(bf16[128,1024]{1,0:T(8,128)(2,1)} %fusion.9), channel_id=1, source_target_pairs={{0,8},{4,12},{8,0},{12,4},{16,24},{20,28},{24,16},{28,20},{1,9},{5... | collective-permute-start | bytes 786440 | tf_op jit(solution)/shard_map/ppermute | solution.py:17
  127.0 9.5 %collective-permute-start.33 = (bf16[128,1024]{1,0:T(8,128)(2,1)}, bf16[128,1024]{1,0:T(8,128)(2,1)}, u32[]{:S(2)}, u32[]{:S(2)}) collective-permute-start(bf16[128,1024]{1,0:T(8,128)(2,1)} %fusion.8), channel_id=1, source_target_pairs={{0,16},{4,20},{8,24},{12,28},{16,0},{20,4},{24,8},{28,12},{1,17},{... | collective-permute-start | bytes 786440 | tf_op jit(solution)/shard_map/ppermute | solution.py:17
  (35 other events, 432.9 us)

commit v6 on v5

--- a/solution.py
+++ b/solution.py
@@ -245,7 +245,7 @@
 def halve(part, axis, bit, n_dp):
     go = lax.index_in_dim(part, 1, axis, keepdims=False).astype(BF16)
     stay = lax.index_in_dim(part, 0, axis, keepdims=False)
-    return stay + swap(go, bit, n_dp).astype(F32)
+    return stay, swap(go, bit, n_dp)
 
 
 def local(hidden, weight, qk_scale, cotangent, n_dp, n_tensor):
@@ -271,22 +271,22 @@
     far = [r for r in range(n_dp) if r not in near and r not in linked]
     share = hidden_share(d_slots, parts, far)
     d_rest = [shift(d_slots[k], k, n_tensor) for k in range(1, n_tensor)]
-    d_t, share, across, d_rest = lax.optimization_barrier((d_t, share, across, d_rest))
+    d_t, share = lax.optimization_barrier((d_t, share))
     cut = share.shape[2] // 2
     via_ahead = shift(share[2, :, :cut], 1, n_tensor)
     via_behind = shift(share[2, :, cut:], -1, n_tensor)
-    mid = {0: across}
-    mid.update({bit: swap(mid[0], bit, n_dp) for bit in bits})
     sent = weight_grad(d_t, hidden, where, n_dp, 1, BF16)
-    due = (d_t, sent, pair, via_ahead, via_behind)
-    d_t, sent, pair, via_ahead, via_behind = lax.optimization_barrier(due)
+    due = (d_t, sent, pair, via_ahead, via_behind, across)
+    d_t, sent, pair, via_ahead, via_behind, across = lax.optimization_barrier(due)
     to_ahead = jnp.concatenate([share[1, :, :cut] + via_ahead, share[1, :, cut:]], 1)
     to_behind = jnp.concatenate([share[-1, :, :cut], share[-1, :, cut:] + via_behind], 1)
     from_ahead, from_behind = shift(to_ahead, 1, n_tensor), shift(to_behind, -1, n_tensor)
+    mid = {0: across}
+    mid.update({bit: swap(mid[0], bit, n_dp) for bit in bits})
     pair = add_core(pair, n_dp)
     keep = weight_grad(d_t, hidden, where, n_dp, 0, F32)
     total = keep + swap(sent, 1, n_dp).astype(F32)
-    total, mid = lax.optimization_barrier((total, mid))
+    total, mid, d_rest = lax.optimization_barrier((total, mid, d_rest))
     mid = add_core(mid, n_dp)
     d_pair = jnp.concatenate([d_rest[0], d_rest[-1]], 1)
     d_all = (d_slots[0], d_pair, d_rest[1], parts, pair, mid, where)
@@ -297,16 +297,19 @@
     orders = [list(range(count)), list(range(count))[::-1]]
     left = [list(range(count))[::-1], list(range(count))[::-1]]
     for step in range(count):
-        if step == count - 1:
-            due = (sides, input_grad, from_ahead, from_behind)
-            sides, input_grad, from_ahead, from_behind = lax.optimization_barrier(due)
         for at in range(2):
             b = orders[at][step]
             axis = left[at].index(b)
             left[at].remove(b)
             sides[at] = halve(sides[at], axis, bits[b], n_dp)
-    input_grad = hidden_grad(*d_all, linked, input_grad)
-    sides, input_grad = lax.optimization_barrier((sides, input_grad))
+        if step == count - 1:
+            input_grad = hidden_grad(*d_all, linked, input_grad)
+        if step == count - 2:
+            due = (sides, input_grad, from_ahead, from_behind)
+            sides, input_grad, from_ahead, from_behind = lax.optimization_barrier(due)
+        else:
+            sides, input_grad = lax.optimization_barrier((sides, input_grad))
+        sides = [stay + came.astype(F32) for stay, came in sides]
     grad = jnp.concatenate(sides, 0)
     input_grad = add_shares([share[0], from_ahead, from_behind], where, far, width, input_grad)
     w = weight.astype(F32)

time: 150 us -> 152 us (1.013)
  local copies, waits for them, and re-layouts: 8.58 us -> 15.8 us
  starting transfers between devices: 38.7 us -> 34.9 us
    ppermute x10, waiting for transfers between devices: 24.7 us -> 34.4 us  [shift(): lax.ppermute(x, 'tensor', [(i, (i - by) % n_tensor) for i in range(n_tens...]
    ppermute x32, waiting for transfers between devices: 21.5 us -> 11.9 us  [swap(): return lax.ppermute(x, 'dp', [(i, i ^ bit) for i in range(n_dp)])]
    squeeze x0 -> x3, local copies, waits for them, and re-layouts: none -> 3.5 us  [halve(): stay = lax.index_in_dim(part, 0, axis, keepdims=False)]
    unnamed x53 -> x54, local copies, waits for them, and re-layouts: 0.18 us -> 3.5 us
    ppermute x10, starting transfers between devices: 16.3 us -> 14.1 us  [shift(): lax.ppermute(x, 'tensor', [(i, (i - by) % n_tensor) for i in range(n_tens...]
    ppermute x32, starting transfers between devices: 22.5 us -> 20.8 us  [swap(): return lax.ppermute(x, 'dp', [(i, i ^ bit) for i in range(n_dp)])]
    add x3 -> x4, other arithmetic: 3.5 us -> 3.77 us  [local(): sides = [stay + came.astype(F32) for stay, came in sides]]
  transfers between devices with their start and end apart: 42 -> 42, of which waited for: 14 -> 15; matrix products, arithmetic and copies ran while one was open for 12% -> 14% of each run, Pallas kernels for 28% -> 27%
where the time goes in v6:
time: 152 us
  waiting for transfers between devices  46.3 us (30%)
  Pallas kernels  41.2 us (27%)
  starting transfers between devices  34.9 us (23%)
  local copies, waits for them, and re-layouts  15.8 us (10%)
  other arithmetic  12.5 us (8%)
    ppermute x10, waiting for transfers between devices, shift(): lax.ppermute(x, 'tensor', [(i, (i - by) % n_tensor) for i in range(n_tens...  34.4 us
    ppermute x32, starting transfers between devices, swap(): return lax.ppermute(x, 'dp', [(i, i ^ bit) for i in range(n_dp)])  20.8 us
    ppermute x10, starting transfers between devices, shift(): lax.ppermute(x, 'tensor', [(i, (i - by) % n_tensor) for i in range(n_tens...  14.1 us
    pallas_call x2, Pallas kernels, weight_grad(): pl.pallas_call(body, grid_spec=pltpu.PrefetchScalarGridSpec(num_scalar_pr...  12.3 us
    ppermute x32, waiting for transfers between devices, swap(): return lax.ppermute(x, 'dp', [(i, i ^ bit) for i in range(n_dp)])  11.9 us
    pallas_call x2, Pallas kernels, hidden_grad(): pl.pallas_call(body, grid_spec=pltpu.PrefetchScalarGridSpec(num_scalar_pr...  11.7 us
    pallas_call x1, Pallas kernels, project(): pl.pallas_call(body, grid_spec=pltpu.PrefetchScalarGridSpec(num_scalar_pr...  11 us
    add x4, other arithmetic, local(): sides = [stay + came.astype(F32) for stay, came in sides]  3.77 us
  transfers between devices with their start and end apart: 42, of which 15 were waited for; matrix products, arithmetic and copies ran while one was open for 14% of the time, Pallas kernels for 27%

profile of v6, /device:TPU:0, one launch (start us, length us, event | category | flops | bytes accessed | tf_op | source)
XLA Modules:
  0.0 151.7 jit_solution(3014593131862890373)
XLA Ops:
  1.8 3.0 %collective-permute-start.2 = (bf16[128,1024]{1,0:T(8,128)(2,1)S(1)}, bf16[128,1024]{1,0:T(8,128)(2,1)S(1)}, u32[]{:S(2)}, u32[]{:S(2)}) collective-permute-start(bf16[128,1024]{1,0:T(8,128)(2,1)S(1)} %get-tuple-element.87.rest_0_.rest_3_), channel_id=1, source_target_pairs={{0,8},{4,12},{8,0},{12,4},{16,24},{20,28},{24,16},{28,20},{1,9},{5... | collective-permute-start | bytes 786440 | tf_op jit(solution)/shard_map/ppermute | solution.py:17
  4.8 1.5 %collective-permute-start.7 = (bf16[128,1024]{1,0:T(8,128)(2,1)S(1)}, bf16[128,1024]{1,0:T(8,128)(2,1)S(1)}, u32[]{:S(2)}, u32[]{:S(2)}) collective-permute-start(bf16[128,1024]{1,0:T(8,128)(2,1)S(1)} %get-tuple-element.86.rest_1_.rest_4_), channel_id=1, source_target_pairs={{0,16},{4,20},{8,24},{12,28},{16,0},{20,4},{24,8},{28,12},{1,17},{... | collective-permute-start | bytes 786440 | tf_op jit(solution)/shard_map/ppermute | solution.py:17
  6.3 3.6 %collective-permute-start.12 = (bf16[256,1024]{1,0:T(8,128)(2,1)}, bf16[256,1024]{1,0:T(8,128)(2,1)S(1)}, u32[]{:S(2)}, u32[]{:S(2)}) collective-permute-start(bf16[256,1024]{1,0:T(8,128)(2,1)} %param.5), channel_id=1, source_target_pairs={{0,3},{1,0},{2,1},{3,2},{4,7},{5,4},{6,5},{7,6},{8,11},{9,8},{10,9... | collective-permute-start | bytes 1572872 | tf_op jit(solution)/shard_map/ppermute | solution.py:132
  11.1 1.8 %collective-permute-start.10 = (bf16[128,1024]{1,0:T(8,128)(2,1)S(1)}, bf16[128,1024]{1,0:T(8,128)(2,1)S(1)}, u32[]{:S(2)}, u32[]{:S(2)}) collective-permute-start(bf16[128,1024]{1,0:T(8,128)(2,1)S(1)} %collective-permute-done.2.rest_4_.rest_3_), channel_id=1, source_target_pairs={{0,16},{4,20},{8,24},{12,28},{16,0},{20,4},{24,8},{28,12},{1,17},{... | collective-permute-start | bytes 786440 | tf_op jit(solution)/shard_map/ppermute | solution.py:17
  12.9 1.5 collective-permute-start.11
  14.9 3.7 %collective-permute-done.10.rest_12_.rest_0_ = bf16[128,1024]{1,0:T(8,128)(2,1)S(1)} collective-permute-done((bf16[128,1024]{1,0:T(8,128)(2,1)S(1)}, bf16[128,1024]{1,0:T(8,128)(2,1)S(1)}, u32[]{:S(2)}, u32[]{:S(2)}) %collective-permute-start.10) | collective-permute-done | bytes 262176 | tf_op jit(solution)/shard_map/ppermute | solution.py:17
  18.6 1.5 collective-permute-start.6
  20.1 2.1 %collective-permute-done.11.rest_13_.rest_1_ = bf16[128,1024]{1,0:T(8,128)(2,1)} collective-permute-done((bf16[128,1024]{1,0:T(8,128)(2,1)S(1)}, bf16[128,1024]{1,0:T(8,128)(2,1)}, u32[]{:S(2)}, u32[]{:S(2)}) %collective-permute-start.11) | collective-permute-done | bytes 262176 | tf_op jit(solution)/shard_map/ppermute | solution.py:17
  22.7 10.2 %collective-permute-done.13 = bf16[256,1024]{1,0:T(8,128)(2,1)S(1)} collective-permute-done((bf16[256,1024]{1,0:T(8,128)(2,1)}, bf16[256,1024]{1,0:T(8,128)(2,1)S(1)}, u32[]{:S(2)}, u32[]{:S(2)}) %collective-permute-start.13) | collective-permute-done | bytes 524320 | tf_op jit(solution)/shard_map/ppermute | solution.py:132
  39.5 11.0 %project.1 = (bf16[512,256]{1,0:T(8,128)(2,1)}, bf16[4,128,256]{2,1,0:T(8,128)(2,1)}, bf16[256,512]{1,0:T(8,128)(2,1)}) custom-call(s32[2]{0:T(128)} %pad_add_fusion.where_ref, bf16[512,8192]{1,0:T(8,128)(2,1)} %h_ref.5, f32[1,128]{1,0:T(1,128)} %s_ref.1, bf16[512,256]{1,0:T(8,128)(2,1)} %c_ref.1, bf16[128,1024]{1,0:T(8,128)(2,1)} %copy-done.8, ...), custom_call_target="tpu_custom_call" | custom-call | tf_op jit(solution)/shard_map/project/pallas_call | solution.py:81
  50.5 3.2 %hidden_share.1 = bf16[4,128,2048]{2,1,0:T(8,128)(2,1)} custom-call(bf16[4,128,256]{2,1,0:T(8,128)(2,1)} %get-tuple-element.43.d_ref, bf16[128,1024]{1,0:T(8,128)(2,1)} %copy-done.18, bf16[128,1024]{1,0:T(8,128)(2,1)} %collective-permute-done.11.rest_13_.rest_1_, bf16[128,1024]{1,0:T(8,128)(2,1)} %collective-permute-done.14.rest_14_.rest_2_, ...), custom_call_target="tpu_custom_call" | custom-call | tf_op jit(solution)/shard_map/hidden_share/pallas_call | solution.py:151
  53.7 2.1 %slice_bitcast_fusion.7 = (bf16[128,1024]{1,0:T(8,128)(2,1)S(1)}, bf16[128,1024]{1,0:T(8,128)(2,1)S(1)}, bf16[128,1024]{1,0:T(8,128)(2,1)}, bf16[128,1024]{1,0:T(8,128)(2,1)}) fusion(bf16[4,128,2048]{2,1,0:T(8,128)(2,1)} %hidden_share.1), kind=kLoop, calls=%fused_computation.32 | loop fusion | bytes 2097152 | tf_op jit(solution)/shard_map/squeeze | solution.py:282
  55.8 3.1 %collective-permute-start.18 = (bf16[128,1024]{1,0:T(8,128)(2,1)}, bf16[128,1024]{1,0:T(8,128)(2,1)}, u32[]{:S(2)}, u32[]{:S(2)}) collective-permute-start(bf16[128,1024]{1,0:T(8,128)(2,1)} %get-tuple-element.83), channel_id=1, source_target_pairs={{0,3},{1,0},{2,1},{3,2},{4,7},{5,4},{6,5},{7,6},{8,11},{9,8},{10,9... | collective-permute-start | bytes 786440 | tf_op jit(solution)/shard_map/ppermute | solution.py:132
  58.9 5.9 %weight_grad_odd.1 = bf16[4,256,1024]{2,1,0:T(8,128)(2,1)} custom-call(s32[2]{0:T(128)} %pad_add_fusion.where_ref, bf16[256,512]{1,0:T(8,128)(2,1)} %get-tuple-element.48.d_ref, bf16[512,8192]{1,0:T(8,128)(2,1)} %h_ref.5), custom_call_target="tpu_custom_call" | custom-call | tf_op jit(solution)/shard_map/weight_grad_odd/pallas_call | solution.py:115
  65.3 10.1 %collective-permute-done.18 = bf16[128,1024]{1,0:T(8,128)(2,1)} collective-permute-done((bf16[128,1024]{1,0:T(8,128)(2,1)}, bf16[128,1024]{1,0:T(8,128)(2,1)}, u32[]{:S(2)}, u32[]{:S(2)}) %collective-permute-start.18) | collective-permute-done | bytes 262176 | tf_op jit(solution)/shard_map/ppermute | solution.py:132
  76.3 1.5 %collective-permute-start.24 = (bf16[128,256]{1,0:T(8,128)(2,1)}, bf16[128,256]{1,0:T(8,128)(2,1)S(1)}, u32[]{:S(2)}, u32[]{:S(2)}) collective-permute-start(bf16[128,256]{1,0:T(8,128)(2,1)} %get-tuple-element.91), channel_id=1, source_target_pairs={{0,3},{1,0},{2,1},{3,2},{4,7},{5,4},{6,5},{7,6},{8,11},{9,8},{10,9... | collective-permute-start | bytes 196616 | tf_op jit(solution)/shard_map/ppermute | solution.py:132
  78.3 1.5 collective-permute-start.22
  79.8 1.5 %collective-permute-start.23 = (bf16[256,1024]{1,0:T(8,128)(2,1)}, bf16[256,1024]{1,0:T(8,128)(2,1)}, u32[]{:S(2)}, u32[]{:S(2)}) collective-permute-start(bf16[256,1024]{1,0:T(8,128)(2,1)} %collective-permute-done.20.rest_6_), channel_id=1, source_target_pairs={{0,16},{4,20},{8,24},{12,28},{16,0},{20,4},{24,8},{28,12},{1,17},{... | collective-permute-start | bytes 1572872 | tf_op jit(solution)/shard_map/ppermute | solution.py:17
  84.1 6.4 %weight_grad_even.1 = f32[4,256,1024]{2,1,0:T(8,128)} custom-call(s32[2]{0:T(128)} %pad_add_fusion.where_ref, bf16[256,512]{1,0:T(8,128)(2,1)} %get-tuple-element.48.d_ref, bf16[512,8192]{1,0:T(8,128)(2,1)} %h_ref.5), custom_call_target="tpu_custom_call" | custom-call | tf_op jit(solution)/shard_map/weight_grad_even/pallas_call | solution.py:115
  91.2 3.6 %convert_add_fusion = f32[4,256,1024]{2,1,0:T(8,128)S(1)} fusion(f32[4,256,1024]{2,1,0:T(8,128)} %weight_grad_even.1, bf16[4,256,1024]{2,1,0:T(8,128)(2,1)} %collective-permute-done.21), kind=kLoop, calls=%fused_computation | loop fusion | flops 2097152 | bytes 10485760 | tf_op jit(solution)/shard_map/add | solution.py:288
  94.8 2.3 %collective-permute-start.32 = (bf16[128,2048]{1,0:T(8,128)(2,1)}, bf16[128,2048]{1,0:T(8,128)(2,1)S(1)}, u32[]{:S(2)}, u32[]{:S(2)}) collective-permute-start(bf16[128,2048]{1,0:T(8,128)(2,1)} %pad_maximum_fusion.2), channel_id=1, source_target_pairs={{0,1},{1,2},{2,3},{3,0},{4,5},{5,6},{6,7},{7,4},{8,9},{9,10},{10,1... | collective-permute-start | bytes 1572872 | tf_op jit(solution)/shard_map/ppermute | solution.py:132
  97.1 1.5 %collective-permute-start.31 = (bf16[128,2048]{1,0:T(8,128)(2,1)}, bf16[128,2048]{1,0:T(8,128)(2,1)}, u32[]{:S(2)}, u32[]{:S(2)}) collective-permute-start(bf16[128,2048]{1,0:T(8,128)(2,1)} %pad_maximum_fusion.1), channel_id=1, source_target_pairs={{0,3},{1,0},{2,1},{3,2},{4,7},{5,4},{6,5},{7,6},{8,11},{9,8},{10,9... | collective-permute-start | bytes 1572872 | tf_op jit(solution)/shard_map/ppermute | solution.py:132
  104.8 4.6 %hidden_grad.2.rest_19_ = bf16[128,8192]{1,0:T(8,128)(2,1)} custom-call(s32[2]{0:T(128)} %pad_add_fusion.where_ref, bf16[128,256]{1,0:T(8,128)(2,1)} %get-tuple-element.88.rest_0_, bf16[128,512]{1,0:T(8,128)(2,1)} %copy-done.20, bf16[128,256]{1,0:T(8,128)(2,1)} %copy-done.24, bf16[128,1024]{1,0:T(8,128)(2,1)} %copy-done.8, bf16[128,1024]{1,0:T(8,128)(2,1)} %copy-done.7, ...), custom_call_target="tpu_custom_call" | custom-call | tf_op jit(solution)/shard_map/hidden_grad/pallas_call | solution.py:201
  109.4 2.3 %collective-permute-done.32.rest_2_ = bf16[128,2048]{1,0:T(8,128)(2,1)S(1)} collective-permute-done((bf16[128,2048]{1,0:T(8,128)(2,1)}, bf16[128,2048]{1,0:T(8,128)(2,1)S(1)}, u32[]{:S(2)}, u32[]{:S(2)}) %collective-permute-start.32) | collective-permute-done | bytes 524320 | tf_op jit(solution)/shard_map/ppermute | solution.py:132
  111.7 10.8 %collective-permute-done.31.rest_1_ = bf16[128,2048]{1,0:T(8,128)(2,1)} collective-permute-done((bf16[128,2048]{1,0:T(8,128)(2,1)}, bf16[128,2048]{1,0:T(8,128)(2,1)}, u32[]{:S(2)}, u32[]{:S(2)}) %collective-permute-start.31) | collective-permute-done | bytes 524320 | tf_op jit(solution)/shard_map/ppermute | solution.py:132
  123.1 1.5 convert_add_fusion.2
  128.7 7.1 %hidden_grad.3.rest_3_ = bf16[128,8192]{1,0:T(8,128)(2,1)} custom-call(s32[2]{0:T(128)} %pad_add_fusion.where_ref, bf16[128,256]{1,0:T(8,128)(2,1)} %get-tuple-element.88.rest_0_, bf16[128,512]{1,0:T(8,128)(2,1)} %copy-done.20, bf16[128,256]{1,0:T(8,128)(2,1)} %copy-done.24, bf16[128,1024]{1,0:T(8,128)(2,1)} %copy-done.9, ...), custom_call_target="tpu_custom_call", output_to_operand_aliasing={{}: (20, {})} | custom-call | tf_op jit(solution)/shard_map/hidden_grad/pallas_call | solution.py:201
  135.9 1.3 slice_bitcast_fusion.2
  141.4 1.6 %collective-permute-start.40 = (f32[3,256]{1,0:T(4,128)S(1)}, f32[3,256]{1,0:T(4,128)S(1)}, u32[]{:S(2)}, u32[]{:S(2)}) collective-permute-start(f32[3,256]{1,0:T(4,128)S(1)} %fusion.8), channel_id=1, source_target_pairs={{0,8},{4,12},{8,0},{12,4},{16,24},{20,28},{24,16},{28,20},{1,9},{5... | collective-permute-start | bytes 9224 | tf_op jit(solution)/shard_map/ppermute | solution.py:17
  143.0 2.1 %collective-permute-done.40 = f32[3,256]{1,0:T(4,128)S(1)} collective-permute-done((f32[3,256]{1,0:T(4,128)S(1)}, f32[3,256]{1,0:T(4,128)S(1)}, u32[]{:S(2)}, u32[]{:S(2)}) %collective-permute-start.40) | collective-permute-done | bytes 3104 | tf_op jit(solution)/shard_map/ppermute | solution.py:17
  145.1 1.6 %collective-permute-start.41 = (f32[3,256]{1,0:T(4,128)S(1)}, f32[3,256]{1,0:T(4,128)S(1)}, u32[]{:S(2)}, u32[]{:S(2)}) collective-permute-start(f32[3,256]{1,0:T(4,128)S(1)} %fusion.11), channel_id=1, source_target_pairs={{0,16},{4,20},{8,24},{12,28},{16,0},{20,4},{24,8},{28,12},{1,17},{... | collective-permute-start | bytes 9224 | tf_op jit(solution)/shard_map/ppermute | solution.py:17
  147.5 3.0 %add_shares.1 = bf16[128,8192]{1,0:T(8,128)(2,1)} custom-call(s32[2]{0:T(128)} %pad_add_fusion.where_ref, bf16[128,2048]{1,0:T(8,128)(2,1)} %slice_bitcast_fusion.6.rest_0_, bf16[128,2048]{1,0:T(8,128)(2,1)} %collective-permute-done.31.rest_1_, bf16[128,2048]{1,0:T(8,128)(2,1)} %copy-done.21, ...), custom_call_target="tpu_custom_call", output_to_operand_aliasing={{}: (4, {})} | custom-call | tf_op jit(solution)/shard_map/add_shares/pallas_call | solution.py:230
  (144 shorter events, 32.3 us)
Async XLA Ops:
  1.8 9.3 %collective-permute-start.2 = (bf16[128,1024]{1,0:T(8,128)(2,1)S(1)}, bf16[128,1024]{1,0:T(8,128)(2,1)S(1)}, u32[]{:S(2)}, u32[]{:S(2)}) collective-permute-start(bf16[128,1024]{1,0:T(8,128)(2,1)S(1)} %get-tuple-element.87.rest_0_.rest_3_), channel_id=1, source_target_pairs={{0,8},{4,12},{8,0},{12,4},{16,24},{20,28},{24,16},{28,20},{1,9},{5... | collective-permute-start | bytes 786440 | tf_op jit(solution)/shard_map/ppermute | solution.py:17
  4.8 8.1 %collective-permute-start.7 = (bf16[128,1024]{1,0:T(8,128)(2,1)S(1)}, bf16[128,1024]{1,0:T(8,128)(2,1)S(1)}, u32[]{:S(2)}, u32[]{:S(2)}) collective-permute-start(bf16[128,1024]{1,0:T(8,128)(2,1)S(1)} %get-tuple-element.86.rest_1_.rest_4_), channel_id=1, source_target_pairs={{0,16},{4,20},{8,24},{12,28},{16,0},{20,4},{24,8},{28,12},{1,17},{... | collective-permute-start | bytes 786440 | tf_op jit(solution)/shard_map/ppermute | solution.py:17
  6.3 16.2 %collective-permute-start.12 = (bf16[256,1024]{1,0:T(8,128)(2,1)}, bf16[256,1024]{1,0:T(8,128)(2,1)S(1)}, u32[]{:S(2)}, u32[]{:S(2)}) collective-permute-start(bf16[256,1024]{1,0:T(8,128)(2,1)} %param.5), channel_id=1, source_target_pairs={{0,3},{1,0},{2,1},{3,2},{4,7},{5,4},{6,5},{7,6},{8,11},{9,8},{10,9... | collective-permute-start | bytes 1572872 | tf_op jit(solution)/shard_map/ppermute | solution.py:132
  9.9 23.0 %collective-permute-start.13 = (bf16[256,1024]{1,0:T(8,128)(2,1)}, bf16[256,1024]{1,0:T(8,128)(2,1)S(1)}, u32[]{:S(2)}, u32[]{:S(2)}) collective-permute-start(bf16[256,1024]{1,0:T(8,128)(2,1)} %param.5), channel_id=1, source_target_pairs={{0,1},{1,2},{2,3},{3,0},{4,5},{5,6},{6,7},{7,4},{8,9},{9,10},{10,1... | collective-permute-start | bytes 1572872 | tf_op jit(solution)/shard_map/ppermute | solution.py:132
  11.1 7.5 %collective-permute-start.10 = (bf16[128,1024]{1,0:T(8,128)(2,1)S(1)}, bf16[128,1024]{1,0:T(8,128)(2,1)S(1)}, u32[]{:S(2)}, u32[]{:S(2)}) collective-permute-start(bf16[128,1024]{1,0:T(8,128)(2,1)S(1)} %collective-permute-done.2.rest_4_.rest_3_), channel_id=1, source_target_pairs={{0,16},{4,20},{8,24},{12,28},{16,0},{20,4},{24,8},{28,12},{1,17},{... | collective-permute-start | bytes 786440 | tf_op jit(solution)/shard_map/ppermute | solution.py:17
  12.9 9.3 %collective-permute-start.11 = (bf16[128,1024]{1,0:T(8,128)(2,1)S(1)}, bf16[128,1024]{1,0:T(8,128)(2,1)}, u32[]{:S(2)}, u32[]{:S(2)}) collective-permute-start(bf16[128,1024]{1,0:T(8,128)(2,1)S(1)} %collective-permute-done.7.rest_9_.rest_12_), channel_id=1, source_target_pairs={{0,8},{4,12},{8,0},{12,4},{16,24},{20,28},{24,16},{28,20},{1,9},{5... | collective-permute-start | bytes 786440 | tf_op jit(solution)/shard_map/ppermute | solution.py:17
  14.4 20.2 %collective-permute-start.3 = (bf16[128,1024]{1,0:T(8,128)(2,1)S(1)}, bf16[128,1024]{1,0:T(8,128)(2,1)S(1)}, u32[]{:S(2)}, u32[]{:S(2)}) collective-permute-start(bf16[128,1024]{1,0:T(8,128)(2,1)S(1)} %get-tuple-element.86.rest_1_.rest_4_), channel_id=1, source_target_pairs={{0,8},{4,12},{8,0},{12,4},{16,24},{20,28},{24,16},{28,20},{1,9},{5... | collective-permute-start | bytes 786440 | tf_op jit(solution)/shard_map/ppermute | solution.py:17
  18.6 16.5 %collective-permute-start.6 = (bf16[128,1024]{1,0:T(8,128)(2,1)S(1)}, bf16[128,1024]{1,0:T(8,128)(2,1)S(1)}, u32[]{:S(2)}, u32[]{:S(2)}) collective-permute-start(bf16[128,1024]{1,0:T(8,128)(2,1)S(1)} %get-tuple-element.87.rest_0_.rest_3_), channel_id=1, source_target_pairs={{0,16},{4,20},{8,24},{12,28},{16,0},{20,4},{24,8},{28,12},{1,17},{... | collective-permute-start | bytes 786440 | tf_op jit(solution)/shard_map/ppermute | solution.py:17
  22.2 13.4 %collective-permute-start = (bf16[128,1024]{1,0:T(8,128)(2,1)S(1)}, bf16[128,1024]{1,0:T(8,128)(2,1)}, u32[]{:S(2)}, u32[]{:S(2)}) collective-permute-start(bf16[128,1024]{1,0:T(8,128)(2,1)S(1)} %get-tuple-element.87.rest_0_.rest_3_), channel_id=1, source_target_pairs={{0,4},{4,0},{8,12},{12,8},{16,20},{20,16},{24,28},{28,24},{1,5},{5... | collective-permute-start | bytes 786440 | tf_op jit(solution)/shard_map/ppermute | solution.py:17
  22.6 13.0 %collective-permute-start.1 = (bf16[128,1024]{1,0:T(8,128)(2,1)S(1)}, bf16[128,1024]{1,0:T(8,128)(2,1)}, u32[]{:S(2)}, u32[]{:S(2)}) collective-permute-start(bf16[128,1024]{1,0:T(8,128)(2,1)S(1)} %get-tuple-element.86.rest_1_.rest_4_), channel_id=1, source_target_pairs={{0,4},{4,0},{8,12},{12,8},{16,20},{20,16},{24,28},{28,24},{1,5},{5... | collective-permute-start | bytes 786440 | tf_op jit(solution)/shard_map/ppermute | solution.py:17
  34.6 40.9 %collective-permute-start.16 = (bf16[512,1024]{1,0:T(8,128)(2,1)}, bf16[512,1024]{1,0:T(8,128)(2,1)}, u32[]{:S(2)}, u32[]{:S(2)}) collective-permute-start(bf16[512,1024]{1,0:T(8,128)(2,1)} %constant_dynamic-update-slice_fusion.rest_5_), channel_id=1, source_target_pairs={{0,8},{4,12},{8,0},{12,4},{16,24},{20,28},{24,16},{28,20},{1,9},{5... | collective-permute-start | bytes 3145736 | tf_op jit(solution)/shard_map/ppermute | solution.py:17
  35.1 40.3 %collective-permute-start.17 = (bf16[512,1024]{1,0:T(8,128)(2,1)}, bf16[512,1024]{1,0:T(8,128)(2,1)}, u32[]{:S(2)}, u32[]{:S(2)}) collective-permute-start(bf16[512,1024]{1,0:T(8,128)(2,1)} %constant_dynamic-update-slice_fusion.rest_5_), channel_id=1, source_target_pairs={{0,16},{4,20},{8,24},{12,28},{16,0},{20,4},{24,8},{28,12},{1,17},{... | collective-permute-start | bytes 3145736 | tf_op jit(solution)/shard_map/ppermute | solution.py:17
  37.9 27.4 %collective-permute-start.20 = (bf16[256,1024]{1,0:T(8,128)(2,1)S(1)}, bf16[256,1024]{1,0:T(8,128)(2,1)}, u32[]{:S(2)}, u32[]{:S(2)}) collective-permute-start(bf16[256,1024]{1,0:T(8,128)(2,1)S(1)} %copy-done.1), channel_id=1, source_target_pairs={{0,2},{1,3},{2,0},{3,1},{4,6},{5,7},{6,4},{7,5},{8,10},{9,11},{10,... | collective-permute-start | bytes 1572872 | tf_op jit(solution)/shard_map/ppermute | solution.py:132
  55.8 19.6 %collective-permute-start.18 = (bf16[128,1024]{1,0:T(8,128)(2,1)}, bf16[128,1024]{1,0:T(8,128)(2,1)}, u32[]{:S(2)}, u32[]{:S(2)}) collective-permute-start(bf16[128,1024]{1,0:T(8,128)(2,1)} %get-tuple-element.83), channel_id=1, source_target_pairs={{0,3},{1,0},{2,1},{3,2},{4,7},{5,4},{6,5},{7,6},{8,11},{9,8},{10,9... | collective-permute-start | bytes 786440 | tf_op jit(solution)/shard_map/ppermute | solution.py:132
  58.8 16.6 %collective-permute-start.19 = (bf16[128,1024]{1,0:T(8,128)(2,1)}, bf16[128,1024]{1,0:T(8,128)(2,1)}, u32[]{:S(2)}, u32[]{:S(2)}) collective-permute-start(bf16[128,1024]{1,0:T(8,128)(2,1)} %get-tuple-element.82), channel_id=1, source_target_pairs={{0,1},{1,2},{2,3},{3,0},{4,5},{5,6},{6,7},{7,4},{8,9},{9,10},{10,1... | collective-permute-start | bytes 786440 | tf_op jit(solution)/shard_map/ppermute | solution.py:132
  75.4 15.8 %collective-permute-start.21 = (bf16[4,256,1024]{2,1,0:T(8,128)(2,1)}, bf16[4,256,1024]{2,1,0:T(8,128)(2,1)}, u32[]{:S(2)}, u32[]{:S(2)}) collective-permute-start(bf16[4,256,1024]{2,1,0:T(8,128)(2,1)} %weight_grad_odd.1), channel_id=1, source_target_pairs={{0,4},{4,0},{8,12},{12,8},{16,20},{20,16},{24,28},{28,24},{1,5},{5... | collective-permute-start | bytes 6291464 | tf_op jit(solution)/shard_map/ppermute | solution.py:17
  76.3 14.2 %collective-permute-start.24 = (bf16[128,256]{1,0:T(8,128)(2,1)}, bf16[128,256]{1,0:T(8,128)(2,1)S(1)}, u32[]{:S(2)}, u32[]{:S(2)}) collective-permute-start(bf16[128,256]{1,0:T(8,128)(2,1)} %get-tuple-element.91), channel_id=1, source_target_pairs={{0,3},{1,0},{2,1},{3,2},{4,7},{5,4},{6,5},{7,6},{8,11},{9,8},{10,9... | collective-permute-start | bytes 196616 | tf_op jit(solution)/shard_map/ppermute | solution.py:132
  77.8 17.0 %collective-permute-start.25 = (bf16[128,256]{1,0:T(8,128)(2,1)}, bf16[128,256]{1,0:T(8,128)(2,1)S(1)}, u32[]{:S(2)}, u32[]{:S(2)}) collective-permute-start(bf16[128,256]{1,0:T(8,128)(2,1)} %get-tuple-element.90), channel_id=1, source_target_pairs={{0,2},{1,3},{2,0},{3,1},{4,6},{5,7},{6,4},{7,5},{8,10},{9,11},{10,... | collective-permute-start | bytes 196616 | tf_op jit(solution)/shard_map/ppermute | solution.py:132
  78.3 20.4 %collective-permute-start.22 = (bf16[256,1024]{1,0:T(8,128)(2,1)}, bf16[256,1024]{1,0:T(8,128)(2,1)}, u32[]{:S(2)}, u32[]{:S(2)}) collective-permute-start(bf16[256,1024]{1,0:T(8,128)(2,1)} %collective-permute-done.20.rest_6_), channel_id=1, source_target_pairs={{0,8},{4,12},{8,0},{12,4},{16,24},{20,28},{24,16},{28,20},{1,9},{5... | collective-permute-start | bytes 1572872 | tf_op jit(solution)/shard_map/ppermute | solution.py:17
  79.8 18.9 %collective-permute-start.23 = (bf16[256,1024]{1,0:T(8,128)(2,1)}, bf16[256,1024]{1,0:T(8,128)(2,1)}, u32[]{:S(2)}, u32[]{:S(2)}) collective-permute-start(bf16[256,1024]{1,0:T(8,128)(2,1)} %collective-permute-done.20.rest_6_), channel_id=1, source_target_pairs={{0,16},{4,20},{8,24},{12,28},{16,0},{20,4},{24,8},{28,12},{1,17},{... | collective-permute-start | bytes 1572872 | tf_op jit(solution)/shard_map/ppermute | solution.py:17
  90.5 6.7 %collective-permute-start.26 = (bf16[128,256]{1,0:T(8,128)(2,1)S(1)}, bf16[128,256]{1,0:T(8,128)(2,1)S(1)}, u32[]{:S(2)}, u32[]{:S(2)}) collective-permute-start(bf16[128,256]{1,0:T(8,128)(2,1)S(1)} %copy-done.25), channel_id=1, source_target_pairs={{0,1},{1,2},{2,3},{3,0},{4,5},{5,6},{6,7},{7,4},{8,9},{9,10},{10,1... | collective-permute-start | bytes 196616 | tf_op jit(solution)/shard_map/ppermute | solution.py:132
  91.2 10.0 %collective-permute-start.29 = (bf16[512,1024]{1,0:T(8,128)(2,1)}, bf16[512,1024]{1,0:T(8,128)(2,1)S(1)}, u32[]{:S(2)}, u32[]{:S(2)}) collective-permute-start(bf16[512,1024]{1,0:T(8,128)(2,1)} %constant_dynamic-update-slice_fusion.rest_5_), channel_id=1, source_target_pairs={{0,4},{4,0},{8,12},{12,8},{16,20},{20,16},{24,28},{28,24},{1,5},{5... | collective-permute-start | bytes 3145736 | tf_op jit(solution)/shard_map/ppermute | solution.py:17
  94.8 16.9 %collective-permute-start.32 = (bf16[128,2048]{1,0:T(8,128)(2,1)}, bf16[128,2048]{1,0:T(8,128)(2,1)S(1)}, u32[]{:S(2)}, u32[]{:S(2)}) collective-permute-start(bf16[128,2048]{1,0:T(8,128)(2,1)} %pad_maximum_fusion.2), channel_id=1, source_target_pairs={{0,1},{1,2},{2,3},{3,0},{4,5},{5,6},{6,7},{7,4},{8,9},{9,10},{10,1... | collective-permute-start | bytes 1572872 | tf_op jit(solution)/shard_map/ppermute | solution.py:132
  97.1 25.4 %collective-permute-start.31 = (bf16[128,2048]{1,0:T(8,128)(2,1)}, bf16[128,2048]{1,0:T(8,128)(2,1)}, u32[]{:S(2)}, u32[]{:S(2)}) collective-permute-start(bf16[128,2048]{1,0:T(8,128)(2,1)} %pad_maximum_fusion.1), channel_id=1, source_target_pairs={{0,3},{1,0},{2,1},{3,2},{4,7},{5,4},{6,5},{7,6},{8,11},{9,8},{10,9... | collective-permute-start | bytes 1572872 | tf_op jit(solution)/shard_map/ppermute | solution.py:132
  99.9 22.7 %collective-permute-start.27 = (bf16[2,128,1024]{2,1,0:T(8,128)(2,1)}, bf16[2,128,1024]{2,1,0:T(8,128)(2,1)}, u32[]{:S(2)}, u32[]{:S(2)}) collective-permute-start(bf16[2,128,1024]{2,1,0:T(8,128)(2,1)} %slice_bitcast_fusion.5), channel_id=1, source_target_pairs={{0,8},{4,12},{8,0},{12,4},{16,24},{20,28},{24,16},{28,20},{1,9},{5... | collective-permute-start | bytes 1572872 | tf_op jit(solution)/shard_map/ppermute | solution.py:17
  101.3 21.8 %collective-permute-start.28 = (bf16[2,128,1024]{2,1,0:T(8,128)(2,1)}, bf16[2,128,1024]{2,1,0:T(8,128)(2,1)}, u32[]{:S(2)}, u32[]{:S(2)}) collective-permute-start(bf16[2,128,1024]{2,1,0:T(8,128)(2,1)} %slice_bitcast_fusion.4), channel_id=1, source_target_pairs={{0,16},{4,20},{8,24},{12,28},{16,0},{20,4},{24,8},{28,12},{1,17},{... | collective-permute-start | bytes 1572872 | tf_op jit(solution)/shard_map/ppermute | solution.py:17
  104.8 23.4 %collective-permute-start.35 = (bf16[512,1024]{1,0:T(8,128)(2,1)}, bf16[512,1024]{1,0:T(8,128)(2,1)}, u32[]{:S(2)}, u32[]{:S(2)}) collective-permute-start(bf16[512,1024]{1,0:T(8,128)(2,1)} %collective-permute-done.16.rest_5_), channel_id=1, source_target_pairs={{0,4},{4,0},{8,12},{12,8},{16,20},{20,16},{24,28},{28,24},{1,5},{5... | collective-permute-start | bytes 3145736 | tf_op jit(solution)/shard_map/ppermute | solution.py:17
  111.7 17.0 %collective-permute-start.37 = (bf16[512,1024]{1,0:T(8,128)(2,1)}, bf16[512,1024]{1,0:T(8,128)(2,1)}, u32[]{:S(2)}, u32[]{:S(2)}) collective-permute-start(bf16[512,1024]{1,0:T(8,128)(2,1)} %collective-permute-done.17.rest_13_), channel_id=1, source_target_pairs={{0,4},{4,0},{8,12},{12,8},{16,20},{20,16},{24,28},{28,24},{1,5},{5... | collective-permute-start | bytes 3145736 | tf_op jit(solution)/shard_map/ppermute | solution.py:17
  122.5 6.2 %collective-permute-start.36 = (bf16[256,1024]{1,0:T(8,128)(2,1)}, bf16[256,1024]{1,0:T(8,128)(2,1)}, u32[]{:S(2)}, u32[]{:S(2)}) collective-permute-start(bf16[256,1024]{1,0:T(8,128)(2,1)} %collective-permute-done.22.rest_6_), channel_id=1, source_target_pairs={{0,4},{4,0},{8,12},{12,8},{16,20},{20,16},{24,28},{28,24},{1,5},{5... | collective-permute-start | bytes 1572872 | tf_op jit(solution)/shard_map/ppermute | solution.py:17
  122.6 6.1 %collective-permute-start.38 = (bf16[256,1024]{1,0:T(8,128)(2,1)}, bf16[256,1024]{1,0:T(8,128)(2,1)}, u32[]{:S(2)}, u32[]{:S(2)}) collective-permute-start(bf16[256,1024]{1,0:T(8,128)(2,1)} %collective-permute-done.23.rest_14_), channel_id=1, source_target_pairs={{0,4},{4,0},{8,12},{12,8},{16,20},{20,16},{24,28},{28,24},{1,5},{5... | collective-permute-start | bytes 1572872 | tf_op jit(solution)/shard_map/ppermute | solution.py:17
  125.4 11.8 %collective-permute-start.33 = (bf16[128,1024]{1,0:T(8,128)(2,1)}, bf16[128,1024]{1,0:T(8,128)(2,1)S(1)}, u32[]{:S(2)}, u32[]{:S(2)}) collective-permute-start(bf16[128,1024]{1,0:T(8,128)(2,1)} %fusion.6), channel_id=1, source_target_pairs={{0,16},{4,20},{8,24},{12,28},{16,0},{20,4},{24,8},{28,12},{1,17},{... | collective-permute-start | bytes 786440 | tf_op jit(solution)/shard_map/ppermute | solution.py:17
  128.2 9.0 %collective-permute-start.34 = (bf16[128,1024]{1,0:T(8,128)(2,1)}, bf16[128,1024]{1,0:T(8,128)(2,1)S(1)}, u32[]{:S(2)}, u32[]{:S(2)}) collective-permute-start(bf16[128,1024]{1,0:T(8,128)(2,1)} %fusion.7), channel_id=1, source_target_pairs={{0,8},{4,12},{8,0},{12,4},{16,24},{20,28},{24,16},{28,20},{1,9},{5... | collective-permute-start | bytes 786440 | tf_op jit(solution)/shard_map/ppermute | solution.py:17
  (36 other events, 331.4 us)

commit v7 on v6

--- a/solution.py
+++ b/solution.py
@@ -304,12 +304,13 @@
             sides[at] = halve(sides[at], axis, bits[b], n_dp)
         if step == count - 1:
             input_grad = hidden_grad(*d_all, linked, input_grad)
+        kept = [stay for stay, came in sides]
+        came = [came for stay, came in sides]
         if step == count - 2:
-            due = (sides, input_grad, from_ahead, from_behind)
-            sides, input_grad, from_ahead, from_behind = lax.optimization_barrier(due)
-        else:
-            sides, input_grad = lax.optimization_barrier((sides, input_grad))
-        sides = [stay + came.astype(F32) for stay, came in sides]
+            came, input_grad, from_ahead = lax.optimization_barrier((came, input_grad, from_ahead))
+        elif step == count - 1:
+            came, input_grad, from_behind = lax.optimization_barrier((came, input_grad, from_behind))
+        sides = [stay + x.astype(F32) for stay, x in zip(kept, came)]
     grad = jnp.concatenate(sides, 0)
     input_grad = add_shares([share[0], from_ahead, from_behind], where, far, width, input_grad)
     w = weight.astype(F32)

time: 152 us -> 142 us (0.934)
  waiting for transfers between devices: 46.3 us -> 36.9 us
  local copies, waits for them, and re-layouts: 15.8 us -> 12.7 us
  starting transfers between devices: 34.9 us -> 37.4 us
    ppermute x10, waiting for transfers between devices: 34.4 us -> 22.1 us  [shift(): lax.ppermute(x, 'tensor', [(i, (i - by) % n_tensor) for i in range(n_tens...]
    squeeze x3 -> x0, local copies, waits for them, and re-layouts: 3.5 us -> none  [halve(): stay = lax.index_in_dim(part, 0, axis, keepdims=False)]
    ppermute x32, waiting for transfers between devices: 11.9 us -> 14.8 us  [swap(): return lax.ppermute(x, 'dp', [(i, i ^ bit) for i in range(n_dp)])]
    ppermute x32, starting transfers between devices: 20.8 us -> 22.3 us  [swap(): return lax.ppermute(x, 'dp', [(i, i ^ bit) for i in range(n_dp)])]
    unnamed x54 -> x58, local copies, waits for them, and re-layouts: 3.5 us -> 3.86 us
    add x4 -> x2, other arithmetic: 3.77 us -> 3.55 us  [local(): sides = [stay + x.astype(F32) for stay, x in zip(kept, came)]]
  transfers between devices with their start and end apart: 42 -> 42, of which waited for: 15 -> 15; matrix products, arithmetic and copies ran while one was open for 14% -> 13% of each run, Pallas kernels for 27% -> 29%
where the time goes in v7:
time: 142 us; the launch traced here: 141 us
  Pallas kernels  41.1 us (29%)
  starting transfers between devices  37.4 us (26%)
  waiting for transfers between devices  36.9 us (26%)
  local copies, waits for them, and re-layouts  12.7 us (9%)
  other arithmetic  12.4 us (9%)
    ppermute x32, starting transfers between devices, swap(): return lax.ppermute(x, 'dp', [(i, i ^ bit) for i in range(n_dp)])  22.3 us
    ppermute x10, waiting for transfers between devices, shift(): lax.ppermute(x, 'tensor', [(i, (i - by) % n_tensor) for i in range(n_tens...  22.1 us
    ppermute x10, starting transfers between devices, shift(): lax.ppermute(x, 'tensor', [(i, (i - by) % n_tensor) for i in range(n_tens...  15 us
    ppermute x32, waiting for transfers between devices, swap(): return lax.ppermute(x, 'dp', [(i, i ^ bit) for i in range(n_dp)])  14.8 us
    pallas_call x2, Pallas kernels, weight_grad(): pl.pallas_call(body, grid_spec=pltpu.PrefetchScalarGridSpec(num_scalar_pr...  12.1 us
    pallas_call x2, Pallas kernels, hidden_grad(): pl.pallas_call(body, grid_spec=pltpu.PrefetchScalarGridSpec(num_scalar_pr...  11.7 us
    pallas_call x1, Pallas kernels, project(): pl.pallas_call(body, grid_spec=pltpu.PrefetchScalarGridSpec(num_scalar_pr...  11 us
    unnamed x58, local copies, waits for them, and re-layouts  3.86 us
  transfers between devices with their start and end apart: 42, of which 15 were waited for; matrix products, arithmetic and copies ran while one was open for 13% of the time, Pallas kernels for 29%

profile of v7, /device:TPU:0, one launch (start us, length us, event | category | flops | bytes accessed | tf_op | source)
XLA Modules:
  0.0 141.4 jit_solution(10643196698851047457)
XLA Ops:
  1.8 3.1 %collective-permute-start.7 = (bf16[128,1024]{1,0:T(8,128)(2,1)S(1)}, bf16[128,1024]{1,0:T(8,128)(2,1)S(1)}, u32[]{:S(2)}, u32[]{:S(2)}) collective-permute-start(bf16[128,1024]{1,0:T(8,128)(2,1)S(1)} %get-tuple-element.80.rest_1_.rest_4_), channel_id=1, source_target_pairs={{0,16},{4,20},{8,24},{12,28},{16,0},{20,4},{24,8},{28,12},{1,17},{... | collective-permute-start | bytes 786440 | tf_op jit(solution)/shard_map/ppermute | solution.py:17
  4.8 1.5 %collective-permute-start.2 = (bf16[128,1024]{1,0:T(8,128)(2,1)S(1)}, bf16[128,1024]{1,0:T(8,128)(2,1)S(1)}, u32[]{:S(2)}, u32[]{:S(2)}) collective-permute-start(bf16[128,1024]{1,0:T(8,128)(2,1)S(1)} %get-tuple-element.81.rest_0_.rest_3_), channel_id=1, source_target_pairs={{0,8},{4,12},{8,0},{12,4},{16,24},{20,28},{24,16},{28,20},{1,9},{5... | collective-permute-start | bytes 786440 | tf_op jit(solution)/shard_map/ppermute | solution.py:17
  6.3 1.6 %collective-permute-start.13 = (bf16[256,1024]{1,0:T(8,128)(2,1)}, bf16[256,1024]{1,0:T(8,128)(2,1)S(1)}, u32[]{:S(2)}, u32[]{:S(2)}) collective-permute-start(bf16[256,1024]{1,0:T(8,128)(2,1)} %param.5), channel_id=1, source_target_pairs={{0,1},{1,2},{2,3},{3,0},{4,5},{5,6},{6,7},{7,4},{8,9},{9,10},{10,1... | collective-permute-start | bytes 1572872 | tf_op jit(solution)/shard_map/ppermute | solution.py:132
  7.9 2.2 %collective-permute-start.12 = (bf16[256,1024]{1,0:T(8,128)(2,1)}, bf16[256,1024]{1,0:T(8,128)(2,1)S(1)}, u32[]{:S(2)}, u32[]{:S(2)}) collective-permute-start(bf16[256,1024]{1,0:T(8,128)(2,1)} %param.5), channel_id=1, source_target_pairs={{0,3},{1,0},{2,1},{3,2},{4,7},{5,4},{6,5},{7,6},{8,11},{9,8},{10,9... | collective-permute-start | bytes 1572872 | tf_op jit(solution)/shard_map/ppermute | solution.py:132
  11.2 1.7 %collective-permute-start.11 = (bf16[128,1024]{1,0:T(8,128)(2,1)S(1)}, bf16[128,1024]{1,0:T(8,128)(2,1)S(1)}, u32[]{:S(2)}, u32[]{:S(2)}) collective-permute-start(bf16[128,1024]{1,0:T(8,128)(2,1)S(1)} %collective-permute-done.7.rest_9_.rest_12_), channel_id=1, source_target_pairs={{0,8},{4,12},{8,0},{12,4},{16,24},{20,28},{24,16},{28,20},{1,9},{5... | collective-permute-start | bytes 786440 | tf_op jit(solution)/shard_map/ppermute | solution.py:17
  12.9 1.5 %collective-permute-start.10 = (bf16[128,1024]{1,0:T(8,128)(2,1)S(1)}, bf16[128,1024]{1,0:T(8,128)(2,1)}, u32[]{:S(2)}, u32[]{:S(2)}) collective-permute-start(bf16[128,1024]{1,0:T(8,128)(2,1)S(1)} %collective-permute-done.2.rest_4_.rest_3_), channel_id=1, source_target_pairs={{0,16},{4,20},{8,24},{12,28},{16,0},{20,4},{24,8},{28,12},{1,17},{... | collective-permute-start | bytes 786440 | tf_op jit(solution)/shard_map/ppermute | solution.py:17
  14.9 5.4 %collective-permute-done.11.rest_13_.rest_1_ = bf16[128,1024]{1,0:T(8,128)(2,1)S(1)} collective-permute-done((bf16[128,1024]{1,0:T(8,128)(2,1)S(1)}, bf16[128,1024]{1,0:T(8,128)(2,1)S(1)}, u32[]{:S(2)}, u32[]{:S(2)}) %collective-permute-start.11) | collective-permute-done | bytes 262176 | tf_op jit(solution)/shard_map/ppermute | solution.py:17
  20.3 1.8 %collective-permute-start.6 = (bf16[128,1024]{1,0:T(8,128)(2,1)S(1)}, bf16[128,1024]{1,0:T(8,128)(2,1)S(1)}, u32[]{:S(2)}, u32[]{:S(2)}) collective-permute-start(bf16[128,1024]{1,0:T(8,128)(2,1)S(1)} %get-tuple-element.81.rest_0_.rest_3_), channel_id=1, source_target_pairs={{0,16},{4,20},{8,24},{12,28},{16,0},{20,4},{24,8},{28,12},{1,17},{... | collective-permute-start | bytes 786440 | tf_op jit(solution)/shard_map/ppermute | solution.py:17
  23.2 9.0 %collective-permute-done.12 = bf16[256,1024]{1,0:T(8,128)(2,1)S(1)} collective-permute-done((bf16[256,1024]{1,0:T(8,128)(2,1)}, bf16[256,1024]{1,0:T(8,128)(2,1)S(1)}, u32[]{:S(2)}, u32[]{:S(2)}) %collective-permute-start.12) | collective-permute-done | bytes 524320 | tf_op jit(solution)/shard_map/ppermute | solution.py:132
  37.4 1.8 %collective-permute-start.20 = (bf16[256,1024]{1,0:T(8,128)(2,1)S(1)}, bf16[256,1024]{1,0:T(8,128)(2,1)}, u32[]{:S(2)}, u32[]{:S(2)}) collective-permute-start(bf16[256,1024]{1,0:T(8,128)(2,1)S(1)} %copy-done.2), channel_id=1, source_target_pairs={{0,2},{1,3},{2,0},{3,1},{4,6},{5,7},{6,4},{7,5},{8,10},{9,11},{10,... | collective-permute-start | bytes 1572872 | tf_op jit(solution)/shard_map/ppermute | solution.py:132
  39.9 11.0 %project.1 = (bf16[512,256]{1,0:T(8,128)(2,1)}, bf16[4,128,256]{2,1,0:T(8,128)(2,1)}, bf16[256,512]{1,0:T(8,128)(2,1)}) custom-call(s32[2]{0:T(128)} %pad_add_fusion.where_ref, bf16[512,8192]{1,0:T(8,128)(2,1)} %h_ref.5, f32[1,128]{1,0:T(1,128)} %s_ref.1, bf16[512,256]{1,0:T(8,128)(2,1)} %c_ref.1, bf16[128,1024]{1,0:T(8,128)(2,1)} %copy-done.8, ...), custom_call_target="tpu_custom_call" | custom-call | tf_op jit(solution)/shard_map/project/pallas_call | solution.py:81
  51.0 3.2 %hidden_share.1 = bf16[4,128,2048]{2,1,0:T(8,128)(2,1)} custom-call(bf16[4,128,256]{2,1,0:T(8,128)(2,1)} %get-tuple-element.39.d_ref, bf16[128,1024]{1,0:T(8,128)(2,1)} %collective-permute-done.10.rest_12_.rest_0_, bf16[128,1024]{1,0:T(8,128)(2,1)} %copy-done.18, bf16[128,1024]{1,0:T(8,128)(2,1)} %collective-permute-done.14.rest_14_.rest_2_, ...), custom_call_target="tpu_custom_call" | custom-call | tf_op jit(solution)/shard_map/hidden_share/pallas_call | solution.py:151
  54.2 2.1 %slice_bitcast_fusion.7 = (bf16[128,1024]{1,0:T(8,128)(2,1)}, bf16[128,1024]{1,0:T(8,128)(2,1)S(1)}, bf16[128,1024]{1,0:T(8,128)(2,1)}, bf16[128,1024]{1,0:T(8,128)(2,1)}) fusion(bf16[4,128,2048]{2,1,0:T(8,128)(2,1)} %hidden_share.1), kind=kLoop, calls=%fused_computation.32 | loop fusion | bytes 2097152 | tf_op jit(solution)/shard_map/squeeze | solution.py:282
  56.3 1.6 %collective-permute-start.19 = (bf16[128,1024]{1,0:T(8,128)(2,1)}, bf16[128,1024]{1,0:T(8,128)(2,1)S(1)}, u32[]{:S(2)}, u32[]{:S(2)}) collective-permute-start(bf16[128,1024]{1,0:T(8,128)(2,1)} %get-tuple-element.76), channel_id=1, source_target_pairs={{0,1},{1,2},{2,3},{3,0},{4,5},{5,6},{6,7},{7,4},{8,9},{9,10},{10,1... | collective-permute-start | bytes 786440 | tf_op jit(solution)/shard_map/ppermute | solution.py:132
  57.8 2.3 %collective-permute-start.18 = (bf16[128,1024]{1,0:T(8,128)(2,1)}, bf16[128,1024]{1,0:T(8,128)(2,1)}, u32[]{:S(2)}, u32[]{:S(2)}) collective-permute-start(bf16[128,1024]{1,0:T(8,128)(2,1)} %get-tuple-element.77), channel_id=1, source_target_pairs={{0,3},{1,0},{2,1},{3,2},{4,7},{5,4},{6,5},{7,6},{8,11},{9,8},{10,9... | collective-permute-start | bytes 786440 | tf_op jit(solution)/shard_map/ppermute | solution.py:132
  60.1 5.7 %weight_grad_odd.1 = bf16[4,256,1024]{2,1,0:T(8,128)(2,1)} custom-call(s32[2]{0:T(128)} %pad_add_fusion.where_ref, bf16[256,512]{1,0:T(8,128)(2,1)} %get-tuple-element.44.d_ref, bf16[512,8192]{1,0:T(8,128)(2,1)} %h_ref.5), custom_call_target="tpu_custom_call" | custom-call | tf_op jit(solution)/shard_map/weight_grad_odd/pallas_call | solution.py:115
  65.8 4.1 %collective-permute-done.20.rest_6_ = bf16[256,1024]{1,0:T(8,128)(2,1)} collective-permute-done((bf16[256,1024]{1,0:T(8,128)(2,1)S(1)}, bf16[256,1024]{1,0:T(8,128)(2,1)}, u32[]{:S(2)}, u32[]{:S(2)}) %collective-permute-start.20) | collective-permute-done | bytes 524320 | tf_op jit(solution)/shard_map/ppermute | solution.py:132
  70.0 4.9 %collective-permute-done.18 = bf16[128,1024]{1,0:T(8,128)(2,1)} collective-permute-done((bf16[128,1024]{1,0:T(8,128)(2,1)}, bf16[128,1024]{1,0:T(8,128)(2,1)}, u32[]{:S(2)}, u32[]{:S(2)}) %collective-permute-start.18) | collective-permute-done | bytes 262176 | tf_op jit(solution)/shard_map/ppermute | solution.py:132
  76.2 2.6 %collective-permute-start.25 = (bf16[128,256]{1,0:T(8,128)(2,1)}, bf16[128,256]{1,0:T(8,128)(2,1)S(1)}, u32[]{:S(2)}, u32[]{:S(2)}) collective-permute-start(bf16[128,256]{1,0:T(8,128)(2,1)} %get-tuple-element.84), channel_id=1, source_target_pairs={{0,2},{1,3},{2,0},{3,1},{4,6},{5,7},{6,4},{7,5},{8,10},{9,11},{10,... | collective-permute-start | bytes 196616 | tf_op jit(solution)/shard_map/ppermute | solution.py:132
  78.9 1.5 %collective-permute-start.23 = (bf16[256,1024]{1,0:T(8,128)(2,1)}, bf16[256,1024]{1,0:T(8,128)(2,1)S(1)}, u32[]{:S(2)}, u32[]{:S(2)}) collective-permute-start(bf16[256,1024]{1,0:T(8,128)(2,1)} %collective-permute-done.20.rest_6_), channel_id=1, source_target_pairs={{0,16},{4,20},{8,24},{12,28},{16,0},{20,4},{24,8},{28,12},{1,17},{... | collective-permute-start | bytes 1572872 | tf_op jit(solution)/shard_map/ppermute | solution.py:17
  83.7 6.4 %weight_grad_even.1 = f32[4,256,1024]{2,1,0:T(8,128)} custom-call(s32[2]{0:T(128)} %pad_add_fusion.where_ref, bf16[256,512]{1,0:T(8,128)(2,1)} %get-tuple-element.44.d_ref, bf16[512,8192]{1,0:T(8,128)(2,1)} %h_ref.5), custom_call_target="tpu_custom_call" | custom-call | tf_op jit(solution)/shard_map/weight_grad_even/pallas_call | solution.py:115
  90.1 1.6 %collective-permute-start.24 = (bf16[128,256]{1,0:T(8,128)(2,1)S(1)}, bf16[128,256]{1,0:T(8,128)(2,1)S(1)}, u32[]{:S(2)}, u32[]{:S(2)}) collective-permute-start(bf16[128,256]{1,0:T(8,128)(2,1)S(1)} %copy-done.27), channel_id=1, source_target_pairs={{0,3},{1,0},{2,1},{3,2},{4,7},{5,4},{6,5},{7,6},{8,11},{9,8},{10,9... | collective-permute-start | bytes 196616 | tf_op jit(solution)/shard_map/ppermute | solution.py:132
  91.7 3.6 %convert_add_fusion = f32[4,256,1024]{2,1,0:T(8,128)S(1)} fusion(f32[4,256,1024]{2,1,0:T(8,128)} %weight_grad_even.1, bf16[4,256,1024]{2,1,0:T(8,128)(2,1)} %collective-permute-done.21), kind=kLoop, calls=%fused_computation | loop fusion | flops 2097152 | bytes 10485760 | tf_op jit(solution)/shard_map/add | solution.py:288
  102.4 4.6 %hidden_grad.2.rest_19_ = bf16[128,8192]{1,0:T(8,128)(2,1)} custom-call(s32[2]{0:T(128)} %pad_add_fusion.where_ref, bf16[128,256]{1,0:T(8,128)(2,1)} %get-tuple-element.82.rest_0_, bf16[128,512]{1,0:T(8,128)(2,1)} %copy-done.22, bf16[128,256]{1,0:T(8,128)(2,1)} %copy-done.25, bf16[128,1024]{1,0:T(8,128)(2,1)} %copy-done.8, bf16[128,1024]{1,0:T(8,128)(2,1)} %copy-done.7, ...), custom_call_target="tpu_custom_call" | custom-call | tf_op jit(solution)/shard_map/hidden_grad/pallas_call | solution.py:201
  107.0 3.0 %collective-permute-done.31.rest_1_ = bf16[128,2048]{1,0:T(8,128)(2,1)} collective-permute-done((bf16[128,2048]{1,0:T(8,128)(2,1)}, bf16[128,2048]{1,0:T(8,128)(2,1)}, u32[]{:S(2)}, u32[]{:S(2)}) %collective-permute-start.31) | collective-permute-done | bytes 524320 | tf_op jit(solution)/shard_map/ppermute | solution.py:132
  110.5 2.5 %collective-permute-done.27 = bf16[2,128,1024]{2,1,0:T(8,128)(2,1)} collective-permute-done((bf16[2,128,1024]{2,1,0:T(8,128)(2,1)}, bf16[2,128,1024]{2,1,0:T(8,128)(2,1)}, u32[]{:S(2)}, u32[]{:S(2)}) %collective-permute-start.27) | collective-permute-done | bytes 524320 | tf_op jit(solution)/shard_map/ppermute | solution.py:17
  114.2 2.1 %fusion.6 = (f32[2,128,1024]{2,1,0:T(8,128)S(1)}, f32[2,128,1024]{2,1,0:T(8,128)S(1)}) fusion(f32[2,2,256,1024]{3,2,1,0:T(8,128)} %bitcast.58, bf16[2,128,1024]{2,1,0:T(8,128)(2,1)} %collective-permute-done.28, bf16[2,128,1024]{2,1,0:T(8,128)(2,1)} %collective-permute-done.27), kind=kLoop, calls=%fused_computation.12 | loop fusion | flops 1048576 | bytes 5242880 | tf_op jit(solution)/shard_map/add | solution.py:313
  120.7 7.1 %hidden_grad.3.rest_3_ = bf16[128,8192]{1,0:T(8,128)(2,1)} custom-call(s32[2]{0:T(128)} %pad_add_fusion.where_ref, bf16[128,256]{1,0:T(8,128)(2,1)} %get-tuple-element.82.rest_0_, bf16[128,512]{1,0:T(8,128)(2,1)} %copy-done.22, bf16[128,256]{1,0:T(8,128)(2,1)} %copy-done.25, bf16[128,1024]{1,0:T(8,128)(2,1)} %copy-done.11, ...), custom_call_target="tpu_custom_call", output_to_operand_aliasing={{}: (20, {})} | custom-call | tf_op jit(solution)/shard_map/hidden_grad/pallas_call | solution.py:201
  131.1 1.5 %collective-permute-start.40 = (f32[3,256]{1,0:T(4,128)S(1)}, f32[3,256]{1,0:T(4,128)S(1)}, u32[]{:S(2)}, u32[]{:S(2)}) collective-permute-start(f32[3,256]{1,0:T(4,128)S(1)} %fusion.12), channel_id=1, source_target_pairs={{0,8},{4,12},{8,0},{12,4},{16,24},{20,28},{24,16},{28,20},{1,9},{5... | collective-permute-start | bytes 9224 | tf_op jit(solution)/shard_map/ppermute | solution.py:17
  132.6 2.2 %collective-permute-done.40 = f32[3,256]{1,0:T(4,128)S(1)} collective-permute-done((f32[3,256]{1,0:T(4,128)S(1)}, f32[3,256]{1,0:T(4,128)S(1)}, u32[]{:S(2)}, u32[]{:S(2)}) %collective-permute-start.40) | collective-permute-done | bytes 3104 | tf_op jit(solution)/shard_map/ppermute | solution.py:17
  134.8 1.6 %collective-permute-start.41 = (f32[3,256]{1,0:T(4,128)S(1)}, f32[3,256]{1,0:T(4,128)S(1)}, u32[]{:S(2)}, u32[]{:S(2)}) collective-permute-start(f32[3,256]{1,0:T(4,128)S(1)} %fusion.15), channel_id=1, source_target_pairs={{0,16},{4,20},{8,24},{12,28},{16,0},{20,4},{24,8},{28,12},{1,17},{... | collective-permute-start | bytes 9224 | tf_op jit(solution)/shard_map/ppermute | solution.py:17
  137.3 3.0 %add_shares.1 = bf16[128,8192]{1,0:T(8,128)(2,1)} custom-call(s32[2]{0:T(128)} %pad_add_fusion.where_ref, bf16[128,2048]{1,0:T(8,128)(2,1)} %slice_bitcast_fusion.6.rest_0_, bf16[128,2048]{1,0:T(8,128)(2,1)} %collective-permute-done.31.rest_1_, bf16[128,2048]{1,0:T(8,128)(2,1)} %collective-permute-done.38.rest_2_, ...), custom_call_target="tpu_custom_call", output_to_operand_aliasing={{}: (4, {})} | custom-call | tf_op jit(solution)/shard_map/add_shares/pallas_call | solution.py:230
  (143 shorter events, 32.7 us)
Async XLA Ops:
  1.8 9.4 %collective-permute-start.7 = (bf16[128,1024]{1,0:T(8,128)(2,1)S(1)}, bf16[128,1024]{1,0:T(8,128)(2,1)S(1)}, u32[]{:S(2)}, u32[]{:S(2)}) collective-permute-start(bf16[128,1024]{1,0:T(8,128)(2,1)S(1)} %get-tuple-element.80.rest_1_.rest_4_), channel_id=1, source_target_pairs={{0,16},{4,20},{8,24},{12,28},{16,0},{20,4},{24,8},{28,12},{1,17},{... | collective-permute-start | bytes 786440 | tf_op jit(solution)/shard_map/ppermute | solution.py:17
  4.8 8.0 %collective-permute-start.2 = (bf16[128,1024]{1,0:T(8,128)(2,1)S(1)}, bf16[128,1024]{1,0:T(8,128)(2,1)S(1)}, u32[]{:S(2)}, u32[]{:S(2)}) collective-permute-start(bf16[128,1024]{1,0:T(8,128)(2,1)S(1)} %get-tuple-element.81.rest_0_.rest_3_), channel_id=1, source_target_pairs={{0,8},{4,12},{8,0},{12,4},{16,24},{20,28},{24,16},{28,20},{1,9},{5... | collective-permute-start | bytes 786440 | tf_op jit(solution)/shard_map/ppermute | solution.py:17
  6.3 16.8 %collective-permute-start.13 = (bf16[256,1024]{1,0:T(8,128)(2,1)}, bf16[256,1024]{1,0:T(8,128)(2,1)S(1)}, u32[]{:S(2)}, u32[]{:S(2)}) collective-permute-start(bf16[256,1024]{1,0:T(8,128)(2,1)} %param.5), channel_id=1, source_target_pairs={{0,1},{1,2},{2,3},{3,0},{4,5},{5,6},{6,7},{7,4},{8,9},{9,10},{10,1... | collective-permute-start | bytes 1572872 | tf_op jit(solution)/shard_map/ppermute | solution.py:132
  7.9 24.3 %collective-permute-start.12 = (bf16[256,1024]{1,0:T(8,128)(2,1)}, bf16[256,1024]{1,0:T(8,128)(2,1)S(1)}, u32[]{:S(2)}, u32[]{:S(2)}) collective-permute-start(bf16[256,1024]{1,0:T(8,128)(2,1)} %param.5), channel_id=1, source_target_pairs={{0,3},{1,0},{2,1},{3,2},{4,7},{5,4},{6,5},{7,6},{8,11},{9,8},{10,9... | collective-permute-start | bytes 1572872 | tf_op jit(solution)/shard_map/ppermute | solution.py:132
  11.2 9.2 %collective-permute-start.11 = (bf16[128,1024]{1,0:T(8,128)(2,1)S(1)}, bf16[128,1024]{1,0:T(8,128)(2,1)S(1)}, u32[]{:S(2)}, u32[]{:S(2)}) collective-permute-start(bf16[128,1024]{1,0:T(8,128)(2,1)S(1)} %collective-permute-done.7.rest_9_.rest_12_), channel_id=1, source_target_pairs={{0,8},{4,12},{8,0},{12,4},{16,24},{20,28},{24,16},{28,20},{1,9},{5... | collective-permute-start | bytes 786440 | tf_op jit(solution)/shard_map/ppermute | solution.py:17
  12.9 7.5 %collective-permute-start.10 = (bf16[128,1024]{1,0:T(8,128)(2,1)S(1)}, bf16[128,1024]{1,0:T(8,128)(2,1)}, u32[]{:S(2)}, u32[]{:S(2)}) collective-permute-start(bf16[128,1024]{1,0:T(8,128)(2,1)S(1)} %collective-permute-done.2.rest_4_.rest_3_), channel_id=1, source_target_pairs={{0,16},{4,20},{8,24},{12,28},{16,0},{20,4},{24,8},{28,12},{1,17},{... | collective-permute-start | bytes 786440 | tf_op jit(solution)/shard_map/ppermute | solution.py:17
  14.4 19.5 %collective-permute-start.3 = (bf16[128,1024]{1,0:T(8,128)(2,1)S(1)}, bf16[128,1024]{1,0:T(8,128)(2,1)S(1)}, u32[]{:S(2)}, u32[]{:S(2)}) collective-permute-start(bf16[128,1024]{1,0:T(8,128)(2,1)S(1)} %get-tuple-element.80.rest_1_.rest_4_), channel_id=1, source_target_pairs={{0,8},{4,12},{8,0},{12,4},{16,24},{20,28},{24,16},{28,20},{1,9},{5... | collective-permute-start | bytes 786440 | tf_op jit(solution)/shard_map/ppermute | solution.py:17
  20.3 14.0 %collective-permute-start.1 = (bf16[128,1024]{1,0:T(8,128)(2,1)S(1)}, bf16[128,1024]{1,0:T(8,128)(2,1)S(1)}, u32[]{:S(2)}, u32[]{:S(2)}) collective-permute-start(bf16[128,1024]{1,0:T(8,128)(2,1)S(1)} %get-tuple-element.80.rest_1_.rest_4_), channel_id=1, source_target_pairs={{0,4},{4,0},{8,12},{12,8},{16,20},{20,16},{24,28},{28,24},{1,5},{5... | collective-permute-start | bytes 786440 | tf_op jit(solution)/shard_map/ppermute | solution.py:17
  20.3 14.7 %collective-permute-start.6 = (bf16[128,1024]{1,0:T(8,128)(2,1)S(1)}, bf16[128,1024]{1,0:T(8,128)(2,1)S(1)}, u32[]{:S(2)}, u32[]{:S(2)}) collective-permute-start(bf16[128,1024]{1,0:T(8,128)(2,1)S(1)} %get-tuple-element.81.rest_0_.rest_3_), channel_id=1, source_target_pairs={{0,16},{4,20},{8,24},{12,28},{16,0},{20,4},{24,8},{28,12},{1,17},{... | collective-permute-start | bytes 786440 | tf_op jit(solution)/shard_map/ppermute | solution.py:17
  23.2 12.1 %collective-permute-start = (bf16[128,1024]{1,0:T(8,128)(2,1)S(1)}, bf16[128,1024]{1,0:T(8,128)(2,1)}, u32[]{:S(2)}, u32[]{:S(2)}) collective-permute-start(bf16[128,1024]{1,0:T(8,128)(2,1)S(1)} %get-tuple-element.81.rest_0_.rest_3_), channel_id=1, source_target_pairs={{0,4},{4,0},{8,12},{12,8},{16,20},{20,16},{24,28},{28,24},{1,5},{5... | collective-permute-start | bytes 786440 | tf_op jit(solution)/shard_map/ppermute | solution.py:17
  33.9 41.0 %collective-permute-start.17 = (bf16[512,1024]{1,0:T(8,128)(2,1)}, bf16[512,1024]{1,0:T(8,128)(2,1)}, u32[]{:S(2)}, u32[]{:S(2)}) collective-permute-start(bf16[512,1024]{1,0:T(8,128)(2,1)} %constant_dynamic-update-slice_fusion.rest_5_), channel_id=1, source_target_pairs={{0,16},{4,20},{8,24},{12,28},{16,0},{20,4},{24,8},{28,12},{1,17},{... | collective-permute-start | bytes 3145736 | tf_op jit(solution)/shard_map/ppermute | solution.py:17
  34.4 40.5 %collective-permute-start.16 = (bf16[512,1024]{1,0:T(8,128)(2,1)}, bf16[512,1024]{1,0:T(8,128)(2,1)}, u32[]{:S(2)}, u32[]{:S(2)}) collective-permute-start(bf16[512,1024]{1,0:T(8,128)(2,1)} %constant_dynamic-update-slice_fusion.rest_5_), channel_id=1, source_target_pairs={{0,8},{4,12},{8,0},{12,4},{16,24},{20,28},{24,16},{28,20},{1,9},{5... | collective-permute-start | bytes 3145736 | tf_op jit(solution)/shard_map/ppermute | solution.py:17
  37.4 32.6 %collective-permute-start.20 = (bf16[256,1024]{1,0:T(8,128)(2,1)S(1)}, bf16[256,1024]{1,0:T(8,128)(2,1)}, u32[]{:S(2)}, u32[]{:S(2)}) collective-permute-start(bf16[256,1024]{1,0:T(8,128)(2,1)S(1)} %copy-done.2), channel_id=1, source_target_pairs={{0,2},{1,3},{2,0},{3,1},{4,6},{5,7},{6,4},{7,5},{8,10},{9,11},{10,... | collective-permute-start | bytes 1572872 | tf_op jit(solution)/shard_map/ppermute | solution.py:132
  56.3 13.7 %collective-permute-start.19 = (bf16[128,1024]{1,0:T(8,128)(2,1)}, bf16[128,1024]{1,0:T(8,128)(2,1)S(1)}, u32[]{:S(2)}, u32[]{:S(2)}) collective-permute-start(bf16[128,1024]{1,0:T(8,128)(2,1)} %get-tuple-element.76), channel_id=1, source_target_pairs={{0,1},{1,2},{2,3},{3,0},{4,5},{5,6},{6,7},{7,4},{8,9},{9,10},{10,1... | collective-permute-start | bytes 786440 | tf_op jit(solution)/shard_map/ppermute | solution.py:132
  57.8 17.0 %collective-permute-start.18 = (bf16[128,1024]{1,0:T(8,128)(2,1)}, bf16[128,1024]{1,0:T(8,128)(2,1)}, u32[]{:S(2)}, u32[]{:S(2)}) collective-permute-start(bf16[128,1024]{1,0:T(8,128)(2,1)} %get-tuple-element.77), channel_id=1, source_target_pairs={{0,3},{1,0},{2,1},{3,2},{4,7},{5,4},{6,5},{7,6},{8,11},{9,8},{10,9... | collective-permute-start | bytes 786440 | tf_op jit(solution)/shard_map/ppermute | solution.py:132
  74.9 16.8 %collective-permute-start.21 = (bf16[4,256,1024]{2,1,0:T(8,128)(2,1)}, bf16[4,256,1024]{2,1,0:T(8,128)(2,1)}, u32[]{:S(2)}, u32[]{:S(2)}) collective-permute-start(bf16[4,256,1024]{2,1,0:T(8,128)(2,1)} %weight_grad_odd.1), channel_id=1, source_target_pairs={{0,4},{4,0},{8,12},{12,8},{16,20},{20,16},{24,28},{28,24},{1,5},{5... | collective-permute-start | bytes 6291464 | tf_op jit(solution)/shard_map/ppermute | solution.py:17
  75.6 14.5 %collective-permute-start.26 = (bf16[128,256]{1,0:T(8,128)(2,1)}, bf16[128,256]{1,0:T(8,128)(2,1)S(1)}, u32[]{:S(2)}, u32[]{:S(2)}) collective-permute-start(bf16[128,256]{1,0:T(8,128)(2,1)} %get-tuple-element.83), channel_id=1, source_target_pairs={{0,1},{1,2},{2,3},{3,0},{4,5},{5,6},{6,7},{7,4},{8,9},{9,10},{10,1... | collective-permute-start | bytes 196616 | tf_op jit(solution)/shard_map/ppermute | solution.py:132
  76.2 19.0 %collective-permute-start.25 = (bf16[128,256]{1,0:T(8,128)(2,1)}, bf16[128,256]{1,0:T(8,128)(2,1)S(1)}, u32[]{:S(2)}, u32[]{:S(2)}) collective-permute-start(bf16[128,256]{1,0:T(8,128)(2,1)} %get-tuple-element.84), channel_id=1, source_target_pairs={{0,2},{1,3},{2,0},{3,1},{4,6},{5,7},{6,4},{7,5},{8,10},{9,11},{10,... | collective-permute-start | bytes 196616 | tf_op jit(solution)/shard_map/ppermute | solution.py:132
  78.9 16.7 %collective-permute-start.23 = (bf16[256,1024]{1,0:T(8,128)(2,1)}, bf16[256,1024]{1,0:T(8,128)(2,1)S(1)}, u32[]{:S(2)}, u32[]{:S(2)}) collective-permute-start(bf16[256,1024]{1,0:T(8,128)(2,1)} %collective-permute-done.20.rest_6_), channel_id=1, source_target_pairs={{0,16},{4,20},{8,24},{12,28},{16,0},{20,4},{24,8},{28,12},{1,17},{... | collective-permute-start | bytes 1572872 | tf_op jit(solution)/shard_map/ppermute | solution.py:17
  80.4 15.2 %collective-permute-start.22 = (bf16[256,1024]{1,0:T(8,128)(2,1)}, bf16[256,1024]{1,0:T(8,128)(2,1)}, u32[]{:S(2)}, u32[]{:S(2)}) collective-permute-start(bf16[256,1024]{1,0:T(8,128)(2,1)} %collective-permute-done.20.rest_6_), channel_id=1, source_target_pairs={{0,8},{4,12},{8,0},{12,4},{16,24},{20,28},{24,16},{28,20},{1,9},{5... | collective-permute-start | bytes 1572872 | tf_op jit(solution)/shard_map/ppermute | solution.py:17
  90.1 5.4 %collective-permute-start.24 = (bf16[128,256]{1,0:T(8,128)(2,1)S(1)}, bf16[128,256]{1,0:T(8,128)(2,1)S(1)}, u32[]{:S(2)}, u32[]{:S(2)}) collective-permute-start(bf16[128,256]{1,0:T(8,128)(2,1)S(1)} %copy-done.27), channel_id=1, source_target_pairs={{0,3},{1,0},{2,1},{3,2},{4,7},{5,4},{6,5},{7,6},{8,11},{9,8},{10,9... | collective-permute-start | bytes 196616 | tf_op jit(solution)/shard_map/ppermute | solution.py:132
  91.7 8.6 %collective-permute-start.29 = (bf16[512,1024]{1,0:T(8,128)(2,1)}, bf16[512,1024]{1,0:T(8,128)(2,1)}, u32[]{:S(2)}, u32[]{:S(2)}) collective-permute-start(bf16[512,1024]{1,0:T(8,128)(2,1)} %constant_dynamic-update-slice_fusion.rest_5_), channel_id=1, source_target_pairs={{0,4},{4,0},{8,12},{12,8},{16,20},{20,16},{24,28},{28,24},{1,5},{5... | collective-permute-start | bytes 3145736 | tf_op jit(solution)/shard_map/ppermute | solution.py:17
  95.3 14.7 %collective-permute-start.31 = (bf16[128,2048]{1,0:T(8,128)(2,1)}, bf16[128,2048]{1,0:T(8,128)(2,1)}, u32[]{:S(2)}, u32[]{:S(2)}) collective-permute-start(bf16[128,2048]{1,0:T(8,128)(2,1)} %pad_maximum_fusion.1), channel_id=1, source_target_pairs={{0,3},{1,0},{2,1},{3,2},{4,7},{5,4},{6,5},{7,6},{8,11},{9,8},{10,9... | collective-permute-start | bytes 1572872 | tf_op jit(solution)/shard_map/ppermute | solution.py:132
  98.3 14.7 %collective-permute-start.27 = (bf16[2,128,1024]{2,1,0:T(8,128)(2,1)}, bf16[2,128,1024]{2,1,0:T(8,128)(2,1)}, u32[]{:S(2)}, u32[]{:S(2)}) collective-permute-start(bf16[2,128,1024]{2,1,0:T(8,128)(2,1)} %slice_bitcast_fusion.5), channel_id=1, source_target_pairs={{0,8},{4,12},{8,0},{12,4},{16,24},{20,28},{24,16},{28,20},{1,9},{5... | collective-permute-start | bytes 1572872 | tf_op jit(solution)/shard_map/ppermute | solution.py:17
  99.8 14.4 %collective-permute-start.28 = (bf16[2,128,1024]{2,1,0:T(8,128)(2,1)}, bf16[2,128,1024]{2,1,0:T(8,128)(2,1)}, u32[]{:S(2)}, u32[]{:S(2)}) collective-permute-start(bf16[2,128,1024]{2,1,0:T(8,128)(2,1)} %slice_bitcast_fusion.4), channel_id=1, source_target_pairs={{0,16},{4,20},{8,24},{12,28},{16,0},{20,4},{24,8},{28,12},{1,17},{... | collective-permute-start | bytes 1572872 | tf_op jit(solution)/shard_map/ppermute | solution.py:17
  100.3 18.5 %collective-permute-start.34 = (bf16[512,1024]{1,0:T(8,128)(2,1)}, bf16[512,1024]{1,0:T(8,128)(2,1)S(1)}, u32[]{:S(2)}, u32[]{:S(2)}) collective-permute-start(bf16[512,1024]{1,0:T(8,128)(2,1)} %collective-permute-done.16.rest_5_), channel_id=1, source_target_pairs={{0,4},{4,0},{8,12},{12,8},{16,20},{20,16},{24,28},{28,24},{1,5},{5... | collective-permute-start | bytes 3145736 | tf_op jit(solution)/shard_map/ppermute | solution.py:17
  100.3 19.0 %collective-permute-start.36 = (bf16[512,1024]{1,0:T(8,128)(2,1)}, bf16[512,1024]{1,0:T(8,128)(2,1)}, u32[]{:S(2)}, u32[]{:S(2)}) collective-permute-start(bf16[512,1024]{1,0:T(8,128)(2,1)} %collective-permute-done.17.rest_13_), channel_id=1, source_target_pairs={{0,4},{4,0},{8,12},{12,8},{16,20},{20,16},{24,28},{28,24},{1,5},{5... | collective-permute-start | bytes 3145736 | tf_op jit(solution)/shard_map/ppermute | solution.py:17
  110.0 17.9 %collective-permute-start.38 = (bf16[128,2048]{1,0:T(8,128)(2,1)}, bf16[128,2048]{1,0:T(8,128)(2,1)}, u32[]{:S(2)}, u32[]{:S(2)}) collective-permute-start(bf16[128,2048]{1,0:T(8,128)(2,1)} %pad_maximum_fusion.2), channel_id=1, source_target_pairs={{0,1},{1,2},{2,3},{3,0},{4,5},{5,6},{6,7},{7,4},{8,9},{9,10},{10,1... | collective-permute-start | bytes 1572872 | tf_op jit(solution)/shard_map/ppermute | solution.py:132
  113.0 7.8 %collective-permute-start.35 = (bf16[256,1024]{1,0:T(8,128)(2,1)}, bf16[256,1024]{1,0:T(8,128)(2,1)}, u32[]{:S(2)}, u32[]{:S(2)}) collective-permute-start(bf16[256,1024]{1,0:T(8,128)(2,1)} %collective-permute-done.22.rest_6_), channel_id=1, source_target_pairs={{0,4},{4,0},{8,12},{12,8},{16,20},{20,16},{24,28},{28,24},{1,5},{5... | collective-permute-start | bytes 1572872 | tf_op jit(solution)/shard_map/ppermute | solution.py:17
  114.2 6.5 %collective-permute-start.37 = (bf16[256,1024]{1,0:T(8,128)(2,1)}, bf16[256,1024]{1,0:T(8,128)(2,1)}, u32[]{:S(2)}, u32[]{:S(2)}) collective-permute-start(bf16[256,1024]{1,0:T(8,128)(2,1)} %copy-done.23), channel_id=1, source_target_pairs={{0,4},{4,0},{8,12},{12,8},{16,20},{20,16},{24,28},{28,24},{1,5},{5... | collective-permute-start | bytes 1572872 | tf_op jit(solution)/shard_map/ppermute | solution.py:17
  118.8 9.1 %collective-permute-start.32 = (bf16[128,1024]{1,0:T(8,128)(2,1)}, bf16[128,1024]{1,0:T(8,128)(2,1)S(1)}, u32[]{:S(2)}, u32[]{:S(2)}) collective-permute-start(bf16[128,1024]{1,0:T(8,128)(2,1)} %fusion.10), channel_id=1, source_target_pairs={{0,16},{4,20},{8,24},{12,28},{16,0},{20,4},{24,8},{28,12},{1,17},{... | collective-permute-start | bytes 786440 | tf_op jit(solution)/shard_map/ppermute | solution.py:17
  119.3 8.8 %collective-permute-start.33 = (bf16[128,1024]{1,0:T(8,128)(2,1)}, bf16[128,1024]{1,0:T(8,128)(2,1)}, u32[]{:S(2)}, u32[]{:S(2)}) collective-permute-start(bf16[128,1024]{1,0:T(8,128)(2,1)} %fusion.11), channel_id=1, source_target_pairs={{0,8},{4,12},{8,0},{12,4},{16,24},{20,28},{24,16},{28,20},{1,9},{5... | collective-permute-start | bytes 786440 | tf_op jit(solution)/shard_map/ppermute | solution.py:17
  (38 other events, 320.6 us)

commit v8 on v7

--- a/solution.py
+++ b/solution.py
@@ -276,15 +276,15 @@
     via_ahead = shift(share[2, :, :cut], 1, n_tensor)
     via_behind = shift(share[2, :, cut:], -1, n_tensor)
     sent = weight_grad(d_t, hidden, where, n_dp, 1, BF16)
-    due = (d_t, sent, pair, via_ahead, via_behind, across)
-    d_t, sent, pair, via_ahead, via_behind, across = lax.optimization_barrier(due)
-    to_ahead = jnp.concatenate([share[1, :, :cut] + via_ahead, share[1, :, cut:]], 1)
-    to_behind = jnp.concatenate([share[-1, :, :cut], share[-1, :, cut:] + via_behind], 1)
-    from_ahead, from_behind = shift(to_ahead, 1, n_tensor), shift(to_behind, -1, n_tensor)
+    d_t, sent, pair, across = lax.optimization_barrier((d_t, sent, pair, across))
     mid = {0: across}
     mid.update({bit: swap(mid[0], bit, n_dp) for bit in bits})
     pair = add_core(pair, n_dp)
     keep = weight_grad(d_t, hidden, where, n_dp, 0, F32)
+    keep, via_ahead, via_behind = lax.optimization_barrier((keep, via_ahead, via_behind))
+    to_ahead = jnp.concatenate([share[1, :, :cut] + via_ahead, share[1, :, cut:]], 1)
+    to_behind = jnp.concatenate([share[-1, :, :cut], share[-1, :, cut:] + via_behind], 1)
+    from_ahead, from_behind = shift(to_ahead, 1, n_tensor), shift(to_behind, -1, n_tensor)
     total = keep + swap(sent, 1, n_dp).astype(F32)
     total, mid, d_rest = lax.optimization_barrier((total, mid, d_rest))
     mid = add_core(mid, n_dp)

time: 142 us -> 139 us (0.979)
  local copies, waits for them, and re-layouts: 12.7 us -> 9.77 us
    ppermute x32, waiting for transfers between devices: 14.8 us -> 19.3 us  [swap(): return lax.ppermute(x, 'dp', [(i, i ^ bit) for i in range(n_dp)])]
    ppermute x10, waiting for transfers between devices: 22.1 us -> 17.6 us  [shift(): lax.ppermute(x, 'tensor', [(i, (i - by) % n_tensor) for i in range(n_tens...]
    unnamed x58 -> x54, local copies, waits for them, and re-layouts: 3.86 us -> 2.22 us
  transfers between devices with their start and end apart: 42 -> 42, of which waited for: 15 -> 20; matrix products, arithmetic and copies ran while one was open for 13% -> 12% of each run, Pallas kernels for 29% -> 30%
where the time goes in v8:
time: 139 us; the launch traced here: 138 us
  Pallas kernels  41.1 us (30%)
  waiting for transfers between devices  36.9 us (27%)
  starting transfers between devices  36.8 us (26%)
  other arithmetic  12.3 us (9%)
  local copies, waits for them, and re-layouts  9.77 us (7%)
    ppermute x32, starting transfers between devices, swap(): return lax.ppermute(x, 'dp', [(i, i ^ bit) for i in range(n_dp)])  21.9 us
    ppermute x32, waiting for transfers between devices, swap(): return lax.ppermute(x, 'dp', [(i, i ^ bit) for i in range(n_dp)])  19.3 us
    ppermute x10, waiting for transfers between devices, shift(): lax.ppermute(x, 'tensor', [(i, (i - by) % n_tensor) for i in range(n_tens...  17.6 us
    ppermute x10, starting transfers between devices, shift(): lax.ppermute(x, 'tensor', [(i, (i - by) % n_tensor) for i in range(n_tens...  14.9 us
    pallas_call x2, Pallas kernels, weight_grad(): pl.pallas_call(body, grid_spec=pltpu.PrefetchScalarGridSpec(num_scalar_pr...  12.1 us
    pallas_call x2, Pallas kernels, hidden_grad(): pl.pallas_call(body, grid_spec=pltpu.PrefetchScalarGridSpec(num_scalar_pr...  11.7 us
    pallas_call x1, Pallas kernels, project(): pl.pallas_call(body, grid_spec=pltpu.PrefetchScalarGridSpec(num_scalar_pr...  11.1 us
    add x1, other arithmetic, local(): total = keep + swap(sent, 1, n_dp).astype(F32)  3.55 us
  transfers between devices with their start and end apart: 42, of which 20 were waited for; matrix products, arithmetic and copies ran while one was open for 12% of the time, Pallas kernels for 30%

profile of v8, /device:TPU:0, one launch (start us, length us, event | category | flops | bytes accessed | tf_op | source)
XLA Modules:
  0.0 137.9 jit_solution(1929728002988758440)
XLA Ops:
  1.8 3.0 %collective-permute-start.2 = (bf16[128,1024]{1,0:T(8,128)(2,1)S(1)}, bf16[128,1024]{1,0:T(8,128)(2,1)S(1)}, u32[]{:S(2)}, u32[]{:S(2)}) collective-permute-start(bf16[128,1024]{1,0:T(8,128)(2,1)S(1)} %get-tuple-element.83.rest_0_.rest_3_), channel_id=1, source_target_pairs={{0,8},{4,12},{8,0},{12,4},{16,24},{20,28},{24,16},{28,20},{1,9},{5... | collective-permute-start | bytes 786440 | tf_op jit(solution)/shard_map/ppermute | solution.py:17
  4.8 1.5 %collective-permute-start.7 = (bf16[128,1024]{1,0:T(8,128)(2,1)S(1)}, bf16[128,1024]{1,0:T(8,128)(2,1)S(1)}, u32[]{:S(2)}, u32[]{:S(2)}) collective-permute-start(bf16[128,1024]{1,0:T(8,128)(2,1)S(1)} %get-tuple-element.82.rest_1_.rest_4_), channel_id=1, source_target_pairs={{0,16},{4,20},{8,24},{12,28},{16,0},{20,4},{24,8},{28,12},{1,17},{... | collective-permute-start | bytes 786440 | tf_op jit(solution)/shard_map/ppermute | solution.py:17
  6.3 3.6 %collective-permute-start.12 = (bf16[256,1024]{1,0:T(8,128)(2,1)}, bf16[256,1024]{1,0:T(8,128)(2,1)S(1)}, u32[]{:S(2)}, u32[]{:S(2)}) collective-permute-start(bf16[256,1024]{1,0:T(8,128)(2,1)} %param.5), channel_id=1, source_target_pairs={{0,3},{1,0},{2,1},{3,2},{4,7},{5,4},{6,5},{7,6},{8,11},{9,8},{10,9... | collective-permute-start | bytes 1572872 | tf_op jit(solution)/shard_map/ppermute | solution.py:132
  11.1 1.8 %collective-permute-start.10 = (bf16[128,1024]{1,0:T(8,128)(2,1)S(1)}, bf16[128,1024]{1,0:T(8,128)(2,1)S(1)}, u32[]{:S(2)}, u32[]{:S(2)}) collective-permute-start(bf16[128,1024]{1,0:T(8,128)(2,1)S(1)} %collective-permute-done.2.rest_4_.rest_3_), channel_id=1, source_target_pairs={{0,16},{4,20},{8,24},{12,28},{16,0},{20,4},{24,8},{28,12},{1,17},{... | collective-permute-start | bytes 786440 | tf_op jit(solution)/shard_map/ppermute | solution.py:17
  12.9 1.5 %collective-permute-start.11 = (bf16[128,1024]{1,0:T(8,128)(2,1)S(1)}, bf16[128,1024]{1,0:T(8,128)(2,1)}, u32[]{:S(2)}, u32[]{:S(2)}) collective-permute-start(bf16[128,1024]{1,0:T(8,128)(2,1)S(1)} %collective-permute-done.7.rest_9_.rest_12_), channel_id=1, source_target_pairs={{0,8},{4,12},{8,0},{12,4},{16,24},{20,28},{24,16},{28,20},{1,9},{5... | collective-permute-start | bytes 786440 | tf_op jit(solution)/shard_map/ppermute | solution.py:17
  14.9 3.7 %collective-permute-done.10.rest_12_.rest_0_ = bf16[128,1024]{1,0:T(8,128)(2,1)S(1)} collective-permute-done((bf16[128,1024]{1,0:T(8,128)(2,1)S(1)}, bf16[128,1024]{1,0:T(8,128)(2,1)S(1)}, u32[]{:S(2)}, u32[]{:S(2)}) %collective-permute-start.10) | collective-permute-done | bytes 262176 | tf_op jit(solution)/shard_map/ppermute | solution.py:17
  18.6 1.5 %collective-permute-start.6 = (bf16[128,1024]{1,0:T(8,128)(2,1)S(1)}, bf16[128,1024]{1,0:T(8,128)(2,1)S(1)}, u32[]{:S(2)}, u32[]{:S(2)}) collective-permute-start(bf16[128,1024]{1,0:T(8,128)(2,1)S(1)} %get-tuple-element.83.rest_0_.rest_3_), channel_id=1, source_target_pairs={{0,16},{4,20},{8,24},{12,28},{16,0},{20,4},{24,8},{28,12},{1,17},{... | collective-permute-start | bytes 786440 | tf_op jit(solution)/shard_map/ppermute | solution.py:17
  20.1 2.1 %collective-permute-done.11.rest_13_.rest_1_ = bf16[128,1024]{1,0:T(8,128)(2,1)} collective-permute-done((bf16[128,1024]{1,0:T(8,128)(2,1)S(1)}, bf16[128,1024]{1,0:T(8,128)(2,1)}, u32[]{:S(2)}, u32[]{:S(2)}) %collective-permute-start.11) | collective-permute-done | bytes 262176 | tf_op jit(solution)/shard_map/ppermute | solution.py:17
  22.6 10.3 %collective-permute-done.13 = bf16[256,1024]{1,0:T(8,128)(2,1)S(1)} collective-permute-done((bf16[256,1024]{1,0:T(8,128)(2,1)}, bf16[256,1024]{1,0:T(8,128)(2,1)S(1)}, u32[]{:S(2)}, u32[]{:S(2)}) %collective-permute-start.13) | collective-permute-done | bytes 524320 | tf_op jit(solution)/shard_map/ppermute | solution.py:132
  41.2 11.1 %project.1 = (bf16[512,256]{1,0:T(8,128)(2,1)}, bf16[4,128,256]{2,1,0:T(8,128)(2,1)}, bf16[256,512]{1,0:T(8,128)(2,1)}) custom-call(s32[2]{0:T(128)} %pad_add_fusion.where_ref, bf16[512,8192]{1,0:T(8,128)(2,1)} %h_ref.5, f32[1,128]{1,0:T(1,128)} %s_ref.1, bf16[512,256]{1,0:T(8,128)(2,1)} %c_ref.1, bf16[128,1024]{1,0:T(8,128)(2,1)} %copy-done.8, ...), custom_call_target="tpu_custom_call" | custom-call | tf_op jit(solution)/shard_map/project/pallas_call | solution.py:81
  52.2 3.2 %hidden_share.1 = bf16[4,128,2048]{2,1,0:T(8,128)(2,1)} custom-call(bf16[4,128,256]{2,1,0:T(8,128)(2,1)} %get-tuple-element.40.d_ref, bf16[128,1024]{1,0:T(8,128)(2,1)} %copy-done.18, bf16[128,1024]{1,0:T(8,128)(2,1)} %collective-permute-done.11.rest_13_.rest_1_, bf16[128,1024]{1,0:T(8,128)(2,1)} %collective-permute-done.14.rest_14_.rest_2_, ...), custom_call_target="tpu_custom_call" | custom-call | tf_op jit(solution)/shard_map/hidden_share/pallas_call | solution.py:151
  55.4 5.9 %weight_grad_odd.1 = bf16[4,256,1024]{2,1,0:T(8,128)(2,1)} custom-call(s32[2]{0:T(128)} %pad_add_fusion.where_ref, bf16[256,512]{1,0:T(8,128)(2,1)} %get-tuple-element.45.d_ref, bf16[512,8192]{1,0:T(8,128)(2,1)} %h_ref.5), custom_call_target="tpu_custom_call" | custom-call | tf_op jit(solution)/shard_map/weight_grad_odd/pallas_call | solution.py:115
  61.3 2.9 %collective-permute-done.18.rest_6_ = bf16[256,1024]{1,0:T(8,128)(2,1)} collective-permute-done((bf16[256,1024]{1,0:T(8,128)(2,1)S(1)}, bf16[256,1024]{1,0:T(8,128)(2,1)}, u32[]{:S(2)}, u32[]{:S(2)}) %collective-permute-start.18) | collective-permute-done | bytes 524320 | tf_op jit(solution)/shard_map/ppermute | solution.py:132
  65.0 1.7 %collective-permute-start.19 = (bf16[128,1024]{1,0:T(8,128)(2,1)S(1)}, bf16[128,1024]{1,0:T(8,128)(2,1)S(1)}, u32[]{:S(2)}, u32[]{:S(2)}) collective-permute-start(bf16[128,1024]{1,0:T(8,128)(2,1)S(1)} %get-tuple-element.79), channel_id=1, source_target_pairs={{0,3},{1,0},{2,1},{3,2},{4,7},{5,4},{6,5},{7,6},{8,11},{9,8},{10,9... | collective-permute-start | bytes 786440 | tf_op jit(solution)/shard_map/ppermute | solution.py:132
  67.7 3.5 %collective-permute-start.24 = (bf16[128,256]{1,0:T(8,128)(2,1)}, bf16[128,256]{1,0:T(8,128)(2,1)S(1)}, u32[]{:S(2)}, u32[]{:S(2)}) collective-permute-start(bf16[128,256]{1,0:T(8,128)(2,1)} %get-tuple-element.87), channel_id=1, source_target_pairs={{0,3},{1,0},{2,1},{3,2},{4,7},{5,4},{6,5},{7,6},{8,11},{9,8},{10,9... | collective-permute-start | bytes 196616 | tf_op jit(solution)/shard_map/ppermute | solution.py:132
  71.2 6.3 %weight_grad_even.1 = f32[4,256,1024]{2,1,0:T(8,128)} custom-call(s32[2]{0:T(128)} %pad_add_fusion.where_ref, bf16[256,512]{1,0:T(8,128)(2,1)} %get-tuple-element.45.d_ref, bf16[512,8192]{1,0:T(8,128)(2,1)} %h_ref.5), custom_call_target="tpu_custom_call" | custom-call | tf_op jit(solution)/shard_map/weight_grad_even/pallas_call | solution.py:115
  77.4 3.7 %collective-permute-done.19 = bf16[128,1024]{1,0:T(8,128)(2,1)S(1)} collective-permute-done((bf16[128,1024]{1,0:T(8,128)(2,1)S(1)}, bf16[128,1024]{1,0:T(8,128)(2,1)S(1)}, u32[]{:S(2)}, u32[]{:S(2)}) %collective-permute-start.19) | collective-permute-done | bytes 262176 | tf_op jit(solution)/shard_map/ppermute | solution.py:132
  81.2 1.5 %collective-permute-start.22 = (bf16[256,1024]{1,0:T(8,128)(2,1)}, bf16[256,1024]{1,0:T(8,128)(2,1)S(1)}, u32[]{:S(2)}, u32[]{:S(2)}) collective-permute-start(bf16[256,1024]{1,0:T(8,128)(2,1)} %collective-permute-done.18.rest_6_), channel_id=1, source_target_pairs={{0,8},{4,12},{8,0},{12,4},{16,24},{20,28},{24,16},{28,20},{1,9},{5... | collective-permute-start | bytes 1572872 | tf_op jit(solution)/shard_map/ppermute | solution.py:17
  82.7 1.5 %collective-permute-start.23 = (bf16[256,1024]{1,0:T(8,128)(2,1)}, bf16[256,1024]{1,0:T(8,128)(2,1)S(1)}, u32[]{:S(2)}, u32[]{:S(2)}) collective-permute-start(bf16[256,1024]{1,0:T(8,128)(2,1)} %collective-permute-done.18.rest_6_), channel_id=1, source_target_pairs={{0,16},{4,20},{8,24},{12,28},{16,0},{20,4},{24,8},{28,12},{1,17},{... | collective-permute-start | bytes 1572872 | tf_op jit(solution)/shard_map/ppermute | solution.py:17
  86.1 3.6 %convert_add_fusion = f32[4,256,1024]{2,1,0:T(8,128)S(1)} fusion(f32[4,256,1024]{2,1,0:T(8,128)} %weight_grad_even.1, bf16[4,256,1024]{2,1,0:T(8,128)(2,1)} %collective-permute-done.21), kind=kLoop, calls=%fused_computation | loop fusion | flops 2097152 | bytes 10485760 | tf_op jit(solution)/shard_map/add | solution.py:288
  89.7 3.8 %collective-permute-start.31 = (bf16[128,2048]{1,0:T(8,128)(2,1)}, bf16[128,2048]{1,0:T(8,128)(2,1)}, u32[]{:S(2)}, u32[]{:S(2)}) collective-permute-start(bf16[128,2048]{1,0:T(8,128)(2,1)} %pad_maximum_fusion.1), channel_id=1, source_target_pairs={{0,3},{1,0},{2,1},{3,2},{4,7},{5,4},{6,5},{7,6},{8,11},{9,8},{10,9... | collective-permute-start | bytes 1572872 | tf_op jit(solution)/shard_map/ppermute | solution.py:132
  97.3 1.5 %collective-permute-start.28 = (bf16[2,128,1024]{2,1,0:T(8,128)(2,1)}, bf16[2,128,1024]{2,1,0:T(8,128)(2,1)}, u32[]{:S(2)}, u32[]{:S(2)}) collective-permute-start(bf16[2,128,1024]{2,1,0:T(8,128)(2,1)} %slice_bitcast_fusion.4), channel_id=1, source_target_pairs={{0,16},{4,20},{8,24},{12,28},{16,0},{20,4},{24,8},{28,12},{1,17},{... | collective-permute-start | bytes 1572872 | tf_op jit(solution)/shard_map/ppermute | solution.py:17
  100.9 4.6 %hidden_grad.2.rest_19_ = bf16[128,8192]{1,0:T(8,128)(2,1)} custom-call(s32[2]{0:T(128)} %pad_add_fusion.where_ref, bf16[128,256]{1,0:T(8,128)(2,1)} %get-tuple-element.84.rest_0_, bf16[128,512]{1,0:T(8,128)(2,1)} %copy-done.20, bf16[128,256]{1,0:T(8,128)(2,1)} %copy-done.24, bf16[128,1024]{1,0:T(8,128)(2,1)} %copy-done.8, bf16[128,1024]{1,0:T(8,128)(2,1)} %copy-done.7, ...), custom_call_target="tpu_custom_call" | custom-call | tf_op jit(solution)/shard_map/hidden_grad/pallas_call | solution.py:201
  105.7 1.3 collective-permute-start.38
  106.9 2.9 %collective-permute-done.27 = bf16[2,128,1024]{2,1,0:T(8,128)(2,1)} collective-permute-done((bf16[2,128,1024]{2,1,0:T(8,128)(2,1)}, bf16[2,128,1024]{2,1,0:T(8,128)(2,1)}, u32[]{:S(2)}, u32[]{:S(2)}) %collective-permute-start.27) | collective-permute-done | bytes 524320 | tf_op jit(solution)/shard_map/ppermute | solution.py:17
  109.8 1.4 %collective-permute-done.28 = bf16[2,128,1024]{2,1,0:T(8,128)(2,1)} collective-permute-done((bf16[2,128,1024]{2,1,0:T(8,128)(2,1)}, bf16[2,128,1024]{2,1,0:T(8,128)(2,1)}, u32[]{:S(2)}, u32[]{:S(2)}) %collective-permute-start.28) | collective-permute-done | bytes 524320 | tf_op jit(solution)/shard_map/ppermute | solution.py:17
  111.3 2.1 %fusion.6 = (f32[2,128,1024]{2,1,0:T(8,128)S(1)}, f32[2,128,1024]{2,1,0:T(8,128)S(1)}) fusion(f32[2,2,256,1024]{3,2,1,0:T(8,128)} %bitcast.58, bf16[2,128,1024]{2,1,0:T(8,128)(2,1)} %collective-permute-done.28, bf16[2,128,1024]{2,1,0:T(8,128)(2,1)} %collective-permute-done.27), kind=kLoop, calls=%fused_computation.12 | loop fusion | flops 1048576 | bytes 5242880 | tf_op jit(solution)/shard_map/add | solution.py:313
  115.3 1.5 %collective-permute-start.32 = (bf16[128,1024]{1,0:T(8,128)(2,1)}, bf16[128,1024]{1,0:T(8,128)(2,1)S(1)}, u32[]{:S(2)}, u32[]{:S(2)}) collective-permute-start(bf16[128,1024]{1,0:T(8,128)(2,1)} %fusion.10), channel_id=1, source_target_pairs={{0,16},{4,20},{8,24},{12,28},{16,0},{20,4},{24,8},{28,12},{1,17},{... | collective-permute-start | bytes 786440 | tf_op jit(solution)/shard_map/ppermute | solution.py:17
  117.4 7.1 %hidden_grad.3.rest_3_ = bf16[128,8192]{1,0:T(8,128)(2,1)} custom-call(s32[2]{0:T(128)} %pad_add_fusion.where_ref, bf16[128,256]{1,0:T(8,128)(2,1)} %get-tuple-element.84.rest_0_, bf16[128,512]{1,0:T(8,128)(2,1)} %copy-done.20, bf16[128,256]{1,0:T(8,128)(2,1)} %copy-done.24, bf16[128,1024]{1,0:T(8,128)(2,1)} %copy-done.10, ...), custom_call_target="tpu_custom_call", output_to_operand_aliasing={{}: (20, {})} | custom-call | tf_op jit(solution)/shard_map/hidden_grad/pallas_call | solution.py:201
  125.6 1.4 %fusion.8 = (f32[128,1024]{1,0:T(8,128)S(1)}, f32[128,1024]{1,0:T(8,128)S(1)}) fusion(f32[2,128,1024]{2,1,0:T(8,128)} %copy-done.5, bf16[128,1024]{1,0:T(8,128)(2,1)} %collective-permute-done.33, bf16[128,1024]{1,0:T(8,128)(2,1)S(1)} %collective-permute-done.32, f32[2,128,1024]{2,1,0:T(8,128)} %copy-done.6), kind=kLoop, calls=%fused_computation.18 | loop fusion | flops 524288 | bytes 2621440 | tf_op jit(solution)/shard_map/add | solution.py:313
  129.3 3.0 %collective-permute-done.40 = f32[3,256]{1,0:T(4,128)S(1)} collective-permute-done((f32[3,256]{1,0:T(4,128)S(1)}, f32[3,256]{1,0:T(4,128)S(1)}, u32[]{:S(2)}, u32[]{:S(2)}) %collective-permute-start.40) | collective-permute-done | bytes 3104 | tf_op jit(solution)/shard_map/ppermute | solution.py:17
  133.8 3.0 %add_shares.1 = bf16[128,8192]{1,0:T(8,128)(2,1)} custom-call(s32[2]{0:T(128)} %pad_add_fusion.where_ref, bf16[128,2048]{1,0:T(8,128)(2,1)} %slice_bitcast_fusion.6.rest_0_, bf16[128,2048]{1,0:T(8,128)(2,1)} %collective-permute-done.31.rest_1_, bf16[128,2048]{1,0:T(8,128)(2,1)} %collective-permute-done.38.rest_2_, ...), custom_call_target="tpu_custom_call", output_to_operand_aliasing={{}: (4, {})} | custom-call | tf_op jit(solution)/shard_map/add_shares/pallas_call | solution.py:230
  (139 shorter events, 29.5 us)
Async XLA Ops:
  1.8 9.3 %collective-permute-start.2 = (bf16[128,1024]{1,0:T(8,128)(2,1)S(1)}, bf16[128,1024]{1,0:T(8,128)(2,1)S(1)}, u32[]{:S(2)}, u32[]{:S(2)}) collective-permute-start(bf16[128,1024]{1,0:T(8,128)(2,1)S(1)} %get-tuple-element.83.rest_0_.rest_3_), channel_id=1, source_target_pairs={{0,8},{4,12},{8,0},{12,4},{16,24},{20,28},{24,16},{28,20},{1,9},{5... | collective-permute-start | bytes 786440 | tf_op jit(solution)/shard_map/ppermute | solution.py:17
  4.8 8.1 %collective-permute-start.7 = (bf16[128,1024]{1,0:T(8,128)(2,1)S(1)}, bf16[128,1024]{1,0:T(8,128)(2,1)S(1)}, u32[]{:S(2)}, u32[]{:S(2)}) collective-permute-start(bf16[128,1024]{1,0:T(8,128)(2,1)S(1)} %get-tuple-element.82.rest_1_.rest_4_), channel_id=1, source_target_pairs={{0,16},{4,20},{8,24},{12,28},{16,0},{20,4},{24,8},{28,12},{1,17},{... | collective-permute-start | bytes 786440 | tf_op jit(solution)/shard_map/ppermute | solution.py:17
  6.3 16.2 %collective-permute-start.12 = (bf16[256,1024]{1,0:T(8,128)(2,1)}, bf16[256,1024]{1,0:T(8,128)(2,1)S(1)}, u32[]{:S(2)}, u32[]{:S(2)}) collective-permute-start(bf16[256,1024]{1,0:T(8,128)(2,1)} %param.5), channel_id=1, source_target_pairs={{0,3},{1,0},{2,1},{3,2},{4,7},{5,4},{6,5},{7,6},{8,11},{9,8},{10,9... | collective-permute-start | bytes 1572872 | tf_op jit(solution)/shard_map/ppermute | solution.py:132
  9.9 23.0 %collective-permute-start.13 = (bf16[256,1024]{1,0:T(8,128)(2,1)}, bf16[256,1024]{1,0:T(8,128)(2,1)S(1)}, u32[]{:S(2)}, u32[]{:S(2)}) collective-permute-start(bf16[256,1024]{1,0:T(8,128)(2,1)} %param.5), channel_id=1, source_target_pairs={{0,1},{1,2},{2,3},{3,0},{4,5},{5,6},{6,7},{7,4},{8,9},{9,10},{10,1... | collective-permute-start | bytes 1572872 | tf_op jit(solution)/shard_map/ppermute | solution.py:132
  11.1 7.5 %collective-permute-start.10 = (bf16[128,1024]{1,0:T(8,128)(2,1)S(1)}, bf16[128,1024]{1,0:T(8,128)(2,1)S(1)}, u32[]{:S(2)}, u32[]{:S(2)}) collective-permute-start(bf16[128,1024]{1,0:T(8,128)(2,1)S(1)} %collective-permute-done.2.rest_4_.rest_3_), channel_id=1, source_target_pairs={{0,16},{4,20},{8,24},{12,28},{16,0},{20,4},{24,8},{28,12},{1,17},{... | collective-permute-start | bytes 786440 | tf_op jit(solution)/shard_map/ppermute | solution.py:17
  12.9 9.3 %collective-permute-start.11 = (bf16[128,1024]{1,0:T(8,128)(2,1)S(1)}, bf16[128,1024]{1,0:T(8,128)(2,1)}, u32[]{:S(2)}, u32[]{:S(2)}) collective-permute-start(bf16[128,1024]{1,0:T(8,128)(2,1)S(1)} %collective-permute-done.7.rest_9_.rest_12_), channel_id=1, source_target_pairs={{0,8},{4,12},{8,0},{12,4},{16,24},{20,28},{24,16},{28,20},{1,9},{5... | collective-permute-start | bytes 786440 | tf_op jit(solution)/shard_map/ppermute | solution.py:17
  14.4 21.2 %collective-permute-start.3 = (bf16[128,1024]{1,0:T(8,128)(2,1)S(1)}, bf16[128,1024]{1,0:T(8,128)(2,1)S(1)}, u32[]{:S(2)}, u32[]{:S(2)}) collective-permute-start(bf16[128,1024]{1,0:T(8,128)(2,1)S(1)} %get-tuple-element.82.rest_1_.rest_4_), channel_id=1, source_target_pairs={{0,8},{4,12},{8,0},{12,4},{16,24},{20,28},{24,16},{28,20},{1,9},{5... | collective-permute-start | bytes 786440 | tf_op jit(solution)/shard_map/ppermute | solution.py:17
  18.6 17.0 %collective-permute-start.6 = (bf16[128,1024]{1,0:T(8,128)(2,1)S(1)}, bf16[128,1024]{1,0:T(8,128)(2,1)S(1)}, u32[]{:S(2)}, u32[]{:S(2)}) collective-permute-start(bf16[128,1024]{1,0:T(8,128)(2,1)S(1)} %get-tuple-element.83.rest_0_.rest_3_), channel_id=1, source_target_pairs={{0,16},{4,20},{8,24},{12,28},{16,0},{20,4},{24,8},{28,12},{1,17},{... | collective-permute-start | bytes 786440 | tf_op jit(solution)/shard_map/ppermute | solution.py:17
  22.2 13.9 %collective-permute-start = (bf16[128,1024]{1,0:T(8,128)(2,1)S(1)}, bf16[128,1024]{1,0:T(8,128)(2,1)}, u32[]{:S(2)}, u32[]{:S(2)}) collective-permute-start(bf16[128,1024]{1,0:T(8,128)(2,1)S(1)} %get-tuple-element.83.rest_0_.rest_3_), channel_id=1, source_target_pairs={{0,4},{4,0},{8,12},{12,8},{16,20},{20,16},{24,28},{28,24},{1,5},{5... | collective-permute-start | bytes 786440 | tf_op jit(solution)/shard_map/ppermute | solution.py:17
  34.6 29.6 %collective-permute-start.16 = (bf16[512,1024]{1,0:T(8,128)(2,1)}, bf16[512,1024]{1,0:T(8,128)(2,1)}, u32[]{:S(2)}, u32[]{:S(2)}) collective-permute-start(bf16[512,1024]{1,0:T(8,128)(2,1)} %constant_dynamic-update-slice_fusion.rest_5_), channel_id=1, source_target_pairs={{0,8},{4,12},{8,0},{12,4},{16,24},{20,28},{24,16},{28,20},{1,9},{5... | collective-permute-start | bytes 3145736 | tf_op jit(solution)/shard_map/ppermute | solution.py:17
  35.1 29.1 %collective-permute-start.17 = (bf16[512,1024]{1,0:T(8,128)(2,1)}, bf16[512,1024]{1,0:T(8,128)(2,1)}, u32[]{:S(2)}, u32[]{:S(2)}) collective-permute-start(bf16[512,1024]{1,0:T(8,128)(2,1)} %constant_dynamic-update-slice_fusion.rest_5_), channel_id=1, source_target_pairs={{0,16},{4,20},{8,24},{12,28},{16,0},{20,4},{24,8},{28,12},{1,17},{... | collective-permute-start | bytes 3145736 | tf_op jit(solution)/shard_map/ppermute | solution.py:17
  37.9 26.3 %collective-permute-start.18 = (bf16[256,1024]{1,0:T(8,128)(2,1)S(1)}, bf16[256,1024]{1,0:T(8,128)(2,1)}, u32[]{:S(2)}, u32[]{:S(2)}) collective-permute-start(bf16[256,1024]{1,0:T(8,128)(2,1)S(1)} %copy-done.2), channel_id=1, source_target_pairs={{0,2},{1,3},{2,0},{3,1},{4,6},{5,7},{6,4},{7,5},{8,10},{9,11},{10,... | collective-permute-start | bytes 1572872 | tf_op jit(solution)/shard_map/ppermute | solution.py:132
  64.2 21.9 %collective-permute-start.21 = (bf16[4,256,1024]{2,1,0:T(8,128)(2,1)}, bf16[4,256,1024]{2,1,0:T(8,128)(2,1)}, u32[]{:S(2)}, u32[]{:S(2)}) collective-permute-start(bf16[4,256,1024]{2,1,0:T(8,128)(2,1)} %weight_grad_odd.1), channel_id=1, source_target_pairs={{0,4},{4,0},{8,12},{12,8},{16,20},{20,16},{24,28},{28,24},{1,5},{5... | collective-permute-start | bytes 6291464 | tf_op jit(solution)/shard_map/ppermute | solution.py:17
  65.0 16.2 %collective-permute-start.19 = (bf16[128,1024]{1,0:T(8,128)(2,1)S(1)}, bf16[128,1024]{1,0:T(8,128)(2,1)S(1)}, u32[]{:S(2)}, u32[]{:S(2)}) collective-permute-start(bf16[128,1024]{1,0:T(8,128)(2,1)S(1)} %get-tuple-element.79), channel_id=1, source_target_pairs={{0,3},{1,0},{2,1},{3,2},{4,7},{5,4},{6,5},{7,6},{8,11},{9,8},{10,9... | collective-permute-start | bytes 786440 | tf_op jit(solution)/shard_map/ppermute | solution.py:132
  66.6 16.0 %collective-permute-start.20 = (bf16[128,1024]{1,0:T(8,128)(2,1)}, bf16[128,1024]{1,0:T(8,128)(2,1)}, u32[]{:S(2)}, u32[]{:S(2)}) collective-permute-start(bf16[128,1024]{1,0:T(8,128)(2,1)} %get-tuple-element.78), channel_id=1, source_target_pairs={{0,1},{1,2},{2,3},{3,0},{4,5},{5,6},{6,7},{7,4},{8,9},{9,10},{10,1... | collective-permute-start | bytes 786440 | tf_op jit(solution)/shard_map/ppermute | solution.py:132
  67.7 18.3 %collective-permute-start.24 = (bf16[128,256]{1,0:T(8,128)(2,1)}, bf16[128,256]{1,0:T(8,128)(2,1)S(1)}, u32[]{:S(2)}, u32[]{:S(2)}) collective-permute-start(bf16[128,256]{1,0:T(8,128)(2,1)} %get-tuple-element.87), channel_id=1, source_target_pairs={{0,3},{1,0},{2,1},{3,2},{4,7},{5,4},{6,5},{7,6},{8,11},{9,8},{10,9... | collective-permute-start | bytes 196616 | tf_op jit(solution)/shard_map/ppermute | solution.py:132
  71.2 18.6 %collective-permute-start.25 = (bf16[128,256]{1,0:T(8,128)(2,1)}, bf16[128,256]{1,0:T(8,128)(2,1)S(1)}, u32[]{:S(2)}, u32[]{:S(2)}) collective-permute-start(bf16[128,256]{1,0:T(8,128)(2,1)} %get-tuple-element.86), channel_id=1, source_target_pairs={{0,2},{1,3},{2,0},{3,1},{4,6},{5,7},{6,4},{7,5},{8,10},{9,11},{10,... | collective-permute-start | bytes 196616 | tf_op jit(solution)/shard_map/ppermute | solution.py:132
  81.2 12.3 %collective-permute-start.22 = (bf16[256,1024]{1,0:T(8,128)(2,1)}, bf16[256,1024]{1,0:T(8,128)(2,1)S(1)}, u32[]{:S(2)}, u32[]{:S(2)}) collective-permute-start(bf16[256,1024]{1,0:T(8,128)(2,1)} %collective-permute-done.18.rest_6_), channel_id=1, source_target_pairs={{0,8},{4,12},{8,0},{12,4},{16,24},{20,28},{24,16},{28,20},{1,9},{5... | collective-permute-start | bytes 1572872 | tf_op jit(solution)/shard_map/ppermute | solution.py:17
  82.7 10.9 %collective-permute-start.23 = (bf16[256,1024]{1,0:T(8,128)(2,1)}, bf16[256,1024]{1,0:T(8,128)(2,1)S(1)}, u32[]{:S(2)}, u32[]{:S(2)}) collective-permute-start(bf16[256,1024]{1,0:T(8,128)(2,1)} %collective-permute-done.18.rest_6_), channel_id=1, source_target_pairs={{0,16},{4,20},{8,24},{12,28},{16,0},{20,4},{24,8},{28,12},{1,17},{... | collective-permute-start | bytes 1572872 | tf_op jit(solution)/shard_map/ppermute | solution.py:17
  86.0 7.5 %collective-permute-start.26 = (bf16[128,256]{1,0:T(8,128)(2,1)S(1)}, bf16[128,256]{1,0:T(8,128)(2,1)S(1)}, u32[]{:S(2)}, u32[]{:S(2)}) collective-permute-start(bf16[128,256]{1,0:T(8,128)(2,1)S(1)} %copy-done.25), channel_id=1, source_target_pairs={{0,1},{1,2},{2,3},{3,0},{4,5},{5,6},{6,7},{7,4},{8,9},{9,10},{10,1... | collective-permute-start | bytes 196616 | tf_op jit(solution)/shard_map/ppermute | solution.py:132
  86.1 12.8 %collective-permute-start.29 = (bf16[512,1024]{1,0:T(8,128)(2,1)}, bf16[512,1024]{1,0:T(8,128)(2,1)}, u32[]{:S(2)}, u32[]{:S(2)}) collective-permute-start(bf16[512,1024]{1,0:T(8,128)(2,1)} %constant_dynamic-update-slice_fusion.rest_5_), channel_id=1, source_target_pairs={{0,4},{4,0},{8,12},{12,8},{16,20},{20,16},{24,28},{28,24},{1,5},{5... | collective-permute-start | bytes 3145736 | tf_op jit(solution)/shard_map/ppermute | solution.py:17
  89.7 16.0 %collective-permute-start.31 = (bf16[128,2048]{1,0:T(8,128)(2,1)}, bf16[128,2048]{1,0:T(8,128)(2,1)}, u32[]{:S(2)}, u32[]{:S(2)}) collective-permute-start(bf16[128,2048]{1,0:T(8,128)(2,1)} %pad_maximum_fusion.1), channel_id=1, source_target_pairs={{0,3},{1,0},{2,1},{3,2},{4,7},{5,4},{6,5},{7,6},{8,11},{9,8},{10,9... | collective-permute-start | bytes 1572872 | tf_op jit(solution)/shard_map/ppermute | solution.py:132
  93.5 5.3 %collective-permute-start.30 = (bf16[256,1024]{1,0:T(8,128)(2,1)}, bf16[256,1024]{1,0:T(8,128)(2,1)S(1)}, u32[]{:S(2)}, u32[]{:S(2)}) collective-permute-start(bf16[256,1024]{1,0:T(8,128)(2,1)} %collective-permute-done.18.rest_6_), channel_id=1, source_target_pairs={{0,4},{4,0},{8,12},{12,8},{16,20},{20,16},{24,28},{28,24},{1,5},{5... | collective-permute-start | bytes 1572872 | tf_op jit(solution)/shard_map/ppermute | solution.py:17
  95.5 14.4 %collective-permute-start.27 = (bf16[2,128,1024]{2,1,0:T(8,128)(2,1)}, bf16[2,128,1024]{2,1,0:T(8,128)(2,1)}, u32[]{:S(2)}, u32[]{:S(2)}) collective-permute-start(bf16[2,128,1024]{2,1,0:T(8,128)(2,1)} %slice_bitcast_fusion.5), channel_id=1, source_target_pairs={{0,8},{4,12},{8,0},{12,4},{16,24},{20,28},{24,16},{28,20},{1,9},{5... | collective-permute-start | bytes 1572872 | tf_op jit(solution)/shard_map/ppermute | solution.py:17
  97.3 13.9 %collective-permute-start.28 = (bf16[2,128,1024]{2,1,0:T(8,128)(2,1)}, bf16[2,128,1024]{2,1,0:T(8,128)(2,1)}, u32[]{:S(2)}, u32[]{:S(2)}) collective-permute-start(bf16[2,128,1024]{2,1,0:T(8,128)(2,1)} %slice_bitcast_fusion.4), channel_id=1, source_target_pairs={{0,16},{4,20},{8,24},{12,28},{16,0},{20,4},{24,8},{28,12},{1,17},{... | collective-permute-start | bytes 1572872 | tf_op jit(solution)/shard_map/ppermute | solution.py:17
  98.8 16.4 %collective-permute-start.34 = (bf16[512,1024]{1,0:T(8,128)(2,1)}, bf16[512,1024]{1,0:T(8,128)(2,1)S(1)}, u32[]{:S(2)}, u32[]{:S(2)}) collective-permute-start(bf16[512,1024]{1,0:T(8,128)(2,1)} %collective-permute-done.16.rest_5_), channel_id=1, source_target_pairs={{0,4},{4,0},{8,12},{12,8},{16,20},{20,16},{24,28},{28,24},{1,5},{5... | collective-permute-start | bytes 3145736 | tf_op jit(solution)/shard_map/ppermute | solution.py:17
  98.8 18.0 %collective-permute-start.36 = (bf16[512,1024]{1,0:T(8,128)(2,1)}, bf16[512,1024]{1,0:T(8,128)(2,1)}, u32[]{:S(2)}, u32[]{:S(2)}) collective-permute-start(bf16[512,1024]{1,0:T(8,128)(2,1)} %collective-permute-done.17.rest_13_), channel_id=1, source_target_pairs={{0,4},{4,0},{8,12},{12,8},{16,20},{20,16},{24,28},{28,24},{1,5},{5... | collective-permute-start | bytes 3145736 | tf_op jit(solution)/shard_map/ppermute | solution.py:17
  105.7 18.8 %collective-permute-start.38 = (bf16[128,2048]{1,0:T(8,128)(2,1)}, bf16[128,2048]{1,0:T(8,128)(2,1)}, u32[]{:S(2)}, u32[]{:S(2)}) collective-permute-start(bf16[128,2048]{1,0:T(8,128)(2,1)} %pad_maximum_fusion.2), channel_id=1, source_target_pairs={{0,1},{1,2},{2,3},{3,0},{4,5},{5,6},{6,7},{7,4},{8,9},{9,10},{10,1... | collective-permute-start | bytes 1572872 | tf_op jit(solution)/shard_map/ppermute | solution.py:132
  109.8 7.5 %collective-permute-start.35 = (bf16[256,1024]{1,0:T(8,128)(2,1)}, bf16[256,1024]{1,0:T(8,128)(2,1)}, u32[]{:S(2)}, u32[]{:S(2)}) collective-permute-start(bf16[256,1024]{1,0:T(8,128)(2,1)} %copy-done.21), channel_id=1, source_target_pairs={{0,4},{4,0},{8,12},{12,8},{16,20},{20,16},{24,28},{28,24},{1,5},{5... | collective-permute-start | bytes 1572872 | tf_op jit(solution)/shard_map/ppermute | solution.py:17
  111.3 6.1 %collective-permute-start.37 = (bf16[256,1024]{1,0:T(8,128)(2,1)}, bf16[256,1024]{1,0:T(8,128)(2,1)}, u32[]{:S(2)}, u32[]{:S(2)}) collective-permute-start(bf16[256,1024]{1,0:T(8,128)(2,1)} %copy-done.22), channel_id=1, source_target_pairs={{0,4},{4,0},{8,12},{12,8},{16,20},{20,16},{24,28},{28,24},{1,5},{5... | collective-permute-start | bytes 1572872 | tf_op jit(solution)/shard_map/ppermute | solution.py:17
  115.3 9.3 %collective-permute-start.32 = (bf16[128,1024]{1,0:T(8,128)(2,1)}, bf16[128,1024]{1,0:T(8,128)(2,1)S(1)}, u32[]{:S(2)}, u32[]{:S(2)}) collective-permute-start(bf16[128,1024]{1,0:T(8,128)(2,1)} %fusion.10), channel_id=1, source_target_pairs={{0,16},{4,20},{8,24},{12,28},{16,0},{20,4},{24,8},{28,12},{1,17},{... | collective-permute-start | bytes 786440 | tf_op jit(solution)/shard_map/ppermute | solution.py:17
  116.8 8.8 %collective-permute-start.33 = (bf16[128,1024]{1,0:T(8,128)(2,1)}, bf16[128,1024]{1,0:T(8,128)(2,1)}, u32[]{:S(2)}, u32[]{:S(2)}) collective-permute-start(bf16[128,1024]{1,0:T(8,128)(2,1)} %fusion.11), channel_id=1, source_target_pairs={{0,8},{4,12},{8,0},{12,4},{16,24},{20,28},{24,16},{28,20},{1,9},{5... | collective-permute-start | bytes 786440 | tf_op jit(solution)/shard_map/ppermute | solution.py:17
  (36 other events, 286.3 us)
